TPU v7x, 32 devices: a whole 2x2x4 slice. The times are simulated.
32 devices in a mesh: rows: 16 (over z, x, core), seq: 2 (over y).
Axes of the slice: x: 2, y: 2, z: 4, core: 2. Of those that a mesh axis runs over, the one named last changes fastest.
Arguments:
- tokens: bfloat16 [2, 16, 512, 768], P(None, 'rows', 'seq'), may hold values from -6 to 6
- cotangent: bfloat16 [2, 16, 512, 768], P(None, 'rows', 'seq'), may hold values from -6 to 6
- w_query: bfloat16 [768, 768], P(('rows', 'seq')), may hold values from -0.109375 to 0.109375
- w_key: bfloat16 [768, 768], P(('rows', 'seq')), may hold values from -0.109375 to 0.109375
- w_value: bfloat16 [768, 768], P(('rows', 'seq')), may hold values from -0.21875 to 0.21875
- w_output: bfloat16 [768, 768], P(('rows', 'seq')), may hold values from -0.875 to 0.875
- w_in: bfloat16 [768, 3072], P(('rows', 'seq')), may hold values from -0.21875 to 0.21875
- w_out: bfloat16 [3072, 768], P(('rows', 'seq')), may hold values from -0.15625 to 0.15625
- gain_attn: bfloat16 [768], P(('rows', 'seq')), may hold values from 0.099609375 to 1.8984375
- gain_ffn: bfloat16 [768], P(('rows', 'seq')), may hold values from 0.099609375 to 1.8984375
- bias_table: float32 [12, 32], P('seq'), may hold values from -4 to 4
- buckets: int32 [1023], replicated, may hold values from 0 to 31
Outputs:
- layer_out: bfloat16 [2, 16, 512, 768], P(None, 'rows', 'seq')
- grad_tokens: bfloat16 [2, 16, 512, 768], P(None, 'rows', 'seq')
- grad_w_query: float32 [768, 768], P(('rows', 'seq'))
- grad_w_key: float32 [768, 768], P(('rows', 'seq'))
- grad_w_value: float32 [768, 768], P(('rows', 'seq'))
- grad_w_output: float32 [768, 768], P(('rows', 'seq'))
- grad_w_in: float32 [768, 3072], P(('rows', 'seq'))
- grad_w_out: float32 [3072, 768], P(('rows', 'seq'))
- grad_gain_attn: float32 [768], P(('rows', 'seq'))
- grad_gain_ffn: float32 [768], P(('rows', 'seq'))
- grad_bias_table: float32 [12, 32], P('seq')
All inputs are finite; a program needn't handle non-finite values.
Results may differ from a plain program's by a relative error of at most 0.014.
The roundings to bfloat16 on the way count: a program that leaves them out, or rounds other values in their place, can miss the bound.
Values may be sent and summed in bfloat16 or wider, within the bound.
No kernel may reach another device: no remote copies, remote signals or barrier semaphores. Data moves between devices by JAX's collectives and lax.ppermute only.
A program may use at most 192 MiB of HBM per device.

v0:
```python
import jax
import jax.numpy as jnp
from jax import lax
from jax.sharding import PartitionSpec as P

HEAD_DIM = 64


epsilon = 1e-06


def normalize(values, gain):
    inv_rms = lax.rsqrt(jnp.mean(values * values, axis=-1, keepdims=True) + epsilon)
    return (values * inv_rms * gain, inv_rms)


def norm_back(grad_out, values, inv_rms, gain):
    scaled_grad = grad_out * gain
    grad_in = inv_rms * scaled_grad - values * (inv_rms * inv_rms * inv_rms) * jnp.mean(
        scaled_grad * values, axis=-1, keepdims=True
    )
    grad_gain = jnp.sum(grad_out * values * inv_rms, axis=0)
    return (grad_in, grad_gain)


def bucket_picker(bias_tab, buckets):
    return (buckets[None, :] == jnp.arange(bias_tab.shape[1], dtype=jnp.int32)[:, None]).astype(
        jnp.float32
    )


def offset_row(bias_tab, buckets):
    return jnp.dot(
        bias_tab,
        bucket_picker(bias_tab, buckets),
        precision=lax.Precision.HIGHEST,
        preferred_element_type=jnp.float32,
    )


def full_bias(offset_bias, seq_len):
    head_count = offset_bias.shape[0]
    span = 2 * seq_len - 1
    tiled = jnp.concatenate(
        [jnp.tile(offset_bias, (1, seq_len)), jnp.zeros((head_count, seq_len), jnp.float32)], axis=1
    )
    skewed = tiled.reshape(head_count, seq_len, span + 1)[:, :, :seq_len]
    return skewed[:, ::-1, :]


def full_bias_back(grad_rows, seq_len):
    head_count = grad_rows.shape[0]
    span = 2 * seq_len - 1
    flipped = grad_rows[:, ::-1, :]
    padded = jnp.pad(flipped, ((0, 0), (0, 0), (0, span + 1 - seq_len)))
    flat = padded.reshape(head_count, seq_len * (span + 1))[:, : seq_len * span]
    return jnp.sum(flat.reshape(head_count, seq_len, span), axis=1)


def to_groups(normed_low, weight, groups):
    projected = jnp.dot(normed_low, weight, preferred_element_type=jnp.float32).astype(jnp.bfloat16)
    return projected.reshape(normed_low.shape[0], groups, weight.shape[1] // groups)


def attend(queries, key_heads, value_heads, bias_full):
    scores = jnp.einsum("qhd,khd->hqk", queries, key_heads, preferred_element_type=jnp.float32)
    scores = scores + bias_full
    row_peak = jnp.max(scores, axis=-1, keepdims=True)
    log_total = row_peak + jnp.log(jnp.sum(jnp.exp(scores - row_peak), axis=-1, keepdims=True))
    probs_low = jnp.exp(scores - log_total).astype(jnp.bfloat16)
    outputs = jnp.einsum(
        "hqk,khd->qhd", probs_low, value_heads, preferred_element_type=jnp.float32
    ).astype(jnp.bfloat16)
    log_sums = [log_total]
    return (outputs, log_sums)


def attend_back(queries, key_heads, value_heads, bias_full, log_sums, grad_heads, score_sums):
    scores = (
        jnp.einsum("qhd,khd->hqk", queries, key_heads, preferred_element_type=jnp.float32)
        + bias_full
    )
    soft_probs = jnp.exp(scores - log_sums[0])
    grad_probs = jnp.einsum(
        "qhd,khd->hqk", grad_heads, value_heads, preferred_element_type=jnp.float32
    )
    center = jnp.sum(soft_probs * grad_probs, axis=-1, keepdims=True)
    grad_scores = (soft_probs * (grad_probs - center)).astype(jnp.bfloat16)
    grad_query_list = jnp.einsum(
        "hqk,khd->qhd", grad_scores, key_heads, preferred_element_type=jnp.float32
    ).astype(jnp.bfloat16)
    grad_keys = jnp.einsum("hqk,qhd->khd", grad_scores, queries, preferred_element_type=jnp.float32)
    grad_values = jnp.einsum(
        "hqk,qhd->khd",
        soft_probs.astype(jnp.bfloat16),
        grad_heads,
        preferred_element_type=jnp.float32,
    )
    block_sum = grad_scores.astype(jnp.float32)
    new_sums = [block_sum if score_sums is None else score_sums[0] + block_sum]
    return (
        grad_query_list,
        grad_keys.astype(jnp.bfloat16),
        grad_values.astype(jnp.bfloat16),
        new_sums,
    )


def shards(
    tokens,
    cotangent,
    w_query,
    w_key,
    w_value,
    w_output,
    w_in,
    w_out,
    gain_attn,
    gain_ffn,
    bias_table,
    buckets,
):
    groups = lax.axis_size("seq")
    micro_count = tokens.shape[0]
    local_len = tokens.shape[2]
    features = tokens.shape[3]
    group_width = features // groups
    seq_len = local_len * groups
    heads_here = bias_table.shape[0]
    owned_shards = (w_query, w_key, w_value, w_output, w_in, w_out, gain_attn, gain_ffn)
    bias_full = full_bias(offset_row(bias_table, buckets), seq_len)
    layer_outs = []
    input_grads = []
    score_sums = None
    collected = None
    for micro_idx in range(micro_count):
        gathered = (
            lax.all_gather(owned_shards[0], ("rows", "seq"), axis=0, tiled=True),
            lax.all_gather(owned_shards[1], ("rows", "seq"), axis=0, tiled=True),
            lax.all_gather(owned_shards[2], ("rows", "seq"), axis=0, tiled=True),
            lax.all_gather(owned_shards[3], ("rows", "seq"), axis=0, tiled=True),
            lax.all_gather(owned_shards[4], ("rows", "seq"), axis=0, tiled=True),
            lax.all_gather(owned_shards[5], ("rows", "seq"), axis=0, tiled=True),
            lax.all_gather(owned_shards[6], ("rows", "seq"), axis=0, tiled=True),
            lax.all_gather(owned_shards[7], ("rows", "seq"), axis=0, tiled=True),
        )
        inputs = tokens[micro_idx, 0].astype(jnp.float32)
        normed, attn_scale = normalize(inputs, gathered[6].astype(jnp.float32))
        attn_input = normed.astype(jnp.bfloat16)
        query_tok = to_groups(attn_input, gathered[0], groups)
        key_tok = to_groups(attn_input, gathered[1], groups)
        value_tok = to_groups(attn_input, gathered[2], groups)
        query_heads, key_heads, value_heads = (
            lax.all_to_all(query_tok, "seq", split_axis=1, concat_axis=0, tiled=True),
            lax.all_to_all(key_tok, "seq", split_axis=1, concat_axis=0, tiled=True),
            lax.all_to_all(value_tok, "seq", split_axis=1, concat_axis=0, tiled=True),
        )
        query_heads = query_heads.reshape(seq_len, heads_here, HEAD_DIM)
        key_heads = key_heads.reshape(seq_len, heads_here, HEAD_DIM)
        value_heads = value_heads.reshape(seq_len, heads_here, HEAD_DIM)
        attended_heads, log_sums = attend(query_heads, key_heads, value_heads, bias_full)
        attended = lax.all_to_all(
            attended_heads.reshape(seq_len, 1, group_width),
            "seq",
            split_axis=0,
            concat_axis=1,
            tiled=True,
        ).reshape(local_len, features)
        middle = inputs + jnp.dot(attended, gathered[3], preferred_element_type=jnp.float32)
        normed_mid, ffn_scale = normalize(middle, gathered[7].astype(jnp.float32))
        ffn_input = normed_mid.astype(jnp.bfloat16)
        pre_act = jnp.dot(ffn_input, gathered[4], preferred_element_type=jnp.float32)
        sigmoid_pre = jax.nn.sigmoid(pre_act)
        hidden_act = (pre_act * sigmoid_pre).astype(jnp.bfloat16)
        layer_outs.append(
            (middle + jnp.dot(hidden_act, gathered[5], preferred_element_type=jnp.float32)).astype(
                jnp.bfloat16
            )
        )
        backward_set = (
            lax.all_gather(owned_shards[0], ("rows", "seq"), axis=0, tiled=True),
            lax.all_gather(owned_shards[1], ("rows", "seq"), axis=0, tiled=True),
            lax.all_gather(owned_shards[2], ("rows", "seq"), axis=0, tiled=True),
            lax.all_gather(owned_shards[3], ("rows", "seq"), axis=0, tiled=True),
            lax.all_gather(owned_shards[4], ("rows", "seq"), axis=0, tiled=True),
            lax.all_gather(owned_shards[5], ("rows", "seq"), axis=0, tiled=True),
            lax.all_gather(owned_shards[6], ("rows", "seq"), axis=0, tiled=True),
            lax.all_gather(owned_shards[7], ("rows", "seq"), axis=0, tiled=True),
        )
        grad_top = cotangent[micro_idx, 0]
        grad_w_out = jnp.einsum(
            "tf,td->fd", hidden_act, grad_top, preferred_element_type=jnp.float32
        )
        grad_act = jnp.einsum(
            "td,fd->tf", grad_top, backward_set[5], preferred_element_type=jnp.float32
        )
        grad_pre = (grad_act * (sigmoid_pre * (1.0 + pre_act * (1.0 - sigmoid_pre)))).astype(
            jnp.bfloat16
        )
        grad_w_in = jnp.einsum("td,tf->df", ffn_input, grad_pre, preferred_element_type=jnp.float32)
        grad_ffn_in = jnp.einsum(
            "tf,df->td", grad_pre, backward_set[4], preferred_element_type=jnp.float32
        )
        grad_middle, grad_gain_ffn = norm_back(
            grad_ffn_in, middle, ffn_scale, backward_set[7].astype(jnp.float32)
        )
        grad_middle = grad_middle + grad_top.astype(jnp.float32)
        grad_middle_low = grad_middle.astype(jnp.bfloat16)
        grad_w_output = jnp.einsum(
            "td,te->de", attended, grad_middle_low, preferred_element_type=jnp.float32
        )
        grad_attended = jnp.einsum(
            "te,de->td", grad_middle_low, backward_set[3], preferred_element_type=jnp.float32
        ).astype(jnp.bfloat16)
        grad_heads = lax.all_to_all(
            grad_attended.reshape(local_len, groups, group_width),
            "seq",
            split_axis=1,
            concat_axis=0,
            tiled=True,
        ).reshape(seq_len, heads_here, HEAD_DIM)
        grad_queries, grad_keys, grad_values, score_sums = attend_back(
            query_heads, key_heads, value_heads, bias_full, log_sums, grad_heads, score_sums
        )
        grad_query_tok, grad_key_tok, grad_value_tok = (
            lax.all_to_all(
                grad_queries.reshape(seq_len, 1, group_width),
                "seq",
                split_axis=0,
                concat_axis=1,
                tiled=True,
            ),
            lax.all_to_all(
                grad_keys.reshape(seq_len, 1, group_width),
                "seq",
                split_axis=0,
                concat_axis=1,
                tiled=True,
            ),
            lax.all_to_all(
                grad_values.reshape(seq_len, 1, group_width),
                "seq",
                split_axis=0,
                concat_axis=1,
                tiled=True,
            ),
        )
        grad_query_tok = grad_query_tok.reshape(local_len, features)
        grad_key_tok = grad_key_tok.reshape(local_len, features)
        grad_value_tok = grad_value_tok.reshape(local_len, features)
        grad_w_query = jnp.einsum(
            "td,te->de", attn_input, grad_query_tok, preferred_element_type=jnp.float32
        )
        grad_w_key = jnp.einsum(
            "td,te->de", attn_input, grad_key_tok, preferred_element_type=jnp.float32
        )
        grad_w_value = jnp.einsum(
            "td,te->de", attn_input, grad_value_tok, preferred_element_type=jnp.float32
        )
        grad_attn_in = jnp.einsum(
            "te,de->td", grad_query_tok, backward_set[0], preferred_element_type=jnp.float32
        )
        grad_attn_in = grad_attn_in + jnp.einsum(
            "te,de->td", grad_key_tok, backward_set[1], preferred_element_type=jnp.float32
        )
        grad_attn_in = grad_attn_in + jnp.einsum(
            "te,de->td", grad_value_tok, backward_set[2], preferred_element_type=jnp.float32
        )
        grad_inputs, grad_gain_attn = norm_back(
            grad_attn_in, inputs, attn_scale, backward_set[6].astype(jnp.float32)
        )
        input_grads.append((grad_inputs + grad_middle).astype(jnp.bfloat16))
        grad_terms = (
            grad_w_query,
            grad_w_key,
            grad_w_value,
            grad_w_output,
            grad_w_in,
            grad_w_out,
            grad_gain_attn,
            grad_gain_ffn,
        )
        shares = (
            lax.psum_scatter(grad_terms[0], ("rows", "seq"), scatter_dimension=0, tiled=True),
            lax.psum_scatter(grad_terms[1], ("rows", "seq"), scatter_dimension=0, tiled=True),
            lax.psum_scatter(grad_terms[2], ("rows", "seq"), scatter_dimension=0, tiled=True),
            lax.psum_scatter(grad_terms[3], ("rows", "seq"), scatter_dimension=0, tiled=True),
            lax.psum_scatter(grad_terms[4], ("rows", "seq"), scatter_dimension=0, tiled=True),
            lax.psum_scatter(grad_terms[5], ("rows", "seq"), scatter_dimension=0, tiled=True),
            lax.psum_scatter(grad_terms[6], ("rows", "seq"), scatter_dimension=0, tiled=True),
            lax.psum_scatter(grad_terms[7], ("rows", "seq"), scatter_dimension=0, tiled=True),
        )
        collected = (
            shares
            if collected is None
            else tuple((old + new for old, new in zip(collected, shares)))
        )
    grad_offset = full_bias_back(score_sums[0], seq_len)
    table_grad = jnp.dot(
        grad_offset,
        bucket_picker(bias_table, buckets).T,
        precision=lax.Precision.HIGHEST,
        preferred_element_type=jnp.float32,
    )
    table_grad = lax.psum(table_grad, "rows")
    layer_out = jnp.stack(layer_outs)[:, None]
    grad_tokens = jnp.stack(input_grads)[:, None]
    return (layer_out, grad_tokens) + tuple(collected) + (table_grad,)


def solution(mesh):
    in_specs = (
        P(None, "rows", "seq", None),
        P(None, "rows", "seq", None),
        P(("rows", "seq"), None),
        P(("rows", "seq"), None),
        P(("rows", "seq"), None),
        P(("rows", "seq"), None),
        P(("rows", "seq"), None),
        P(("rows", "seq"), None),
        P(("rows", "seq")),
        P(("rows", "seq")),
        P("seq", None),
        P(),
    )
    out_specs = (
        P(None, "rows", "seq", None),
        P(None, "rows", "seq", None),
        P(("rows", "seq"), None),
        P(("rows", "seq"), None),
        P(("rows", "seq"), None),
        P(("rows", "seq"), None),
        P(("rows", "seq"), None),
        P(("rows", "seq"), None),
        P(("rows", "seq")),
        P(("rows", "seq")),
        P("seq", None),
    )
    return jax.shard_map(shards, mesh=mesh, in_specs=in_specs, out_specs=out_specs, check_vma=False)
```

profile of v0, /device:TPU:0, one launch (start us, length us, event | category | flops | bytes accessed | tf_op | source)
XLA Modules:
  0.0 1121.7 jit_solution(80101778057908682)
XLA Ops:
  12.9 42.0 %all-reduce.7 = (bf16[768]{0:T(1024)(128)(2,1)S(1)}, bf16[768]{0:T(1024)(128)(2,1)S(1)}) all-reduce(bf16[768]{0:T(1024)(128)(2,1)S(1)} %dynamic-update-slice, bf16[768]{0:T(1024)(128)(2,1)S(1)} %dynamic-update-slice.1), channel_id=1, replica_groups=mesh['rows'=16,'seq'=2] {'rows','seq'}, use_global_device_ids=true, to_apply=%add.2 | all-reduce | flops 1536 | bytes 6144
  56.9 11.0 all-gather.9.cloned.1.call-done
  74.1 49.9 %all-gather.11.cloned.1.call-done = bf16[768,768]{1,0:T(8,128)(2,1)} async-done(((bf16[24,768]{1,0:T(8,128)(2,1)}), bf16[768,768]{1,0:T(8,128)(2,1)}) %all-gather.11.cloned.1.call-update) | async-done | bytes 1179664 | tf_op jit(solution)/shard_map/all_gather | solution.py:139
  130.7 49.3 %all-gather.7.cloned.1.call-done = bf16[768,768]{1,0:T(8,128)(2,1)} async-done(((bf16[24,768]{1,0:T(8,128)(2,1)}), bf16[768,768]{1,0:T(8,128)(2,1)}) %all-gather.7.cloned.1.call-update) | async-done | bytes 1179664 | tf_op jit(solution)/shard_map/all_gather | solution.py:140
  188.1 6.3 all-to-all-done.4
  217.2 6.2 tile.4
  223.3 13.6 %reshape.365 = f32[3142656]{0:T(1024)} reshape(f32[6,512,1023]{2,1,0:T(8,128)} %tile.4) | data formatting | bytes 25141248
  237.0 14.0 %tile.10 = f32[6,523776]{1,0:T(8,128)} reshape(f32[3142656]{0:T(1024)} %reshape.365) | data formatting | bytes 25141248 | tf_op jit(solution)/shard_map/tile | solution.py:45
  251.0 11.8 %concatenate.3 = f32[6,524288]{1,0:T(8,128)} pad(f32[6,523776]{1,0:T(8,128)} %tile.10, f32[]{:T(128)} %constant.16.clone.1), padding=0_0x0_512 | pad | bytes 25153540 | tf_op jit(solution)/shard_map/concatenate | solution.py:44
  262.8 17.6 %copy.178 = f32[1,6,512,1024]{3,2,1,0:T(8,128)} copy(f32[1,6,512,1024]{3,1,2,0:T(8,128)} %bitcast.321) | data formatting | bytes 25165824
  280.5 7.5 slice.24
  288.0 6.6 copy.157
  294.6 51.0 %rev.6 = f32[6,512,512]{1,2,0:T(8,128)} reverse(f32[6,512,512]{1,2,0:T(8,128)} %copy.157), dimensions={1} | reverse | bytes 12582912 | tf_op jit(solution)/shard_map/rev | solution.py:48
  394.8 5.6 fusion.68
  464.0 6.7 multiply_reduce_fusion.1
  480.6 8.5 convert_add_fusion
  569.2 5.7 convolution_add_fusion
  579.1 5.2 convolution_add_fusion.1
  584.9 5.2 fusion.7
  595.4 51.4 %rev.7 = f32[6,512,512]{1,2,0:T(8,128)} reverse(f32[6,512,512]{1,2,0:T(8,128)} %get-tuple-element.71), dimensions={1} | reverse | bytes 12582912 | tf_op jit(solution)/shard_map/rev | solution.py:54
  646.8 6.7 copy.158
  653.5 9.3 pad_bitcast_fusion
  662.8 18.1 %copy.168 = f32[1,6,512,1024]{3,1,2,0:T(8,128)} copy(f32[1,6,512,1024]{3,2,1,0:T(8,128)} %pad_bitcast_fusion) | data formatting | bytes 25165824
  680.9 11.5 %slice.25 = f32[6,523776]{1,0:T(8,128)} slice(f32[6,524288]{1,0:T(8,128)} %bitcast.322), slice={[0:6], [0:523776]} | slice | bytes 25141248 | tf_op jit(solution)/shard_map/slice | solution.py:56
  692.5 12.4 %reshape.367 = f32[3142656]{0:T(1024)} reshape(f32[6,523776]{1,0:T(8,128)} %slice.25) | data formatting | bytes 25141248
  704.8 14.3 %reshape.358 = f32[6,512,1023]{2,1,0:T(8,128)} reshape(f32[3142656]{0:T(1024)} %reshape.367) | data formatting | bytes 25141248 | tf_op jit(solution)/shard_map/reshape | solution.py:57
  719.1 6.3 reduce_sum.169
  726.4 30.1 %psum.7 = f32[6,32]{1,0:T(8,128)} all-reduce(f32[6,32]{1,0:T(8,128)S(1)} %fusion.64), channel_id=1, replica_groups=mesh['rows'=16,'seq'=2] {'rows'}, use_global_device_ids=true, to_apply=%region_35.36 | all-reduce | flops 192 | bytes 1536 | tf_op jit(solution)/shard_map/psum | solution.py:305
  763.4 37.7 %all-reduce.6 = (f32[768]{0:T(1024)S(1)}, f32[768]{0:T(1024)S(1)}) all-reduce(f32[768]{0:T(1024)S(1)} %add.220, f32[768]{0:T(1024)S(1)} %add.221), channel_id=16, replica_groups=mesh['rows'=16,'seq'=2] {'rows','seq'}, use_global_device_ids=true, to_apply=%region_27.0.clone | all-reduce | flops 1536 | bytes 12288
  804.9 26.6 %reduce-scatter.7.cloned.1.call-done = f32[24,768]{1,0:T(8,128)} async-done(((f32[768,768]{1,0:T(8,128)}), f32[24,768]{1,0:T(8,128)}) %reduce-scatter.7.cloned.1.call-update) | async-done | bytes 73744 | tf_op jit(solution)/shard_map/reduce_scatter | solution.py:284
  831.5 141.2 %reduce-scatter.17.cloned.1.call-done = f32[96,768]{1,0:T(8,128)} async-done(((f32[3072,768]{1,0:T(8,128)}), f32[96,768]{1,0:T(8,128)}) %reduce-scatter.17.cloned.1.call-update) | async-done | bytes 294928 | tf_op jit(solution)/shard_map/reduce_scatter | solution.py:289
  972.7 142.0 %reduce-scatter.15.cloned.1.call-done = f32[24,3072]{1,0:T(8,128)} async-done(((f32[768,3072]{1,0:T(8,128)}), f32[24,3072]{1,0:T(8,128)}) %reduce-scatter.15.cloned.1.call-update) | async-done | bytes 294928 | tf_op jit(solution)/shard_map/reduce_scatter | solution.py:288
  (369 shorter events, 274.3 us)
Async XLA Ops:
  7.2 209.8 %copy-start = (f32[6,32]{1,0:T(8,128)S(1)}, f32[6,32]{1,0:T(8,128)}, u32[]{:S(2)}) copy-start(f32[6,32]{1,0:T(8,128)} %param.22) | copy-start | bytes 2308
  7.2 60.7 %all-gather.9.cloned.1.call-start = ((), (), s32[]{:S(2)}) async-start(), calls=%async_computation.23 | async-start | bytes 1216512 | tf_op jit(solution)/shard_map/all_gather | solution.py:138
  7.9 116.0 %all-gather.11.cloned.1.call-start = ((), (), s32[]{:S(2)}) async-start(), calls=%async_computation.24 | async-start | bytes 1216512 | tf_op jit(solution)/shard_map/all_gather | solution.py:139
  8.7 171.3 %all-gather.7.cloned.1.call-start = ((), (), s32[]{:S(2)}) async-start(), calls=%async_computation.22 | async-start | bytes 1216512 | tf_op jit(solution)/shard_map/all_gather | solution.py:140
  9.4 380.2 %all-gather.13.cloned.1.call-start = ((), (), s32[]{:S(2)}) async-start(), calls=%async_computation.25 | async-start | bytes 1216512 | tf_op jit(solution)/shard_map/all_gather | solution.py:141
  10.0 384.8 %all-gather.15.cloned.1.call-start = ((), (), s32[]{:S(2)}) async-start(), calls=%async_computation.26 | async-start | bytes 4866048 | tf_op jit(solution)/shard_map/all_gather | solution.py:142
  10.6 393.0 %all-gather.17.cloned.1.call-start = ((), (), s32[]{:S(2)}) async-start(), calls=%async_computation.27 | async-start | bytes 4866048 | tf_op jit(solution)/shard_map/all_gather | solution.py:143
  56.9 123.1 %copy-start.64 = (f32[256]{0:T(256)}, f32[256]{0:T(256)S(1)}, u32[]{:S(2)}) copy-start(f32[256]{0:T(256)S(1)} %get-tuple-element.83) | copy-start | bytes 3076
  56.9 150.8 %copy-start.60 = (f32[256]{0:T(256)}, f32[256]{0:T(256)S(1)}, u32[]{:S(2)}) copy-start(f32[256]{0:T(256)S(1)} %get-tuple-element.102) | copy-start | bytes 3076
  70.6 55.9 %all-to-all-start.5 = ((bf16[256,2,384]{2,0,1:T(8,128)(2,1)}), bf16[256,2,384]{2,0,1:T(8,128)(2,1)S(1)}, u32[]{:S(2)}, u32[]{:S(2)}) async-start(bf16[256,2,384]{2,0,1:T(8,128)(2,1)} %bitcast.314), calls=%async_computation.5 | async-start | bytes 786432 | tf_op jit(solution)/shard_map/all_to_all | solution.py:154
  126.5 56.0 %all-to-all-start.6 = ((bf16[256,2,384]{2,0,1:T(8,128)(2,1)}), bf16[256,2,384]{2,0,1:T(8,128)(2,1)}, u32[]{:S(2)}, u32[]{:S(2)}) async-start(bf16[256,2,384]{2,0,1:T(8,128)(2,1)} %bitcast.313), calls=%async_computation.6 | async-start | bytes 786432 | tf_op jit(solution)/shard_map/all_to_all | solution.py:155
  182.6 11.8 %all-to-all-start.4 = ((bf16[256,2,384]{2,0,1:T(8,128)(2,1)}), bf16[256,2,384]{2,0,1:T(8,128)(2,1)}, u32[]{:S(2)}, u32[]{:S(2)}) async-start(bf16[256,2,384]{2,0,1:T(8,128)(2,1)} %bitcast.345), calls=%async_computation.4 | async-start | bytes 786432 | tf_op jit(solution)/shard_map/all_to_all | solution.py:156
  194.4 9.8 all-to-all-start.1
  204.2 9.3 all-to-all-start.2
  213.5 140.1 %all-to-all-start = ((bf16[256,2,384]{2,0,1:T(8,128)(2,1)}), bf16[256,2,384]{2,0,1:T(8,128)(2,1)S(1)}, u32[]{:S(2)}, u32[]{:S(2)}) async-start(bf16[256,2,384]{2,0,1:T(8,128)(2,1)} %bitcast.318), calls=%async_computation | async-start | bytes 786432 | tf_op jit(solution)/shard_map/all_to_all | solution.py:156
  366.4 13.2 %all-to-all-start.3 = ((bf16[2,2,49152]{2,1,0:T(2,128)(2,1)}), bf16[2,2,49152]{2,1,0:T(2,128)(2,1)S(1)}, u32[]{:S(2)}, u32[]{:S(2)}) async-start(bf16[2,2,49152]{2,1,0:T(2,128)(2,1)} %reshape.371), calls=%async_computation.3 | async-start | bytes 786432 | tf_op jit(solution)/shard_map/all_to_all | solution.py:162
  379.6 9.4 all-to-all-start.7
  383.1 421.8 %reduce-scatter.13.cloned.1.call-start = ((), (), s32[]{:S(2)}) async-start(), calls=%async_computation.31 | async-start | bytes 2433024 | tf_op jit(solution)/shard_map/reduce_scatter | solution.py:287
  422.5 9.8 all-to-all-start.8
  432.2 9.3 all-to-all-start.12
  448.5 11.3 %all-to-all-start.15 = ((bf16[2,2,49152]{2,1,0:T(2,128)(2,1)}), bf16[2,2,49152]{2,1,0:T(2,128)(2,1)S(1)}, u32[]{:S(2)}, u32[]{:S(2)}) async-start(bf16[2,2,49152]{2,1,0:T(2,128)(2,1)} %reshape.377), calls=%async_computation.15 | async-start | bytes 786432 | tf_op jit(solution)/shard_map/all_to_all | solution.py:240
  459.8 11.6 %all-to-all-start.11 = ((bf16[2,2,49152]{2,1,0:T(2,128)(2,1)}), bf16[2,2,49152]{2,1,0:T(2,128)(2,1)}, u32[]{:S(2)}, u32[]{:S(2)}) async-start(bf16[2,2,49152]{2,1,0:T(2,128)(2,1)} %reshape.383), calls=%async_computation.11 | async-start | bytes 786432 | tf_op jit(solution)/shard_map/all_to_all | solution.py:240
  464.0 340.9 %reduce-scatter.11.cloned.1.call-start = ((), (), s32[]{:S(2)}) async-start(), calls=%async_computation.30 | async-start | bytes 2433024 | tf_op jit(solution)/shard_map/reduce_scatter | solution.py:286
  499.0 10.9 all-to-all-start.10
  509.9 10.1 all-to-all-start.14
  514.1 290.8 %reduce-scatter.9.cloned.1.call-start = ((), (), s32[]{:S(2)}) async-start(), calls=%async_computation.29 | async-start | bytes 2433024 | tf_op jit(solution)/shard_map/reduce_scatter | solution.py:285
  540.4 11.9 %all-to-all-start.9 = ((bf16[2,2,49152]{2,1,0:T(2,128)(2,1)}), bf16[2,2,49152]{2,1,0:T(2,128)(2,1)}, u32[]{:S(2)}, u32[]{:S(2)}) async-start(bf16[2,2,49152]{2,1,0:T(2,128)(2,1)} %reshape.379), calls=%async_computation.9 | async-start | bytes 786432 | tf_op jit(solution)/shard_map/all_to_all | solution.py:226
  552.3 9.3 all-to-all-start.13
  555.8 275.7 %reduce-scatter.7.cloned.1.call-start = ((), (), s32[]{:S(2)}) async-start(), calls=%async_computation.28 | async-start | bytes 2433024 | tf_op jit(solution)/shard_map/reduce_scatter | solution.py:284
  565.0 407.7 %reduce-scatter.17.cloned.1.call-start = ((), (), s32[]{:S(2)}) async-start(), calls=%async_computation.33 | async-start | bytes 9732096 | tf_op jit(solution)/shard_map/reduce_scatter | solution.py:289
  574.9 539.8 %reduce-scatter.15.cloned.1.call-start = ((), (), s32[]{:S(2)}) async-start(), calls=%async_computation.32 | async-start | bytes 9732096 | tf_op jit(solution)/shard_map/reduce_scatter | solution.py:288
  802.3 312.4 %copy-start.1 = (f32[6,32]{1,0:T(8,128)S(1)}, f32[6,32]{1,0:T(8,128)}, u32[]{:S(2)}) copy-start(f32[6,32]{1,0:T(8,128)} %param.22) | copy-start | bytes 2308
  (77 other events, 849.7 us)
Sparse Core Ops, SparseCore 0:
  11.0 56.8 all-gather.8
  70.8 53.0 all-gather.10
  126.9 53.0 all-gather.6
  182.7 53.0 all-gather.12
  238.6 62.6 all-gather.14
  304.0 62.5 all-gather.16
  419.9 98.0 reduce-scatter.12
  524.7 98.1 reduce-scatter.10
  628.8 97.9 reduce-scatter.8
  733.4 98.0 reduce-scatter.6
  838.0 134.6 reduce-scatter.16
  980.0 134.5 reduce-scatter.14
where the time goes:
time: 1140 us; the launch traced here: 1120 us
  waiting for transfers between devices  460 us (40%)
  local copies, waits for them, and re-layouts  317 us (28%)
  matrix products  120 us (11%)
  blocking collectives  110 us (10%)
  starting transfers between devices  60.7 us (5%)
  other arithmetic  39.1 us (3%)
  between operations  16 us (1%)
    reduce_scatter x1, waiting for transfers between devices, shards(): lax.psum_scatter(grad_terms[4], ('rows', 'seq'), scatter_dimension=0, til...  142 us
    reduce_scatter x1, waiting for transfers between devices, shards(): lax.psum_scatter(grad_terms[5], ('rows', 'seq'), scatter_dimension=0, til...  141 us
    unnamed x207, local copies, waits for them, and re-layouts  126 us
    unnamed x2, blocking collectives  79.7 us
    rev x1, local copies, waits for them, and re-layouts, full_bias_back(): flipped = grad_rows[:, ::-1, :]  51.4 us
    rev x1, local copies, waits for them, and re-layouts, full_bias(): return skewed[:, ::-1, :]  51 us
    all_gather x1, waiting for transfers between devices, shards(): lax.all_gather(owned_shards[1], ('rows', 'seq'), axis=0, tiled=True)  49.9 us
    all_gather x1, waiting for transfers between devices, shards(): lax.all_gather(owned_shards[2], ('rows', 'seq'), axis=0, tiled=True)  49.3 us
  transfers between devices with their start and end apart: 28, of which 15 were waited for; matrix products, arithmetic and copies ran while one was open for 40% of the time, Pallas kernels for 0%

commit v1 on v0

v1 whole, which is shorter than its diff:
```python
import jax
import jax.numpy as jnp
from jax import lax
from jax.experimental import pallas as pl
from jax.experimental.pallas import tpu as pltpu
from jax.sharding import PartitionSpec as P

HD = 64
RB = 128
epsilon = 1e-06


def bias_slab(vec):
    wide = jnp.broadcast_to(vec, (RB, vec.shape[1]))
    return pltpu.roll(wide, vec.shape[1] - RB + 1, 1, stride=1, stride_axis=0)

def diag_sums(slab):
    rows = slab.shape[0]
    while rows > 1:
        rows //= 2
        slab = pltpu.roll(slab[:rows], rows, 1) + slab[rows:]
    return slab

def dot_nt(a, b):
    return lax.dot_general(a, b, (((1,), (1,)), ((), ())), preferred_element_type=jnp.float32)
def dot_nn(a, b):
    return lax.dot_general(a, b, (((1,), (0,)), ((), ())), preferred_element_type=jnp.float32)
def dot_tn(a, b):
    return lax.dot_general(a, b, (((0,), (0,)), ((), ())), preferred_element_type=jnp.float32)

def attend_kernel(q_ref, k_ref, v_ref, vec_ref, o_ref):
    length = q_ref.shape[0]
    for head in range(2):
        cols = slice(head * HD, (head + 1) * HD)
        k = k_ref[:, cols]
        v = v_ref[:, cols]
        slab = bias_slab(vec_ref[0, head:head+1, :])
        for first in range(0, length, RB):
            lane = length - RB - first
            s = dot_nt(q_ref[first:first+RB, cols], k) + slab[:, lane:lane+length]
            e = jnp.exp(s - jnp.max(s, axis=1, keepdims=True))
            p = e * (1.0 / jnp.sum(e, axis=1, keepdims=True))
            o_ref[first:first+RB, cols] = dot_nn(p.astype(jnp.bfloat16), v).astype(jnp.bfloat16)

def attend(qkv, vec):
    length, width = qkv.shape[0], qkv.shape[1] // 3
    steps = width // (2 * HD)
    spec = lambda g: pl.BlockSpec((length, 2 * HD), lambda h: (0, g * steps + h))
    return pl.pallas_call(attend_kernel, grid=(steps,),
        in_specs=[spec(0), spec(1), spec(2), pl.BlockSpec((1, 2, vec.shape[2]), lambda h: (h, 0, 0))],
        out_specs=pl.BlockSpec((length, 2 * HD), lambda h: (0, h)),
        out_shape=jax.ShapeDtypeStruct((length, width), jnp.bfloat16),
        compiler_params=pltpu.CompilerParams(vmem_limit_bytes=48 << 20))(qkv, qkv, qkv, vec)

def attend_back_kernel(q_ref, k_ref, v_ref, go_ref, vec_ref, dq_ref, dk_ref, dv_ref, dvec_ref, slab_ref):
    length = q_ref.shape[0]
    for head in range(2):
        cols = slice(head * HD, (head + 1) * HD)
        k = k_ref[:, cols]
        v = v_ref[:, cols]
        slab = bias_slab(vec_ref[0, head:head+1, :])
        slab_ref[...] = jnp.zeros(slab_ref.shape, jnp.float32)
        dk = jnp.zeros((length, HD), jnp.float32)
        dv = jnp.zeros((length, HD), jnp.float32)
        for first in range(0, length, RB):
            lane = length - RB - first
            rows = slice(first, first + RB)
            q = q_ref[rows, cols]
            go = go_ref[rows, cols]
            s = dot_nt(q, k) + slab[:, lane:lane+length]
            e = jnp.exp(s - jnp.max(s, axis=1, keepdims=True))
            p = e * (1.0 / jnp.sum(e, axis=1, keepdims=True))
            gp = dot_nt(go, v)
            center = jnp.sum(p * gp, axis=1, keepdims=True)
            ds = (p * (gp - center)).astype(jnp.bfloat16)
            slab_ref[:, lane:lane+length] += ds.astype(jnp.float32)
            dq_ref[rows, cols] = dot_nn(ds, k).astype(jnp.bfloat16)
            dk += dot_tn(ds, q)
            dv += dot_tn(p.astype(jnp.bfloat16), go)
        dk_ref[:, cols] = dk.astype(jnp.bfloat16)
        dv_ref[:, cols] = dv.astype(jnp.bfloat16)
        dvec_ref[0, head:head+1, :] = diag_sums(slab_ref[...])

def attend_back(qkv, go, vec):
    length, width = go.shape
    steps = width // (2 * HD)
    spec = lambda g: pl.BlockSpec((length, 2 * HD), lambda h: (0, g * steps + h))
    vspec = pl.BlockSpec((1, 2, vec.shape[2]), lambda h: (h, 0, 0))
    o = jax.ShapeDtypeStruct((length, width), jnp.bfloat16)
    return pl.pallas_call(attend_back_kernel, grid=(steps,),
        in_specs=[spec(0), spec(1), spec(2), spec(0), vspec],
        out_specs=[spec(0), spec(0), spec(0), vspec],
        out_shape=[o, o, o, jax.ShapeDtypeStruct(vec.shape, jnp.float32)],
        scratch_shapes=[pltpu.VMEM((RB, vec.shape[2]), jnp.float32)],
        compiler_params=pltpu.CompilerParams(vmem_limit_bytes=48 << 20))(qkv, qkv, qkv, go, vec)

def ffn_kernel(x_ref, top_ref, win_ref, wout_ref, out_ref, gx_ref, dwin_ref, dwout_ref):
    x = x_ref[...]
    top = top_ref[...]
    pre = dot_nn(x, win_ref[...])
    sig = 1.0 / (1.0 + jnp.exp(-pre))
    hid = (pre * sig).astype(jnp.bfloat16)
    gact = dot_nt(top, wout_ref[...])
    gpre = (gact * (sig * (1.0 + pre * (1.0 - sig)))).astype(jnp.bfloat16)
    @pl.when(pl.program_id(0) == 0)
    def _():
        out_ref[...] = jnp.zeros(out_ref.shape, jnp.float32)
        gx_ref[...] = jnp.zeros(gx_ref.shape, jnp.float32)
    out_ref[...] += dot_nn(hid, wout_ref[...])
    gx_ref[...] += dot_nt(gpre, win_ref[...])
    dwin_ref[...] = dot_tn(x, gpre).astype(jnp.bfloat16)
    dwout_ref[...] = dot_tn(hid, top).astype(jnp.bfloat16)

def ffn(x, top, gathered, win_at, wout_at, chunks):
    length, width = x.shape
    full = pl.BlockSpec((length, width), lambda j: (0, 0))
    col = lambda at: pl.BlockSpec((width, width), lambda j: (0, at + j))
    f = jax.ShapeDtypeStruct((length, width), jnp.float32)
    g = jax.ShapeDtypeStruct((width, chunks * width), jnp.bfloat16)
    return pl.pallas_call(ffn_kernel, grid=(chunks,),
        in_specs=[full, full, col(win_at), col(wout_at)],
        out_specs=[full, full, col(0), col(0)],
        out_shape=[f, f, g, g],
        compiler_params=pltpu.CompilerParams(vmem_limit_bytes=56 << 20))(x, top, gathered, gathered)


def rms_scale(values):
    return lax.rsqrt(jnp.mean(values * values, axis=-1, keepdims=True) + epsilon)


def norm_back(grad_out, values, inv_rms, gain):
    scaled = grad_out * gain
    inner = jnp.mean(scaled * values, axis=-1, keepdims=True)
    grad_in = inv_rms * scaled - values * (inv_rms * inv_rms * inv_rms) * inner
    return grad_in, jnp.sum(grad_out * values * inv_rms, axis=0)


def bucket_picker(buckets, bucket_count):
    padded = jnp.pad(buckets, (0, 1), constant_values=-1)
    rows = jnp.arange(bucket_count, dtype=jnp.int32)[:, None]
    return (padded[None, :] == rows).astype(jnp.float32)


def swap_halves(mine, other, half):
    received = lax.ppermute(other, "seq", [(0, 1), (1, 0)])
    first = jnp.where(half == 0, mine, received)
    second = jnp.where(half == 0, received, mine)
    return jnp.concatenate([first, second], axis=-2)


def whole_sequence(array, half):
    mine = lax.dynamic_index_in_dim(array, half, 0, keepdims=False)[0]
    other = lax.dynamic_index_in_dim(array, 1 - half, 0, keepdims=False)[0]
    return swap_halves(mine, other, half)


def split_sequence(array, half):
    rows = array.shape[0] // 2
    mine = lax.dynamic_slice_in_dim(array, half * rows, rows, 0)
    other = lax.dynamic_slice_in_dim(array, (1 - half) * rows, rows, 0)
    received = lax.ppermute(other, "seq", [(0, 1), (1, 0)])
    first = jnp.where(half == 0, mine, received)
    second = jnp.where(half == 0, received, mine)
    return jnp.stack([first, second])[:, None]


def shards(
    tokens,
    cotangent,
    w_query,
    w_key,
    w_value,
    w_output,
    w_in,
    w_out,
    gain_attn,
    gain_ffn,
    bias_table,
    buckets,
):
    everyone = ("rows", "seq")
    devices = lax.axis_size("rows") * lax.axis_size("seq")
    half = lax.axis_index("seq")
    own, width = w_query.shape
    chunks = w_in.shape[1] // width
    head_pairs = width // (2 * HD)
    bf16, f32 = jnp.bfloat16, jnp.float32

    w_in_chunks = w_in.reshape(own, devices, chunks, own).transpose(0, 2, 1, 3).reshape(own, -1)
    w_out_chunks = w_out.reshape(chunks, own, width).transpose(1, 0, 2).reshape(own, -1)
    gains = jnp.pad(jnp.stack([gain_attn, gain_ffn], axis=1), ((0, 0), (0, 126)))
    packed = jnp.concatenate(
        [w_query, w_key, w_value, w_output, w_in_chunks, w_out_chunks, gains], axis=1
    )
    gathered = lax.all_gather(packed, everyone, axis=0, tiled=True)
    w_qkv = gathered[:, : 3 * width]
    w_o = gathered[:, 3 * width : 4 * width]
    g_attn = gathered[:, -128].astype(f32)
    g_ffn = gathered[:, -127].astype(f32)

    inputs = whole_sequence(tokens, half).astype(f32)
    top = whole_sequence(cotangent, half)
    tables = lax.all_gather(bias_table, "seq", axis=0, tiled=True)
    picker = bucket_picker(buckets, bias_table.shape[1])
    vec = jnp.dot(tables, picker, precision=lax.Precision.HIGHEST, preferred_element_type=f32)
    vec = vec.reshape(head_pairs, 2, -1)

    attn_scale = rms_scale(inputs)
    attn_input = (inputs * attn_scale * g_attn).astype(bf16)
    qkv = jnp.dot(attn_input, w_qkv, preferred_element_type=f32).astype(bf16)
    attended = attend(qkv, vec)
    middle = inputs + jnp.dot(attended, w_o, preferred_element_type=f32)
    ffn_scale = rms_scale(middle)
    ffn_input = (middle * ffn_scale * g_ffn).astype(bf16)
    ffn_out, grad_ffn_in, d_w_in, d_w_out = ffn(ffn_input, top, gathered, 4, 4 + chunks, chunks)
    layer_out = split_sequence((middle + ffn_out).astype(bf16), half)

    grad_middle, grad_gain_ffn = norm_back(grad_ffn_in, middle, ffn_scale, g_ffn)
    grad_middle = grad_middle + top.astype(f32)
    grad_middle_low = grad_middle.astype(bf16)
    d_w_o = dot_tn(attended, grad_middle_low)
    grad_attended = dot_nt(grad_middle_low, w_o).astype(bf16)
    d_query, d_key, d_value, d_vec = attend_back(qkv, grad_attended, vec)
    d_qkv = jnp.concatenate([d_query, d_key, d_value], axis=1)
    d_w_qkv = dot_tn(attn_input, d_qkv)
    grad_attn_in = dot_nt(d_qkv, w_qkv)
    grad_inputs, grad_gain_attn = norm_back(grad_attn_in, inputs, attn_scale, g_attn)
    grad_tokens = split_sequence((grad_inputs + grad_middle).astype(bf16), half)

    d_table = jnp.dot(
        d_vec.reshape(2 * head_pairs, -1),
        picker.T,
        precision=lax.Precision.HIGHEST,
        preferred_element_type=f32,
    )
    table_cols = bias_table.size // own
    table_part = d_table.reshape(2, own, table_cols)
    table_high = table_part.astype(bf16)
    table_low = (table_part - table_high.astype(f32)).astype(bf16)
    repeat = lambda part: jnp.tile(part, (devices // 2, 1, 1)).reshape(width, table_cols)
    extras = jnp.concatenate(
        [
            grad_gain_attn[:, None].astype(bf16),
            grad_gain_ffn[:, None].astype(bf16),
            repeat(table_high),
            repeat(table_low),
        ],
        axis=1,
    )
    extras = jnp.pad(extras, ((0, 0), (0, -extras.shape[1] % 128)))
    grads = jnp.concatenate(
        [d_w_qkv.astype(bf16), d_w_o.astype(bf16), d_w_in, d_w_out, extras], axis=1
    )
    mine = lax.psum_scatter(grads, everyone, scatter_dimension=0, tiled=True).astype(f32)
    block = lambda at, count=1: mine[:, at * width : (at + count) * width]
    own_w_in = block(4, chunks).reshape(own, chunks, devices, own).transpose(0, 2, 1, 3)
    own_w_out = block(4 + chunks, chunks).reshape(own, chunks, width).transpose(1, 0, 2)
    rest = mine[:, (4 + 2 * chunks) * width :]
    own_table = rest[:, 2 : 2 + table_cols] + rest[:, 2 + table_cols : 2 + 2 * table_cols]
    return (
        layer_out,
        grad_tokens,
        block(0),
        block(1),
        block(2),
        block(3),
        own_w_in.reshape(w_in.shape),
        own_w_out.reshape(w_out.shape),
        rest[:, 0],
        rest[:, 1],
        own_table.reshape(bias_table.shape),
    )


def solution(mesh):
    in_specs = (
        P(None, "rows", "seq", None),
        P(None, "rows", "seq", None),
        P(("rows", "seq"), None),
        P(("rows", "seq"), None),
        P(("rows", "seq"), None),
        P(("rows", "seq"), None),
        P(("rows", "seq"), None),
        P(("rows", "seq"), None),
        P(("rows", "seq")),
        P(("rows", "seq")),
        P("seq", None),
        P(),
    )
    out_specs = (
        P(None, "rows", "seq", None),
        P(None, "rows", "seq", None),
        P(("rows", "seq"), None),
        P(("rows", "seq"), None),
        P(("rows", "seq"), None),
        P(("rows", "seq"), None),
        P(("rows", "seq"), None),
        P(("rows", "seq"), None),
        P(("rows", "seq")),
        P(("rows", "seq")),
        P("seq", None),
    )
    return jax.shard_map(shards, mesh=mesh, in_specs=in_specs, out_specs=out_specs, check_vma=False)
```

time: 1140 us -> 413 us (0.36); the launches traced: 1120 us -> 413 us
  local copies, waits for them, and re-layouts: 317 us -> 26.1 us
  waiting for transfers between devices: 460 us -> 237 us
  matrix products: 120 us -> 20.4 us
  blocking collectives: 110 us -> 20.8 us
  Pallas kernels: 0 us -> 74 us
  starting transfers between devices: 60.7 us -> 5.37 us
  other arithmetic: 39.1 us -> 14.4 us
    reduce_scatter x6 -> x0, waiting for transfers between devices: 310 us -> none  [the longest x1 142 us: shards(): lax.psum_scatter(grad_terms[4], ('rows', 'seq'), scatter_dimension=0, til...]
    unnamed x12 -> x3, waiting for transfers between devices: 3.73 us -> 136 us
    unnamed x207 -> x48, local copies, waits for them, and re-layouts: 126 us -> 12.7 us
    rev x2 -> x0, local copies, waits for them, and re-layouts: 102 us -> none  [the longest x1 51.4 us: full_bias_back(): flipped = grad_rows[:, ::-1, :]]
    dot_general x50 -> x8, matrix products: 120 us -> 20.4 us  [the longest x2 8.13 us: dot_nt(): lax.dot_general(a, b, (((1,), (1,)), ((), ())), preferred_element_type=jn...]
    unnamed x2 -> x0, blocking collectives: 79.7 us -> none
    pallas_call x0 -> x3, Pallas kernels: none -> 74 us  [the longest x1 35 us: attend_back(): pl.pallas_call(attend_back_kernel, grid=(steps,), in_specs=[spec(0), spec...]
    all_to_all x16 -> x0, starting transfers between devices: 60.2 us -> none  [the longest x2 8.47 us: shards(): lax.all_to_all(grad_keys.reshape(seq_len, 1, group_width), 'seq', split_a...]
  transfers between devices with their start and end apart: 28 -> 6, of which waited for: 15 -> 4; matrix products, arithmetic and copies ran while one was open for 40% -> 2% of each run, Pallas kernels for 0% -> 0%
where the time goes in v1:
time: 413 us
  waiting for transfers between devices  237 us (57%)
  Pallas kernels  74 us (18%)
  local copies, waits for them, and re-layouts  26.1 us (6%)
  blocking collectives  20.8 us (5%)
  matrix products  20.4 us (5%)
  between operations  14.6 us (4%)
  other arithmetic  14.4 us (3%)
  starting transfers between devices  5.37 us (1%)
    unnamed x3, waiting for transfers between devices  136 us
    all_gather x1, waiting for transfers between devices, shards(): gathered = lax.all_gather(packed, everyone, axis=0, tiled=True)  82.9 us
    pallas_call x1, Pallas kernels, attend_back(): pl.pallas_call(attend_back_kernel, grid=(steps,), in_specs=[spec(0), spec...  35 us
    all_gather x1, blocking collectives, shards(): tables = lax.all_gather(bias_table, 'seq', axis=0, tiled=True)  20.8 us
    pallas_call x1, Pallas kernels, ffn(): pl.pallas_call(ffn_kernel, grid=(chunks,), in_specs=[full, full, col(win_...  19.9 us
    pallas_call x1, Pallas kernels, attend(): pl.pallas_call(attend_kernel, grid=(steps,), in_specs=[spec(0), spec(1),...  19 us
    ppermute x2, waiting for transfers between devices, split_sequence(): received = lax.ppermute(other, 'seq', [(0, 1), (1, 0)])  17.6 us
    unnamed x48, local copies, waits for them, and re-layouts  12.7 us
  transfers between devices with their start and end apart: 6, of which 4 were waited for; matrix products, arithmetic and copies ran while one was open for 2% of the time, Pallas kernels for 0%

profile of v1, /device:TPU:0, one launch (start us, length us, event | category | flops | bytes accessed | tf_op | source)
XLA Modules:
  0.0 412.5 jit_solution(12893077953800378157)
XLA Ops:
  8.0 2.2 reshape.151
  10.4 1.3 reshape.152
  12.9 3.0 collective-permute-start
  16.1 20.8 %all-gather = f32[2,6,32]{2,1,0:T(8,128)S(1)} all-gather(f32[1,6,32]{2,1,0:T(8,128)S(1)} %bitcast.58), channel_id=1, replica_groups=mesh['rows'=16,'seq'=2] {'seq'}, dimensions={0}, use_global_device_ids=true | all-gather | bytes 2304 | tf_op jit(solution)/shard_map/all_gather | solution.py:203
  37.4 1.1 bitcast_select_fusion.1
  39.4 82.9 %all-gather.3.cloned.1.call-done.win_ref.wout_ref = bf16[768,9344]{1,0:T(8,128)(2,1)} async-done(((bf16[24,9344]{1,0:T(8,128)(2,1)}), bf16[768,9344]{1,0:T(8,128)(2,1)}) %all-gather.3.cloned.1.call-update) | async-done | bytes 14352400 | tf_op jit(solution)/shard_map/all_gather | solution.py:195
  122.4 1.3 convert_reduce_fusion
  123.7 4.1 convolution_convert_fusion.1.q_ref.k_ref.v_ref
  127.8 19.0 %shard_map.203 = bf16[512,768]{1,0:T(8,128)(2,1)S(1)} custom-call(bf16[512,2304]{1,0:T(8,128)(2,1)S(1)} %convolution_convert_fusion.1.q_ref.k_ref.v_ref, bf16[512,2304]{1,0:T(8,128)(2,1)S(1)} %convolution_convert_fusion.1.q_ref.k_ref.v_ref, bf16[512,2304]{1,0:T(8,128)(2,1)S(1)} %convolution_convert_fusion.1.q_ref.k_ref.v_ref, f32[6,2,1024]{2,1,0:T(2,128)S(1)} %reshape.155.vec_ref), custom_call_target="tpu_custom_call" | custom-call | tf_op jit(solution)/shard_map/pallas_call | solution.py:49
  146.8 2.1 multiply_reduce_fusion.2
  149.0 1.1 multiply_convert_fusion.x_ref
  150.0 19.9 %shard_map.204 = (f32[512,768]{1,0:T(8,128)}, f32[512,768]{1,0:T(8,128)}, bf16[768,3072]{1,0:T(8,128)(2,1)}, bf16[768,3072]{1,0:T(8,128)(2,1)}) custom-call(bf16[512,768]{1,0:T(8,128)(2,1)} %multiply_convert_fusion.x_ref, bf16[512,768]{1,0:T(8,128)(2,1)} %pad_maximum_fusion.1.top_ref, bf16[768,9344]{1,0:T(8,128)(2,1)} %all-gather.3.cloned.1.call-done.win_ref.wout_ref, ...), custom_call_target="tpu_custom_call" | custom-call | tf_op jit(solution)/shard_map/pallas_call | solution.py:120
  170.0 2.0 multiply_reduce_fusion
  172.3 1.4 convert_add_fusion.1
  173.7 2.1 convolution_convert_fusion.3.go_ref
  175.8 35.0 %shard_map.205 = (bf16[512,768]{1,0:T(8,128)(2,1)S(1)}, bf16[512,768]{1,0:T(8,128)(2,1)S(1)}, bf16[512,768]{1,0:T(8,128)(2,1)S(1)}, f32[6,2,1024]{2,1,0:T(2,128)S(1)}) custom-call(bf16[512,2304]{1,0:T(8,128)(2,1)S(1)} %convolution_convert_fusion.1.q_ref.k_ref.v_ref, bf16[512,2304]{1,0:T(8,128)(2,1)S(1)} %convolution_convert_fusion.1.q_ref.k_ref.v_ref, ...), custom_call_target="tpu_custom_call" | custom-call | tf_op jit(solution)/shard_map/pallas_call | solution.py:90
  211.0 3.9 fusion
  214.9 1.9 fusion.14
  217.5 6.1 %fusion.13 = (bf16[768]{0:T(1024)(128)(2,1)S(1)}, f32[512]{0:T(512)S(1)}, f32[512,768]{1,0:T(8,128)}) fusion(f32[512]{0:T(512)S(1)} %get-tuple-element.98, bf16[256,768]{1,0:T(8,128)(2,1)S(1)} %get-tuple-element.90, bf16[256,768]{1,0:T(8,128)(2,1)S(1)} %get-tuple-element.89, f32[768]{0:T(1024)S(1)} %get-tuple-element.72, bf16[512,2304]{1,0:T(8,128)(2,1)} %copy-done.9, ...), kind=kOutput, calls=%fused_computation.21 | convolution fusion | flops 1815870208 | bytes 8266240 | tf_op jit(solution)/shard_map/dot_general | solution.py:25
  223.8 4.8 %constant_dynamic-update-slice_fusion.11 = bf16[768,9344]{1,0:T(8,128)(2,1)} fusion(bf16[768,9344]{1,0:T(8,128)(2,1)} %fusion.14, bf16[768,3072]{1,0:T(8,128)(2,1)} %get-tuple-element.24), kind=kLoop, calls=%fused_computation.69 | loop fusion | bytes 9437184
  228.6 4.9 %constant_dynamic-update-slice_fusion.10 = bf16[768,9344]{1,0:T(8,128)(2,1)} fusion(bf16[768,9344]{1,0:T(8,128)(2,1)} %constant_dynamic-update-slice_fusion.11, bf16[768,3072]{1,0:T(8,128)(2,1)} %get-tuple-element.25), kind=kLoop, calls=%fused_computation.68 | loop fusion | bytes 9437184
  234.3 1.9 fusion.10
  237.1 1.5 collective-permute-start.3
  239.3 9.8 %collective-permute-done.3 = bf16[256,768]{1,0:T(8,128)(2,1)S(1)} collective-permute-done((bf16[256,768]{1,0:T(8,128)(2,1)S(1)}, bf16[256,768]{1,0:T(8,128)(2,1)S(1)}, u32[]{:S(2)}, u32[]{:S(2)}) %collective-permute-start.3) | collective-permute-done | bytes 393248 | tf_op jit(solution)/shard_map/ppermute | solution.py:161
  249.1 7.8 %collective-permute-done.2 = bf16[256,768]{1,0:T(8,128)(2,1)S(1)} collective-permute-done((bf16[256,768]{1,0:T(8,128)(2,1)S(1)}, bf16[256,768]{1,0:T(8,128)(2,1)S(1)}, u32[]{:S(2)}, u32[]{:S(2)}) %collective-permute-start.2) | collective-permute-done | bytes 393248 | tf_op jit(solution)/shard_map/ppermute | solution.py:161
  256.9 1.3 select_bitcast_fusion.1
  258.2 0.9 maximum_bitcast_fusion
  260.1 136.4 %reduce-scatter.4.cloned.1.call-done = bf16[24,9344]{1,0:T(8,128)(2,1)} async-done(((bf16[768,9344]{1,0:T(8,128)(2,1)}), bf16[24,9344]{1,0:T(8,128)(2,1)}) %reduce-scatter.4.cloned.1.call-update) | async-done | bytes 448528
  396.5 1.1 convert_element_type.135
  398.4 1.1 reshape.158
  399.6 1.2 copy.63
  400.8 2.6 reshape.159
  (98 shorter events, 11.5 us)
Async XLA Ops:
  7.2 115.2 %all-gather.3.cloned.1.call-start = ((), (), s32[]{:S(2)}) async-start(), calls=%async_computation.1 | async-start | bytes 14800896 | tf_op jit(solution)/shard_map/all_gather | solution.py:195
  8.0 3.7 copy-start.10
  10.2 1.6 copy-start.16
  10.2 1.6 copy-start.17
  10.2 1.7 copy-start.11
  10.2 1.7 copy-start.12
  10.2 1.7 copy-start.13
  10.4 2.5 copy-start.6
  11.6 4.3 %copy-start.7 = (bf16[2,1,256,768]{3,2,1,0:T(8,128)(2,1)S(1)}, bf16[2,1,256,768]{3,2,1,0:T(8,128)(2,1)}, u32[]{:S(2)}) copy-start(bf16[2,1,256,768]{3,2,1,0:T(8,128)(2,1)} %param.13) | copy-start | bytes 2359300
  11.7 4.4 %copy-start.14 = (f32[6,32]{1,0:T(8,128)S(1)}, f32[6,32]{1,0:T(8,128)}, u32[]{:S(2)}) copy-start(f32[6,32]{1,0:T(8,128)} %param.22) | copy-start | bytes 2308
  11.7 25.1 %copy-start.15 = (s32[1023]{0:T(1024)S(1)}, s32[1023]{0:T(1024)}, u32[]{:S(2)}) copy-start(s32[1023]{0:T(1024)} %param.23) | copy-start | bytes 12280
  12.0 0.8 copy-start.8
  12.8 383.6 %reduce-scatter.4.cloned.1.call-start = ((), (), s32[]{:S(2)}) async-start(), calls=%async_computation.2 | async-start | bytes 14800896
  12.9 24.2 %collective-permute-start = (bf16[256,768]{1,0:T(8,128)(2,1)S(1)}, bf16[256,768]{1,0:T(8,128)(2,1)S(1)}, u32[]{:S(2)}, u32[]{:S(2)}) collective-permute-start(bf16[256,768]{1,0:T(8,128)(2,1)S(1)} %dynamic-slice_bitcast_fusion.1), channel_id=1, source_target_pairs={{0,1},{1,0},{2,3},{3,2},{4,5},{5,4},{6,7},{7,6},{8,9},{9,8},{10,11... | collective-permute-start | bytes 1179656 | tf_op jit(solution)/shard_map/ppermute | solution.py:145
  16.0 21.4 %collective-permute-start.1 = (bf16[256,768]{1,0:T(8,128)(2,1)S(1)}, bf16[256,768]{1,0:T(8,128)(2,1)}, u32[]{:S(2)}, u32[]{:S(2)}) collective-permute-start(bf16[256,768]{1,0:T(8,128)(2,1)S(1)} %dynamic-slice_bitcast_fusion), channel_id=1, source_target_pairs={{0,1},{1,0},{2,3},{3,2},{4,5},{5,4},{6,7},{7,6},{8,9},{9,8},{10,11... | collective-permute-start | bytes 1179656 | tf_op jit(solution)/shard_map/ppermute | solution.py:145
  170.0 2.0 copy-start
  170.0 2.4 copy-start.5
  211.0 3.9 copy-start.9
  234.3 4.4 %copy-start.3 = (bf16[512,768]{1,0:T(8,128)(2,1)S(1)}, bf16[512,768]{1,0:T(8,128)(2,1)}, u32[]{:S(2)}) copy-start(bf16[512,768]{1,0:T(8,128)(2,1)} %get-tuple-element.82) | copy-start | bytes 2359300
  236.2 0.9 copy-start.4
  237.1 12.0 %collective-permute-start.3 = (bf16[256,768]{1,0:T(8,128)(2,1)S(1)}, bf16[256,768]{1,0:T(8,128)(2,1)S(1)}, u32[]{:S(2)}, u32[]{:S(2)}) collective-permute-start(bf16[256,768]{1,0:T(8,128)(2,1)S(1)} %constant_dynamic-slice_fusion), channel_id=1, source_target_pairs={{0,1},{1,0},{2,3},{3,2},{4,5},{5,4},{6,7},{7,6},{8,9},{9,8},{10,11... | collective-permute-start | bytes 1179656 | tf_op jit(solution)/shard_map/ppermute | solution.py:161
  238.7 18.2 %collective-permute-start.2 = (bf16[256,768]{1,0:T(8,128)(2,1)S(1)}, bf16[256,768]{1,0:T(8,128)(2,1)S(1)}, u32[]{:S(2)}, u32[]{:S(2)}) collective-permute-start(bf16[256,768]{1,0:T(8,128)(2,1)S(1)} %constant_dynamic-slice_fusion.1), channel_id=1, source_target_pairs={{0,1},{1,0},{2,3},{3,2},{4,5},{5,4},{6,7},{7,6},{8,9},{9,8},{10,11... | collective-permute-start | bytes 1179656 | tf_op jit(solution)/shard_map/ppermute | solution.py:161
  396.5 1.9 copy-start.1
  400.8 4.1 %copy-start.2 = (bf16[24,9344]{1,0:T(8,128)(2,1)S(1)}, bf16[24,9344]{1,0:T(8,128)(2,1)}, u32[]{:S(2)}) copy-start(bf16[24,9344]{1,0:T(8,128)(2,1)} %reduce-scatter.4.cloned.1.call-done) | copy-start | bytes 1345540
Sparse Core Ops, SparseCore 0:
  12.9 109.3 all-gather.2
  234.4 162.0 reduce-scatter.3

commit v2 on v1

v2 whole, which is shorter than its diff:
```python
import jax
import jax.numpy as jnp
from jax import lax
from jax.experimental import pallas as pl
from jax.experimental.pallas import tpu as pltpu
from jax.sharding import PartitionSpec as P

HD = 64
RB = 128
epsilon = 1e-06


def bias_slab(vec):
    wide = jnp.broadcast_to(vec, (RB, vec.shape[1]))
    return pltpu.roll(wide, vec.shape[1] - RB + 1, 1, stride=1, stride_axis=0)


def diag_sums(slab):
    rows = slab.shape[0]
    while rows > 1:
        rows //= 2
        slab = pltpu.roll(slab[:rows], rows, 1) + slab[rows:]
    return slab


def dot_nt(a, b):
    return lax.dot_general(a, b, (((1,), (1,)), ((), ())), preferred_element_type=jnp.float32)


def dot_nn(a, b):
    return lax.dot_general(a, b, (((1,), (0,)), ((), ())), preferred_element_type=jnp.float32)


def dot_tn(a, b):
    return lax.dot_general(a, b, (((0,), (0,)), ((), ())), preferred_element_type=jnp.float32)


def attend_kernel(q_ref, k_ref, v_ref, vec_ref, o_ref):
    length = q_ref.shape[0]
    for head in range(2):
        cols = slice(head * HD, (head + 1) * HD)
        k = k_ref[:, cols]
        v = v_ref[:, cols]
        slab = bias_slab(vec_ref[0, head : head + 1, :])
        for first in range(0, length, RB):
            lane = length - RB - first
            s = dot_nt(q_ref[first : first + RB, cols], k) + slab[:, lane : lane + length]
            e = jnp.exp(s - jnp.max(s, axis=1, keepdims=True))
            p = e * (1.0 / jnp.sum(e, axis=1, keepdims=True))
            o_ref[first : first + RB, cols] = dot_nn(p.astype(jnp.bfloat16), v).astype(jnp.bfloat16)


def attend(qkv, vec, start, count):
    length, width = qkv.shape[0], qkv.shape[1] // 3
    steps = width // (2 * HD)
    spec = lambda at: pl.BlockSpec((length, 2 * HD), lambda h: (0, at + h))
    return pl.pallas_call(
        attend_kernel,
        grid=(count,),
        in_specs=[
            spec(start),
            spec(steps + start),
            spec(2 * steps + start),
            pl.BlockSpec((1, 2, vec.shape[2]), lambda h: (start + h, 0, 0)),
        ],
        out_specs=spec(0),
        out_shape=jax.ShapeDtypeStruct((length, count * 2 * HD), jnp.bfloat16),
        cost_estimate=pl.CostEstimate(
            flops=20 * length * length * 2 * HD * count,
            bytes_accessed=8 * length * 2 * HD * count,
            transcendentals=0,
        ),
        compiler_params=pltpu.CompilerParams(vmem_limit_bytes=48 << 20),
    )(qkv, qkv, qkv, vec)


def attend_back_kernel(
    q_ref, k_ref, v_ref, go_ref, vec_ref, dq_ref, dk_ref, dv_ref, dvec_ref, slab_ref
):
    length = q_ref.shape[0]
    for head in range(2):
        cols = slice(head * HD, (head + 1) * HD)
        k = k_ref[:, cols]
        v = v_ref[:, cols]
        slab = bias_slab(vec_ref[0, head : head + 1, :])
        slab_ref[...] = jnp.zeros(slab_ref.shape, jnp.float32)
        dk = jnp.zeros((length, HD), jnp.float32)
        dv = jnp.zeros((length, HD), jnp.float32)
        for first in range(0, length, RB):
            lane = length - RB - first
            rows = slice(first, first + RB)
            q = q_ref[rows, cols]
            go = go_ref[rows, cols]
            s = dot_nt(q, k) + slab[:, lane : lane + length]
            e = jnp.exp(s - jnp.max(s, axis=1, keepdims=True))
            p = e * (1.0 / jnp.sum(e, axis=1, keepdims=True))
            gp = dot_nt(go, v)
            center = jnp.sum(p * gp, axis=1, keepdims=True)
            ds = (p * (gp - center)).astype(jnp.bfloat16)
            slab_ref[:, lane : lane + length] += ds.astype(jnp.float32)
            dq_ref[rows, cols] = dot_nn(ds, k).astype(jnp.bfloat16)
            dk += dot_tn(ds, q)
            dv += dot_tn(p.astype(jnp.bfloat16), go)
        dk_ref[:, cols] = dk.astype(jnp.bfloat16)
        dv_ref[:, cols] = dv.astype(jnp.bfloat16)
        dvec_ref[0, head : head + 1, :] = diag_sums(slab_ref[...])


def attend_back(qkv, go, vec, start, count):
    length, width = go.shape
    steps = width // (2 * HD)
    spec = lambda at: pl.BlockSpec((length, 2 * HD), lambda h: (0, at + h))
    vspec = lambda at: pl.BlockSpec((1, 2, vec.shape[2]), lambda h: (at + h, 0, 0))
    o = jax.ShapeDtypeStruct((length, count * 2 * HD), jnp.bfloat16)
    return pl.pallas_call(
        attend_back_kernel,
        grid=(count,),
        in_specs=[
            spec(start),
            spec(steps + start),
            spec(2 * steps + start),
            spec(start),
            vspec(start),
        ],
        out_specs=[spec(0), spec(0), spec(0), vspec(0)],
        out_shape=[o, o, o, jax.ShapeDtypeStruct((count,) + vec.shape[1:], jnp.float32)],
        scratch_shapes=[pltpu.VMEM((RB, vec.shape[2]), jnp.float32)],
        cost_estimate=pl.CostEstimate(
            flops=36 * length * length * 2 * HD * count,
            bytes_accessed=8 * length * 2 * HD * count,
            transcendentals=0,
        ),
        compiler_params=pltpu.CompilerParams(vmem_limit_bytes=48 << 20),
    )(qkv, qkv, qkv, go, vec)


def ffn_step(x_ref, top_ref, win_ref, wout_ref, out_ref, gx_ref):
    x = x_ref[...]
    top = top_ref[...]
    pre = dot_nn(x, win_ref[...])
    sig = 1.0 / (1.0 + jnp.exp(-pre))
    hid = (pre * sig).astype(jnp.bfloat16)
    gact = dot_nt(top, wout_ref[...])
    gpre = (gact * (sig * (1.0 + pre * (1.0 - sig)))).astype(jnp.bfloat16)

    @pl.when(pl.program_id(0) == 0)
    def _():
        out_ref[...] = jnp.zeros(out_ref.shape, jnp.float32)
        gx_ref[...] = jnp.zeros(gx_ref.shape, jnp.float32)

    out_ref[...] += dot_nn(hid, wout_ref[...])
    gx_ref[...] += dot_nt(gpre, win_ref[...])
    return dot_tn(x, gpre).astype(jnp.bfloat16), dot_tn(hid, top).astype(jnp.bfloat16)


def store_blocks(seat_ref, value, rows, blocks, keep_ref, send_ref, put):
    for core in range(2):

        @pl.when(seat_ref[0] == core)
        def _():
            for block in range(blocks):
                ref = keep_ref if (block >> 1 & 1) == core else send_ref
                x = (block >> 2 & 1) ^ seat_ref[1]
                y = (block & 1) ^ seat_ref[2]
                put(ref, x, y, block >> 3, value[block * rows : (block + 1) * rows])


def ffn_kernel(
    seat_ref,
    x_ref,
    top_ref,
    win_ref,
    wout_ref,
    out_ref,
    gx_ref,
    in_keep_ref,
    in_send_ref,
    out_keep_ref,
    out_send_ref,
):
    d_in, d_out = ffn_step(x_ref, top_ref, win_ref, wout_ref, out_ref, gx_ref)
    own = in_keep_ref.shape[4]

    def put_in(ref, x, y, far, block):
        ref[x, y, far ^ seat_ref[3], 0] = block

    def put_out(ref, x, y, far, block):
        ref[x, y, 0] = block

    store_blocks(seat_ref, d_in, own, d_in.shape[0] // own, in_keep_ref, in_send_ref, put_in)
    tall = out_keep_ref.shape[3]
    store_blocks(seat_ref, d_out, tall, 8, out_keep_ref, out_send_ref, put_out)


def ffn_plain_kernel(x_ref, top_ref, win_ref, wout_ref, out_ref, gx_ref, d_in_ref, d_out_ref):
    d_in, d_out = ffn_step(x_ref, top_ref, win_ref, wout_ref, out_ref, gx_ref)
    d_in_ref[...] = d_in
    d_out_ref[...] = d_out


def ffn(x, top, w_in, w_out, ranks):
    length, width = x.shape
    chunks = w_in.shape[1] // width
    own = width // ranks.devices
    far = ranks.devices // 8
    f = jax.ShapeDtypeStruct((length, width), jnp.float32)
    cost = pl.CostEstimate(
        flops=12 * length * width * chunks * width,
        bytes_accessed=8 * chunks * width * width,
        transcendentals=0,
    )
    params = pltpu.CompilerParams(vmem_limit_bytes=56 << 20)
    if own % 8 or far != chunks:
        full = pl.BlockSpec((length, width), lambda j: (0, 0))
        column = pl.BlockSpec((width, width), lambda j: (0, j))
        row = pl.BlockSpec((width, width), lambda j: (j, 0))
        out, gx, d_in, d_out = pl.pallas_call(
            ffn_plain_kernel,
            grid=(chunks,),
            in_specs=[full, full, column, row],
            out_specs=[full, full, column, row],
            out_shape=[
                f,
                f,
                jax.ShapeDtypeStruct(w_in.shape, jnp.bfloat16),
                jax.ShapeDtypeStruct(w_out.shape, jnp.bfloat16),
            ],
            cost_estimate=cost,
            compiler_params=params,
        )(x, top, w_in, w_out)
        d_in = d_in.reshape(ranks.devices, own, chunks, width).transpose(0, 2, 1, 3)
        d_out = d_out.reshape(ranks.devices, own * chunks, width)
        return out, gx, ranks.by_seat(d_in), ranks.by_seat(d_out)
    full = pl.BlockSpec((length, width), lambda j, seat: (0, 0))
    column = pl.BlockSpec((width, width), lambda j, seat: (0, j))
    row = pl.BlockSpec((width, width), lambda j, seat: (j, 0))
    d_in_spec = pl.BlockSpec((2, 2, far, 1, own, width), lambda j, seat: (0, 0, 0, j, 0, 0))
    tall = own * chunks
    d_out_spec = pl.BlockSpec((2, 2, 1, tall, width), lambda j, seat: (0, 0, j ^ seat[3], 0, 0))
    d_in = jax.ShapeDtypeStruct((2, 2, far, chunks, own, width), jnp.bfloat16)
    d_out = jax.ShapeDtypeStruct((2, 2, far, tall, width), jnp.bfloat16)
    out, gx, in_keep, in_send, out_keep, out_send = pl.pallas_call(
        ffn_kernel,
        grid_spec=pltpu.PrefetchScalarGridSpec(
            num_scalar_prefetch=1,
            grid=(chunks,),
            in_specs=[full, full, column, row],
            out_specs=[full, full, d_in_spec, d_in_spec, d_out_spec, d_out_spec],
        ),
        out_shape=[f, f, d_in, d_in, d_out, d_out],
        cost_estimate=cost,
        compiler_params=params,
    )(ranks.seat, x, top, w_in, w_out)
    return out, gx, (in_keep, in_send), (out_keep, out_send)


def weight_grads_kernel(
    seat_ref,
    x_ref,
    dq_ref,
    dk_ref,
    dv_ref,
    a_ref,
    gm_ref,
    extra_ref,
    qk_keep_ref,
    qk_send_ref,
    vo_keep_ref,
    vo_send_ref,
):
    x = x_ref[...]
    own = qk_keep_ref.shape[3] // 2
    blocks = x.shape[1] // own
    for lhs, rhs, keep_ref, send_ref, at in (
        (x, dq_ref, qk_keep_ref, qk_send_ref, 0),
        (x, dk_ref, qk_keep_ref, qk_send_ref, own),
        (x, dv_ref, vo_keep_ref, vo_send_ref, 0),
        (a_ref[...], gm_ref, vo_keep_ref, vo_send_ref, own),
    ):

        def put(ref, x, y, far, block):
            ref[x, y, far ^ seat_ref[3], at : at + own, :] = block

        value = dot_tn(lhs, rhs[...]).astype(jnp.bfloat16)
        store_blocks(seat_ref, value, own, blocks, keep_ref, send_ref, put)

    def put_extra(ref, x, y, far, block):
        ref[x, y, far ^ seat_ref[3], 2 * own :, :] = block

    store_blocks(seat_ref, extra_ref[...], 8, blocks, vo_keep_ref, vo_send_ref, put_extra)


def weight_grads(x, d_query, d_key, d_value, attended, grad_low, extra, ranks):
    width = x.shape[1]
    own = width // ranks.devices
    far = ranks.devices // 8
    if own % 8:
        block = lambda a, b: dot_tn(a, b).astype(jnp.bfloat16).reshape(ranks.devices, own, width)
        qk = jnp.concatenate([block(x, d_query), block(x, d_key)], axis=1)
        extra = extra.reshape(ranks.devices, 8, width)
        vo = jnp.concatenate([block(x, d_value), block(attended, grad_low), extra], axis=1)
        return ranks.by_seat(qk), ranks.by_seat(vo)
    qk = jax.ShapeDtypeStruct((2, 2, far, 2 * own, width), jnp.bfloat16)
    vo = jax.ShapeDtypeStruct((2, 2, far, 2 * own + 8, width), jnp.bfloat16)
    whole = lambda a: pl.BlockSpec(a.shape, lambda i, seat: (0,) * len(a.shape))
    args = (x, d_query, d_key, d_value, attended, grad_low, extra)
    outs = pl.pallas_call(
        weight_grads_kernel,
        grid_spec=pltpu.PrefetchScalarGridSpec(
            num_scalar_prefetch=1,
            grid=(1,),
            in_specs=[whole(a) for a in args],
            out_specs=[whole(a) for a in (qk, qk, vo, vo)],
        ),
        out_shape=[qk, qk, vo, vo],
        cost_estimate=pl.CostEstimate(
            flops=8 * x.shape[0] * width * width,
            bytes_accessed=8 * width * width,
            transcendentals=0,
        ),
        compiler_params=pltpu.CompilerParams(vmem_limit_bytes=56 << 20),
    )(ranks.seat, *args)
    return (outs[0], outs[1]), (outs[2], outs[3])


def rms_scale(values):
    return lax.rsqrt(jnp.mean(values * values, axis=-1, keepdims=True) + epsilon)


def norm_back(grad_out, values, inv_rms, gain):
    scaled = grad_out * gain
    inner = jnp.mean(scaled * values, axis=-1, keepdims=True)
    grad_in = inv_rms * scaled - values * (inv_rms * inv_rms * inv_rms) * inner
    return grad_in, jnp.sum(grad_out * values * inv_rms, axis=0)


def bucket_picker(buckets, bucket_count):
    padded = jnp.pad(buckets, (0, 1), constant_values=-1)
    rows = jnp.arange(bucket_count, dtype=jnp.int32)[:, None]
    return (padded[None, :] == rows).astype(jnp.float32)


def swap_halves(mine, other, half):
    received = lax.ppermute(other, "seq", [(0, 1), (1, 0)])
    first = jnp.where(half == 0, mine, received)
    second = jnp.where(half == 0, received, mine)
    return jnp.concatenate([first, second], axis=-2)


def whole_sequence(array, half):
    mine = lax.dynamic_index_in_dim(array, half, 0, keepdims=False)[0]
    other = lax.dynamic_index_in_dim(array, 1 - half, 0, keepdims=False)[0]
    return swap_halves(mine, other, half)


def split_sequence(array, half):
    rows = array.shape[0] // 2
    mine = lax.dynamic_slice_in_dim(array, half * rows, rows, 0)
    other = lax.dynamic_slice_in_dim(array, (1 - half) * rows, rows, 0)
    received = lax.ppermute(other, "seq", [(0, 1), (1, 0)])
    first = jnp.where(half == 0, mine, received)
    second = jnp.where(half == 0, received, mine)
    return jnp.stack([first, second])[:, None]


def partner_sends(array, mask, devices):
    return lax.ppermute(array, ("rows", "seq"), [(b, b ^ mask) for b in range(devices)])


def together(first, second):
    return lax.optimization_barrier((first, second))


class Ranks:
    def __init__(self):
        self.devices = lax.axis_size("rows") * lax.axis_size("seq")
        self.count = self.devices.bit_length() - 1
        rank = lax.axis_index("rows") * lax.axis_size("seq") + lax.axis_index("seq")
        rank = rank.astype(jnp.int32)
        self.bits = [(rank >> b) & 1 for b in range(self.count)]
        self.seat = jnp.stack([self.bits[1], self.bits[2], self.bits[0], rank >> 3])
        far = list(range(3, self.count))
        self.far_groups = [far[at : at + 2] for at in range(0, len(far), 2)]

    def by_seat(self, array):
        far = self.devices // 8
        grid = array.reshape((far, 2, 2, 2) + array.shape[1:])
        for axis, bit in ((1, 2), (2, 1), (3, 0)):
            grid = jnp.where(self.bits[bit] == 0, grid, jnp.flip(grid, axis))
        order = jnp.arange(far, dtype=jnp.int32) ^ self.seat[3]
        grid = jnp.take(grid, order, axis=0)
        grid = jnp.moveaxis(grid, 0, 3)
        return grid[:, 0], grid[:, 1]


def group_masks(group):
    for code in range(1, 1 << len(group)):
        yield sum(1 << bit for at, bit in enumerate(group) if code >> at & 1)


class Gather:
    def __init__(self, ranks, shard, held=()):
        self.ranks, self.value, self.held = ranks, shard, list(held)

    def send(self, group):
        self.group = group
        self.arrived = {
            mask: partner_sends(self.value, mask, self.ranks.devices) for mask in group_masks(group)
        }

    def merge(self):
        by_mask = {0: self.value, **self.arrived}
        for bit in self.group:
            self.held = sorted(self.held + [bit], reverse=True)
            axis = self.held.index(bit)
            flag = self.ranks.bits[bit] == 0
            merged = {}
            for mask in by_mask:
                if mask >> bit & 1:
                    continue
                here, there = by_mask[mask], by_mask[mask | 1 << bit]
                merged[mask] = jnp.stack(
                    [jnp.where(flag, here, there), jnp.where(flag, there, here)], axis=axis
                )
            by_mask = merged
        self.value = by_mask[0]

    def blocks(self):
        return self.value.reshape((-1,) + self.value.shape[-2:])


class Scatter:
    def __init__(self, ranks, halves, near):
        self.ranks, self.near = ranks, near
        self.terms, self.outgoing = [halves[0]], [halves[1]]

    def send(self, masks):
        self.arrived = [
            partner_sends(array, mask, self.ranks.devices)
            for array, mask in zip(self.outgoing, masks)
        ]

    def total(self, pick):
        return sum(pick(term).astype(jnp.float32) for term in self.terms)

    def take_core(self):
        self.terms += self.arrived
        self.axis = 0 if self.near == 2 else 1
        self.split(self.axis)

    def split(self, axis):
        side = lambda at: lambda term: lax.index_in_dim(term, at, axis, keepdims=False)
        self.outgoing = [self.total(side(1)).astype(jnp.bfloat16)]
        self.terms = [side(0)(term) for term in self.terms]

    def take_near(self):
        self.terms += self.arrived
        self.split(0)

    def take_next(self):
        self.terms += self.arrived
        far = self.terms[0].shape[0]
        self.outgoing = [
            self.total(lambda term: term[at]).astype(jnp.bfloat16) for at in range(1, far)
        ]
        self.terms = [term[0] for term in self.terms]

    def take_far(self):
        self.terms += self.arrived
        return self.total(lambda term: term)

    def far_masks(self):
        return [at << 3 for at in range(1, self.ranks.devices // 8)]


def begin(scatters):
    for scatter in scatters:
        scatter.send([2])


def advance(scatters, stage, waited):
    arrived, waited = together([scatter.arrived for scatter in scatters], waited)
    for scatter, got in zip(scatters, arrived):
        scatter.arrived = got
        (scatter.take_core, scatter.take_near, scatter.take_next)[stage]()
    outgoing, waited = together([scatter.outgoing for scatter in scatters], waited)
    for scatter, out in zip(scatters, outgoing):
        scatter.outgoing = out
        near = 1 << scatter.near
        scatter.send(([near], [5 - near], scatter.far_masks())[stage])
    return waited


def shards(
    tokens,
    cotangent,
    w_query,
    w_key,
    w_value,
    w_output,
    w_in,
    w_out,
    gain_attn,
    gain_ffn,
    bias_table,
    buckets,
):
    ranks = Ranks()
    devices = ranks.devices
    half = lax.axis_index("seq")
    own, width = w_query.shape
    chunks = w_in.shape[1] // width
    head_pairs = width // (2 * HD)
    bf16, f32 = jnp.bfloat16, jnp.float32

    w_in_all = lax.all_gather(w_in, ("rows", "seq"), axis=0, tiled=True)
    gains = jnp.pad(jnp.stack([gain_attn, gain_ffn], axis=1), ((0, 0), (0, 126)))
    first = Gather(ranks, jnp.concatenate([w_query, w_key, w_value, gains], axis=1))
    second = Gather(ranks, jnp.concatenate([w_output, w_out], axis=0))
    for group in ranks.far_groups:
        first.send(group)
        first.arrived, second.value = together(first.arrived, second.value)
        first.merge()
    inputs = whole_sequence(tokens, half).astype(f32)
    cut = width // 2 * 3
    pair = [
        Gather(ranks, first.value[..., :cut], first.held),
        Gather(ranks, first.value[..., cut:], first.held),
    ]
    pair[0].send([2])
    pair[1].send([0])
    for group in ranks.far_groups:
        second.send(group)
        second.merge()
    for part in pair:
        part.merge()
    pair[0].send([0])
    pair[1].send([2])
    arrived, second.value = together([part.arrived for part in pair], second.value)
    for part, got in zip(pair, arrived):
        part.arrived = got
        part.merge()
        part.send([1])
    cut = max(second.value.shape[-2] // 16 * 8, own)
    late = [
        Gather(ranks, second.value[..., :cut, :], second.held),
        Gather(ranks, second.value[..., cut:, :], second.held),
    ]
    late[0].send([2])
    late[1].send([0])
    for part in pair:
        part.merge()
    w_qkv = jnp.concatenate(
        [part.value.reshape(-1, part.value.shape[-1]) for part in pair], axis=1
    )
    g_attn = w_qkv[:, 3 * width].astype(f32)
    g_ffn = w_qkv[:, 3 * width + 1].astype(f32)
    w_qkv = w_qkv[:, : 3 * width]

    other_table = lax.ppermute(bias_table, "seq", [(0, 1), (1, 0)])
    tables = jnp.where(
        half == 0,
        jnp.concatenate([bias_table, other_table]),
        jnp.concatenate([other_table, bias_table]),
    )
    picker = bucket_picker(buckets, bias_table.shape[1])
    vec = jnp.dot(tables, picker, precision=lax.Precision.HIGHEST, preferred_element_type=f32)
    vec = vec.reshape(head_pairs, 2, -1)

    attn_scale = rms_scale(inputs)
    attn_input = (inputs * attn_scale * g_attn).astype(bf16)
    qkv = jnp.dot(attn_input, w_qkv, preferred_element_type=f32).astype(bf16)
    cotangent, qkv = together(cotangent, qkv)
    top = whole_sequence(cotangent, half)
    each = head_pairs // 2
    left = attend(qkv, vec, 0, each)
    arrived, left, qkv = lax.optimization_barrier(([part.arrived for part in late], left, qkv))
    for part, got in zip(late, arrived):
        part.arrived = got
        part.merge()
    values, qkv = together([part.value for part in late], qkv)
    for part, got in zip(late, values):
        part.value = got
    late[0].send([0])
    late[1].send([2])
    right = attend(qkv, vec, each, each)
    arrived, right = together([part.arrived for part in late], right)
    for part, got in zip(late, arrived):
        part.arrived = got
        part.merge()
        part.send([1])
        part.merge()
    low, high = [part.blocks() for part in late]
    w_o = low[:, :own].reshape(width, width)
    w_out_all = jnp.concatenate([low[:, own:], high], axis=1).reshape(-1, width)
    attended = jnp.concatenate([left, right], axis=1)
    middle = inputs + jnp.dot(attended, w_o, preferred_element_type=f32)
    ffn_scale = rms_scale(middle)
    ffn_input = (middle * ffn_scale * g_ffn).astype(bf16)
    ffn_out, grad_ffn_in, d_w_in, d_w_out = ffn(ffn_input, top, w_in_all, w_out_all, ranks)
    big = [Scatter(ranks, d_w_in, 2), Scatter(ranks, d_w_out, 0)]
    begin(big)

    grad_middle, grad_gain_ffn = norm_back(grad_ffn_in, middle, ffn_scale, g_ffn)
    grad_middle = grad_middle + top.astype(f32)
    grad_middle_low = grad_middle.astype(bf16)
    grad_attended = dot_nt(grad_middle_low, w_o).astype(bf16)
    grad_attended = advance(big, 0, grad_attended)
    layer_low, grad_attended = together((middle + ffn_out).astype(bf16), grad_attended)
    layer_out = split_sequence(layer_low, half)
    each = head_pairs // 3
    piece_0 = attend_back(qkv, grad_attended, vec, 0, each)
    piece_0, grad_attended = together(piece_0, grad_attended)
    piece_1 = attend_back(qkv, grad_attended, vec, each, each)
    piece_1, grad_attended = advance(big, 1, (piece_1, grad_attended))
    piece_2 = attend_back(qkv, grad_attended, vec, 2 * each, each)
    piece_2 = advance(big, 2, piece_2)
    pieces = [piece_0, piece_1, piece_2]
    d_query, d_key, d_value = [
        jnp.concatenate([piece[which] for piece in pieces], axis=1) for which in range(3)
    ]
    d_vec = jnp.concatenate([piece[3] for piece in pieces])
    w_parts = [w_qkv[:, at * width : (at + 1) * width] for at in range(3)]
    grad_attn_in = (
        dot_nt(d_query, w_parts[0]) + dot_nt(d_key, w_parts[1]) + dot_nt(d_value, w_parts[2])
    )
    grad_inputs, grad_gain_attn = norm_back(grad_attn_in, inputs, attn_scale, g_attn)

    d_table = jnp.dot(
        d_vec.reshape(2 * head_pairs, -1),
        picker.T,
        precision=lax.Precision.HIGHEST,
        preferred_element_type=f32,
    )
    table_part = d_table.reshape(2, bias_table.size)
    table_high = table_part.astype(bf16)
    table_low = (table_part - table_high.astype(f32)).astype(bf16)
    extra = jnp.concatenate(
        [
            grad_gain_attn.astype(bf16).reshape(devices, own),
            grad_gain_ffn.astype(bf16).reshape(devices, own),
            jnp.tile(table_high, (devices // 2, 1)),
            jnp.tile(table_low, (devices // 2, 1)),
        ],
        axis=1,
    )
    used = extra.shape[1]
    extra = jnp.pad(extra[:, None], ((0, 0), (0, 7), (0, width - used))).reshape(-1, width)
    d_qk, d_vo = weight_grads(
        attn_input, d_query, d_key, d_value, attended, grad_middle_low, extra, ranks
    )
    small = [Scatter(ranks, d_qk, 2), Scatter(ranks, d_vo, 0)]
    begin(small)
    token_low, small[0].arrived = together((grad_inputs + grad_middle).astype(bf16), small[0].arrived)
    grad_tokens = split_sequence(token_low, half)
    advance(small, 0, ())
    advance(small, 1, ())
    advance(small, 2, ())
    own_qk, own_vo = [scatter.take_far() for scatter in small]
    own_w_in, own_w_out = [scatter.take_far() for scatter in big]
    own_w_in = own_w_in.transpose(1, 0, 2)
    rest = own_vo[2 * own]
    table_at = 2 * own
    own_table = rest[table_at : table_at + bias_table.size]
    own_table = own_table + rest[table_at + bias_table.size : used]
    return (
        layer_out,
        grad_tokens,
        own_qk[:own],
        own_qk[own:],
        own_vo[:own],
        own_vo[own : 2 * own],
        own_w_in.reshape(w_in.shape),
        own_w_out.reshape(w_out.shape),
        rest[:own],
        rest[own : 2 * own],
        own_table.reshape(bias_table.shape),
    )


def solution(mesh):
    in_specs = (
        P(None, "rows", "seq", None),
        P(None, "rows", "seq", None),
        P(("rows", "seq"), None),
        P(("rows", "seq"), None),
        P(("rows", "seq"), None),
        P(("rows", "seq"), None),
        P(("rows", "seq"), None),
        P(("rows", "seq"), None),
        P(("rows", "seq")),
        P(("rows", "seq")),
        P("seq", None),
        P(),
    )
    out_specs = (
        P(None, "rows", "seq", None),
        P(None, "rows", "seq", None),
        P(("rows", "seq"), None),
        P(("rows", "seq"), None),
        P(("rows", "seq"), None),
        P(("rows", "seq"), None),
        P(("rows", "seq"), None),
        P(("rows", "seq"), None),
        P(("rows", "seq")),
        P(("rows", "seq")),
        P("seq", None),
    )
    return jax.shard_map(shards, mesh=mesh, in_specs=in_specs, out_specs=out_specs, check_vma=False)
```

time: 413 us -> 309 us (0.75); the launches traced: 413 us -> 304 us
  waiting for transfers between devices: 237 us -> 76.8 us
  starting transfers between devices: 5.37 us -> 55.2 us
  other arithmetic: 14.4 us -> 43.2 us
  blocking collectives: 20.8 us -> 0 us
  Pallas kernels: 74 us -> 87.6 us
  local copies, waits for them, and re-layouts: 26.1 us -> 15.3 us
  matrix products: 20.4 us -> 10.5 us
    unnamed x3 -> x1, waiting for transfers between devices: 136 us -> 0.02 us
    all_gather x1, waiting for transfers between devices: 82.9 us -> 0.01 us  [shards(): w_in_all = lax.all_gather(w_in, ('rows', 'seq'), axis=0, tiled=True)]
    ppermute x0 -> x43, waiting for transfers between devices: none -> 66.1 us  [the longest x42 66.1 us: partner_sends(): lax.ppermute(array, ('rows', 'seq'), [(b, b ^ mask) for b in range(device...]
    ppermute x0 -> x43, starting transfers between devices: none -> 51.3 us  [the longest x42 49.5 us: partner_sends(): lax.ppermute(array, ('rows', 'seq'), [(b, b ^ mask) for b in range(device...]
    all_gather x1 -> x0, blocking collectives: 20.8 us -> none  [shards(): tables = lax.all_gather(bias_table, 'seq', axis=0, tiled=True)]
    convert_element_type x3 -> x16, other arithmetic: 4.37 us -> 22.1 us  [the longest x8 10.7 us: split(): self.outgoing = [self.total(side(1)).astype(jnp.bfloat16)]]
    ppermute x2, waiting for transfers between devices: 17.6 us -> 2.47 us  [split_sequence(): received = lax.ppermute(other, 'seq', [(0, 1), (1, 0)])]
    pallas_call x3 -> x7, Pallas kernels: 74 us -> 87.6 us  [the longest x3 35.4 us: attend_back(): pl.pallas_call(attend_back_kernel, grid=(count,), in_specs=[spec(start),...]
  transfers between devices with their start and end apart: 6 -> 48, of which waited for: 4 -> 21; matrix products, arithmetic and copies ran while one was open for 2% -> 12% of each run, Pallas kernels for 0% -> 18%
where the time goes in v2:
time: 309 us; the launch traced here: 304 us
  Pallas kernels  87.6 us (28%)
  waiting for transfers between devices  76.8 us (25%)
  starting transfers between devices  55.2 us (18%)
  other arithmetic  43.2 us (14%)
  between operations  15.4 us (5%)
  local copies, waits for them, and re-layouts  15.3 us (5%)
  matrix products  10.5 us (3%)
    ppermute x42, waiting for transfers between devices, partner_sends(): lax.ppermute(array, ('rows', 'seq'), [(b, b ^ mask) for b in range(device...  66.1 us
    ppermute x42, starting transfers between devices, partner_sends(): lax.ppermute(array, ('rows', 'seq'), [(b, b ^ mask) for b in range(device...  49.5 us
    pallas_call x3, Pallas kernels, attend_back(): pl.pallas_call(attend_back_kernel, grid=(count,), in_specs=[spec(start),...  35.4 us
    pallas_call x1, Pallas kernels, ffn(): pl.pallas_call(ffn_kernel, grid_spec=pltpu.PrefetchScalarGridSpec(num_sca...  23.3 us
    pallas_call x2, Pallas kernels, attend(): pl.pallas_call(attend_kernel, grid=(count,), in_specs=[spec(start), spec(...  18.9 us
    convert_element_type x8, other arithmetic, split(): self.outgoing = [self.total(side(1)).astype(jnp.bfloat16)]  10.7 us
    pallas_call x1, Pallas kernels, weight_grads(): pl.pallas_call(weight_grads_kernel, grid_spec=pltpu.PrefetchScalarGridSpe...  9.94 us
    ppermute x2, waiting for transfers between devices, swap_halves(): received = lax.ppermute(other, 'seq', [(0, 1), (1, 0)])  8.24 us
  transfers between devices with their start and end apart: 48, of which 21 were waited for; matrix products, arithmetic and copies ran while one was open for 12% of the time, Pallas kernels for 18%

profile of v2, /device:TPU:0, one launch (start us, length us, event | category | flops | bytes accessed | tf_op | source)
XLA Modules:
  0.0 304.1 jit_solution(8915184146812479460)
XLA Ops:
  8.9 5.1 %collective-permute-start.3 = (bf16[24,2432]{1,0:T(8,128)(2,1)S(1)}, bf16[24,2432]{1,0:T(8,128)(2,1)S(1)}, u32[]{:S(2)}, u32[]{:S(2)}) collective-permute-start(bf16[24,2432]{1,0:T(8,128)(2,1)S(1)} %fusion.53), channel_id=1, source_target_pairs={{0,24},{1,25},{2,26},{3,27},{4,28},{5,29},{6,30},{7,31},{8,16},{9,... | collective-permute-start | bytes 350216 | tf_op jit(solution)/shard_map/ppermute | solution.py:367
  19.1 4.8 %collective-permute-done.2 = bf16[24,2432]{1,0:T(8,128)(2,1)S(1)} collective-permute-done((bf16[24,2432]{1,0:T(8,128)(2,1)S(1)}, bf16[24,2432]{1,0:T(8,128)(2,1)S(1)}, u32[]{:S(2)}, u32[]{:S(2)}) %collective-permute-start.2) | collective-permute-done | bytes 116768 | tf_op jit(solution)/shard_map/ppermute | solution.py:367
  29.1 13.4 %collective-permute-done.8 = bf16[120,768]{1,0:T(8,128)(2,1)S(1)} collective-permute-done((bf16[120,768]{1,0:T(8,128)(2,1)S(1)}, bf16[120,768]{1,0:T(8,128)(2,1)S(1)}, u32[]{:S(2)}, u32[]{:S(2)}) %collective-permute-start.8) | collective-permute-done | bytes 184352 | tf_op jit(solution)/shard_map/ppermute | solution.py:367
  44.8 8.5 %collective-permute-done.6 = bf16[2,2,24,1280]{3,2,1,0:T(8,128)(2,1)S(1)} collective-permute-done((bf16[2,2,24,1280]{3,2,1,0:T(8,128)(2,1)S(1)}, bf16[2,2,24,1280]{3,2,1,0:T(8,128)(2,1)S(1)}, u32[]{:S(2)}, u32[]{:S(2)}) %collective-permute-start.6) | collective-permute-done | bytes 245792 | tf_op jit(solution)/shard_map/ppermute | solution.py:367
  55.5 2.5 collective-permute-done.5
  58.0 4.3 %collective-permute-done.7 = bf16[2,2,2,24,1280]{4,3,2,1,0:T(8,128)(2,1)S(1)} collective-permute-done((bf16[2,2,2,24,1280]{4,3,2,1,0:T(8,128)(2,1)S(1)}, bf16[2,2,2,24,1280]{4,3,2,1,0:T(8,128)(2,1)S(1)}, u32[]{:S(2)}, u32[]{:S(2)}) %collective-permute-start.7) | collective-permute-done | bytes 491552 | tf_op jit(solution)/shard_map/ppermute | solution.py:367
  68.9 3.1 %convolution_convert_fusion.q_ref.k_ref.v_ref = bf16[512,2304]{1,0:T(8,128)(2,1)S(1)} fusion(bf16[512,768]{1,0:T(8,128)(2,1)S(1)} %fusion.4.x_ref, bf16[768,1152]{1,0:T(8,128)(2,1)S(1)} %bitcast.298, bf16[768,1280]{1,0:T(8,128)(2,1)S(1)} %bitcast.295), kind=kOutput, calls=%fused_computation.1 | convolution fusion | flops 1820196864 | bytes 6881280 | tf_op jit(solution)/shard_map/dot_general | solution.py:572
  72.0 9.5 %shard_map.203 = bf16[512,384]{1,0:T(8,128)(2,1)S(1)} custom-call(bf16[512,2304]{1,0:T(8,128)(2,1)S(1)} %convolution_convert_fusion.q_ref.k_ref.v_ref, bf16[512,2304]{1,0:T(8,128)(2,1)S(1)} %convolution_convert_fusion.q_ref.k_ref.v_ref, bf16[512,2304]{1,0:T(8,128)(2,1)S(1)} %convolution_convert_fusion.q_ref.k_ref.v_ref, f32[6,2,1024]{2,1,0:T(2,128)S(1)} %reshape.658.vec_ref), custom_call_target="tpu_custom_call" | custom-call | flops 2013265920 | bytes 1572864 | tf_op jit(solution)/shard_map/pallas_call | solution.py:57
  83.7 2.4 collective-permute-start.16
  86.1 9.5 %shard_map.204 = bf16[512,384]{1,0:T(8,128)(2,1)S(1)} custom-call(bf16[512,2304]{1,0:T(8,128)(2,1)S(1)} %convolution_convert_fusion.q_ref.k_ref.v_ref, bf16[512,2304]{1,0:T(8,128)(2,1)S(1)} %convolution_convert_fusion.q_ref.k_ref.v_ref, bf16[512,2304]{1,0:T(8,128)(2,1)S(1)} %convolution_convert_fusion.q_ref.k_ref.v_ref, f32[6,2,1024]{2,1,0:T(2,128)S(1)} %reshape.658.vec_ref), custom_call_target="tpu_custom_call" | custom-call | flops 2013265920 | bytes 1572864 | tf_op jit(solution)/shard_map/pallas_call | solution.py:57
  95.6 4.1 %collective-permute-done.16 = bf16[2,2,2,56,768]{4,3,2,1,0:T(8,128)(2,1)S(1)} collective-permute-done((bf16[2,2,2,56,768]{4,3,2,1,0:T(8,128)(2,1)S(1)}, bf16[2,2,2,56,768]{4,3,2,1,0:T(8,128)(2,1)S(1)}, u32[]{:S(2)}, u32[]{:S(2)}) %collective-permute-start.16) | collective-permute-done | bytes 688160 | tf_op jit(solution)/shard_map/ppermute | solution.py:367
  102.1 2.4 collective-permute-start.19
  105.1 8.2 %collective-permute-done.19 = bf16[256,768]{1,0:T(8,128)(2,1)S(1)} collective-permute-done((bf16[256,768]{1,0:T(8,128)(2,1)S(1)}, bf16[256,768]{1,0:T(8,128)(2,1)S(1)}, u32[]{:S(2)}, u32[]{:S(2)}) %collective-permute-start.19) | collective-permute-done | bytes 393248 | tf_op jit(solution)/shard_map/ppermute | solution.py:344
  120.3 2.6 pad_maximum_fusion
  122.9 23.3 %shard_map.205 = (f32[512,768]{1,0:T(8,128)}, f32[512,768]{1,0:T(8,128)}, bf16[2,2,4,4,24,768]{5,4,3,2,1,0:T(8,128)(2,1)}, bf16[2,2,4,4,24,768]{5,4,3,2,1,0:T(8,...) custom-call(s32[4]{0:T(128)} %pad_add_fusion.seat_ref, ...), custom_call_target="tpu_custom_call" | custom-call | flops 14495514624 | bytes 18874368 | tf_op jit(solution)/shard_map/pallas_call | solution.py:242
  152.0 2.5 collective-permute-done.22
  161.2 11.6 %shard_map.206 = (bf16[512,256]{1,0:T(8,128)(2,1)S(1)}, bf16[512,256]{1,0:T(8,128)(2,1)S(1)}, bf16[512,256]{1,0:T(8,128)(2,1)S(1)}, f32[2,2,1024]{2,1,0:T(2,128)S(1)}) custom-call(bf16[512,2304]{1,0:T(8,128)(2,1)S(1)} %convolution_convert_fusion.q_ref.k_ref.v_ref, bf16[512,2304]{1,0:T(8,128)(2,1)S(1)} %convolution_convert_fusion.q_ref.k_ref.v_ref, ...), custom_call_target="tpu_custom_call" | custom-call | flops 2415919104 | bytes 1048576 | tf_op jit(solution)/shard_map/pallas_call | solution.py:115
  172.9 11.8 %shard_map.207 = (bf16[512,256]{1,0:T(8,128)(2,1)S(1)}, bf16[512,256]{1,0:T(8,128)(2,1)S(1)}, bf16[512,256]{1,0:T(8,128)(2,1)S(1)}, f32[2,2,1024]{2,1,0:T(2,128)S(1)}) custom-call(bf16[512,2304]{1,0:T(8,128)(2,1)S(1)} %convolution_convert_fusion.q_ref.k_ref.v_ref, bf16[512,2304]{1,0:T(8,128)(2,1)S(1)} %convolution_convert_fusion.q_ref.k_ref.v_ref, ...), custom_call_target="tpu_custom_call" | custom-call | flops 2415919104 | bytes 1048576 | tf_op jit(solution)/shard_map/pallas_call | solution.py:115
  184.7 2.6 collective-permute-done.24
  194.3 11.9 %shard_map.208 = (bf16[512,256]{1,0:T(8,128)(2,1)S(1)}, bf16[512,256]{1,0:T(8,128)(2,1)S(1)}, bf16[512,256]{1,0:T(8,128)(2,1)S(1)}, f32[2,2,1024]{2,1,0:T(2,128)S(1)}) custom-call(bf16[512,2304]{1,0:T(8,128)(2,1)S(1)} %convolution_convert_fusion.q_ref.k_ref.v_ref, bf16[512,2304]{1,0:T(8,128)(2,1)S(1)} %convolution_convert_fusion.q_ref.k_ref.v_ref, ...), custom_call_target="tpu_custom_call" | custom-call | flops 2415919104 | bytes 1048576 | tf_op jit(solution)/shard_map/pallas_call | solution.py:115
  207.0 2.5 fusion.35
  217.0 2.4 fusion.11
  220.5 9.9 %shard_map.209 = (bf16[2,2,4,48,768]{4,3,2,1,0:T(8,128)(2,1)}, bf16[2,2,4,48,768]{4,3,2,1,0:T(8,128)(2,1)}, bf16[2,2,4,56,768]{4,3,2,1,0:T(8,128)(2,1)}, bf16[2,2,4,56,768]{4,3,2,1,0:T(8,128)(2,1)}) custom-call(s32[4]{0:T(128)} %pad_add_fusion.seat_ref, bf16[512,768]{1,0:T(8,128)(2,1)} %copy-done.25, bf16[512,768]{1,0:T(8,128)(2,1)} %copy-done.40, ...), custom_call_target="tpu_custom_call" | custom-call | flops 2415919104 | bytes 4718592 | tf_op jit(solution)/shard_map/pallas_call | solution.py:307
  234.5 3.5 %collective-permute-start.42 = (bf16[4,24,768]{2,1,0:T(8,128)(2,1)S(1)}, bf16[4,24,768]{2,1,0:T(8,128)(2,1)S(1)}, u32[]{:S(2)}, u32[]{:S(2)}) collective-permute-start(bf16[4,24,768]{2,1,0:T(8,128)(2,1)S(1)} %copy-done.34), channel_id=1, source_target_pairs={{0,16},{1,17},{2,18},{3,19},{4,20},{5,21},{6,22},{7,23},{8,24},{9,... | collective-permute-start | bytes 442376 | tf_op jit(solution)/shard_map/ppermute | solution.py:367
  248.3 2.9 collective-permute-start.45
  252.8 5.5 %collective-permute-done.31 = bf16[2,4,48,768]{3,2,1,0:T(8,128)(2,1)S(1)} collective-permute-done((bf16[2,4,48,768]{3,2,1,0:T(8,128)(2,1)S(1)}, bf16[2,4,48,768]{3,2,1,0:T(8,128)(2,1)S(1)}, u32[]{:S(2)}, u32[]{:S(2)}) %collective-permute-start.31) | collective-permute-done | bytes 589856 | tf_op jit(solution)/shard_map/ppermute | solution.py:367
  258.8 4.2 %collective-permute-done.32 = bf16[2,4,56,768]{3,2,1,0:T(8,128)(2,1)S(1)} collective-permute-done((bf16[2,4,56,768]{3,2,1,0:T(8,128)(2,1)S(1)}, bf16[2,4,56,768]{3,2,1,0:T(8,128)(2,1)S(1)}, u32[]{:S(2)}, u32[]{:S(2)}) %collective-permute-start.32) | collective-permute-done | bytes 688160 | tf_op jit(solution)/shard_map/ppermute | solution.py:367
  268.9 2.5 collective-permute-done.29
  271.6 4.7 %collective-permute-done.33 = bf16[4,48,768]{2,1,0:T(8,128)(2,1)S(1)} collective-permute-done((bf16[4,48,768]{2,1,0:T(8,128)(2,1)S(1)}, bf16[4,48,768]{2,1,0:T(8,128)(2,1)S(1)}, u32[]{:S(2)}, u32[]{:S(2)}) %collective-permute-start.33) | collective-permute-done | bytes 294944 | tf_op jit(solution)/shard_map/ppermute | solution.py:367
  278.6 3.5 %collective-permute-start.36 = (bf16[48,768]{1,0:T(8,128)(2,1)S(1)}, bf16[48,768]{1,0:T(8,128)(2,1)S(1)}, u32[]{:S(2)}, u32[]{:S(2)}) collective-permute-start(bf16[48,768]{1,0:T(8,128)(2,1)S(1)} %get-tuple-element.204), channel_id=1, source_target_pairs={{0,16},{1,17},{2,18},{3,19},{4,20},{5,21},{6,22},{7,23},{8,24},{9,... | collective-permute-start | bytes 221192 | tf_op jit(solution)/shard_map/ppermute | solution.py:367
  283.9 3.5 %collective-permute-start.39 = (bf16[56,768]{1,0:T(8,128)(2,1)S(1)}, bf16[56,768]{1,0:T(8,128)(2,1)S(1)}, u32[]{:S(2)}, u32[]{:S(2)}) collective-permute-start(bf16[56,768]{1,0:T(8,128)(2,1)S(1)} %get-tuple-element.207), channel_id=1, source_target_pairs={{0,16},{1,17},{2,18},{3,19},{4,20},{5,21},{6,22},{7,23},{8,24},{9,... | collective-permute-start | bytes 258056 | tf_op jit(solution)/shard_map/ppermute | solution.py:367
  290.5 3.5 %collective-permute-done.39 = bf16[56,768]{1,0:T(8,128)(2,1)S(1)} collective-permute-done((bf16[56,768]{1,0:T(8,128)(2,1)S(1)}, bf16[56,768]{1,0:T(8,128)(2,1)S(1)}, u32[]{:S(2)}, u32[]{:S(2)}) %collective-permute-start.39) | collective-permute-done | bytes 86048 | tf_op jit(solution)/shard_map/ppermute | solution.py:367
  (286 shorter events, 96.0 us)
Async XLA Ops:
  7.2 115.7 %all-gather.2.cloned.1.call-start = ((), (), s32[]{:S(2)}) async-start(), calls=%async_computation | async-start | bytes 4866048 | tf_op jit(solution)/shard_map/all_gather | solution.py:516
  8.9 10.2 %collective-permute-start.3 = (bf16[24,2432]{1,0:T(8,128)(2,1)S(1)}, bf16[24,2432]{1,0:T(8,128)(2,1)S(1)}, u32[]{:S(2)}, u32[]{:S(2)}) collective-permute-start(bf16[24,2432]{1,0:T(8,128)(2,1)S(1)} %fusion.53), channel_id=1, source_target_pairs={{0,24},{1,25},{2,26},{3,27},{4,28},{5,29},{6,30},{7,31},{8,16},{9,... | collective-permute-start | bytes 350216 | tf_op jit(solution)/shard_map/ppermute | solution.py:367
  17.4 37.7 %collective-permute-start = (bf16[256,768]{1,0:T(8,128)(2,1)S(1)}, bf16[256,768]{1,0:T(8,128)(2,1)S(1)}, u32[]{:S(2)}, u32[]{:S(2)}) collective-permute-start(bf16[256,768]{1,0:T(8,128)(2,1)S(1)} %dynamic-slice_bitcast_fusion.1), channel_id=1, source_target_pairs={{0,1},{1,0},{2,3},{3,2},{4,5},{5,4},{6,7},{7,6},{8,9},{9,8},{10,11... | collective-permute-start | bytes 1179656 | tf_op jit(solution)/shard_map/ppermute | solution.py:344
  23.8 20.2 %collective-permute-start.9 = (bf16[120,768]{1,0:T(8,128)(2,1)S(1)}, bf16[120,768]{1,0:T(8,128)(2,1)S(1)}, u32[]{:S(2)}, u32[]{:S(2)}) collective-permute-start(bf16[120,768]{1,0:T(8,128)(2,1)S(1)} %pad_maximum_fusion.24), channel_id=1, source_target_pairs={{0,16},{1,17},{2,18},{3,19},{4,20},{5,21},{6,22},{7,23},{8,24},{9,... | collective-permute-start | bytes 552968 | tf_op jit(solution)/shard_map/ppermute | solution.py:367
  24.1 19.9 %collective-permute-start.10 = (bf16[120,768]{1,0:T(8,128)(2,1)S(1)}, bf16[120,768]{1,0:T(8,128)(2,1)S(1)}, u32[]{:S(2)}, u32[]{:S(2)}) collective-permute-start(bf16[120,768]{1,0:T(8,128)(2,1)S(1)} %pad_maximum_fusion.24), channel_id=1, source_target_pairs={{0,24},{1,25},{2,26},{3,27},{4,28},{5,29},{6,30},{7,31},{8,16},{9,... | collective-permute-start | bytes 552968 | tf_op jit(solution)/shard_map/ppermute | solution.py:367
  26.3 16.1 %collective-permute-start.8 = (bf16[120,768]{1,0:T(8,128)(2,1)S(1)}, bf16[120,768]{1,0:T(8,128)(2,1)S(1)}, u32[]{:S(2)}, u32[]{:S(2)}) collective-permute-start(bf16[120,768]{1,0:T(8,128)(2,1)S(1)} %pad_maximum_fusion.24), channel_id=1, source_target_pairs={{0,8},{1,9},{2,10},{3,11},{4,12},{5,13},{6,14},{7,15},{8,0},{9,1},... | collective-permute-start | bytes 552968 | tf_op jit(solution)/shard_map/ppermute | solution.py:367
  27.5 16.5 %collective-permute-start.4 = (bf16[2,2,24,1152]{3,2,1,0:T(8,128)(2,1)S(1)}, bf16[2,2,24,1152]{3,2,1,0:T(8,128)(2,1)S(1)}, u32[]{:S(2)}, u32[]{:S(2)}) collective-permute-start(bf16[2,2,24,1152]{3,2,1,0:T(8,128)(2,1)S(1)} %pad_maximum_fusion.23), channel_id=1, source_target_pairs={{0,4},{1,5},{2,6},{3,7},{4,0},{5,1},{6,2},{7,3},{8,12},{9,13},{10,... | collective-permute-start | bytes 663560 | tf_op jit(solution)/shard_map/ppermute | solution.py:367
  42.5 10.8 %collective-permute-start.6 = (bf16[2,2,24,1280]{3,2,1,0:T(8,128)(2,1)S(1)}, bf16[2,2,24,1280]{3,2,1,0:T(8,128)(2,1)S(1)}, u32[]{:S(2)}, u32[]{:S(2)}) collective-permute-start(bf16[2,2,24,1280]{3,2,1,0:T(8,128)(2,1)S(1)} %pad_maximum_fusion.20), channel_id=1, source_target_pairs={{0,1},{1,0},{2,3},{3,2},{4,5},{5,4},{6,7},{7,6},{8,9},{9,8},{10,11... | collective-permute-start | bytes 737288 | tf_op jit(solution)/shard_map/ppermute | solution.py:367
  44.2 13.8 %collective-permute-start.5 = (bf16[2,2,2,24,1152]{4,3,1,0,2:T(8,128)(2,1)S(1)}, bf16[2,2,2,24,1152]{4,3,1,0,2:T(8,128)(2,1)S(1)}, u32[]{:S(2)}, u32[]{:S(2)}) collective-permute-start(bf16[2,2,2,24,1152]{4,3,1,0,2:T(8,128)(2,1)S(1)} %pad_maximum_fusion.17), channel_id=1, source_target_pairs={{0,1},{1,0},{2,3},{3,2},{4,5},{5,4},{6,7},{7,6},{8,9},{9,8},{10,11... | collective-permute-start | bytes 1327112 | tf_op jit(solution)/shard_map/ppermute | solution.py:367
  63.4 18.1 %collective-permute-start.11 = (bf16[2,2,56,768]{3,2,1,0:T(8,128)(2,1)S(1)}, bf16[2,2,56,768]{3,2,1,0:T(8,128)(2,1)S(1)}, u32[]{:S(2)}, u32[]{:S(2)}) collective-permute-start(bf16[2,2,56,768]{3,2,1,0:T(8,128)(2,1)S(1)} %slice.480), channel_id=1, source_target_pairs={{0,4},{1,5},{2,6},{3,7},{4,0},{5,1},{6,2},{7,3},{8,12},{9,13},{10,... | collective-permute-start | bytes 1032200 | tf_op jit(solution)/shard_map/ppermute | solution.py:367
  65.0 18.4 %collective-permute-start.12 = (bf16[2,2,64,768]{3,2,1,0:T(8,128)(2,1)S(1)}, bf16[2,2,64,768]{3,2,1,0:T(8,128)(2,1)S(1)}, u32[]{:S(2)}, u32[]{:S(2)}) collective-permute-start(bf16[2,2,64,768]{3,2,1,0:T(8,128)(2,1)S(1)} %slice.481), channel_id=1, source_target_pairs={{0,1},{1,0},{2,3},{3,2},{4,5},{5,4},{6,7},{7,6},{8,9},{9,8},{10,11... | collective-permute-start | bytes 1179656 | tf_op jit(solution)/shard_map/ppermute | solution.py:367
  83.6 17.2 %collective-permute-start.17 = (bf16[2,2,2,64,768]{4,3,1,0,2:T(8,128)(2,1)S(1)}, bf16[2,2,2,64,768]{4,3,1,0,2:T(8,128)(2,1)S(1)}, u32[]{:S(2)}, u32[]{:S(2)}) collective-permute-start(bf16[2,2,2,64,768]{4,3,1,0,2:T(8,128)(2,1)S(1)} %pad_maximum_fusion.12), channel_id=1, source_target_pairs={{0,4},{1,5},{2,6},{3,7},{4,0},{5,1},{6,2},{7,3},{8,12},{9,13},{10,... | collective-permute-start | bytes 2359304 | tf_op jit(solution)/shard_map/ppermute | solution.py:367
  83.7 16.0 %collective-permute-start.16 = (bf16[2,2,2,56,768]{4,3,2,1,0:T(8,128)(2,1)S(1)}, bf16[2,2,2,56,768]{4,3,2,1,0:T(8,128)(2,1)S(1)}, u32[]{:S(2)}, u32[]{:S(2)}) collective-permute-start(bf16[2,2,2,56,768]{4,3,2,1,0:T(8,128)(2,1)S(1)} %pad_maximum_fusion.15), channel_id=1, source_target_pairs={{0,1},{1,0},{2,3},{3,2},{4,5},{5,4},{6,7},{7,6},{8,9},{9,8},{10,11... | collective-permute-start | bytes 2064392 | tf_op jit(solution)/shard_map/ppermute | solution.py:367
  101.0 13.7 %collective-permute-start.18 = (bf16[2,2,2,2,56,768]{5,4,3,2,1,0:T(8,128)(2,1)S(1)}, bf16[2,2,2,2,56,768]{5,4,3,2,1,0:T(8,128)(2,1)S(1)}, u32[]{:S(2)}, u32[]{:S(2)}) collective-permute-start(bf16[2,2,2,2,56,768]{5,4,3,2,1,0:T(8,128)(2,1)S(1)} %pad_maximum_fusion.6), channel_id=1, source_target_pairs={{0,2},{1,3},{2,0},{3,1},{4,6},{5,7},{6,4},{7,5},{8,10},{9,11},{10,... | collective-permute-start | bytes 4128776 | tf_op jit(solution)/shard_map/ppermute | solution.py:367
  102.1 11.3 %collective-permute-start.19 = (bf16[256,768]{1,0:T(8,128)(2,1)S(1)}, bf16[256,768]{1,0:T(8,128)(2,1)S(1)}, u32[]{:S(2)}, u32[]{:S(2)}) collective-permute-start(bf16[256,768]{1,0:T(8,128)(2,1)S(1)} %dynamic-slice_bitcast_fusion), channel_id=1, source_target_pairs={{0,1},{1,0},{2,3},{3,2},{4,5},{5,4},{6,7},{7,6},{8,9},{9,8},{10,11... | collective-permute-start | bytes 1179656 | tf_op jit(solution)/shard_map/ppermute | solution.py:344
  158.8 28.6 %collective-permute-start.24 = (bf16[2,4,4,24,768]{4,3,2,1,0:T(8,128)(2,1)}, bf16[2,4,4,24,768]{4,3,2,1,0:T(8,128)(2,1)}, u32[]{:S(2)}, u32[]{:S(2)}) collective-permute-start(bf16[2,4,4,24,768]{4,3,2,1,0:T(8,128)(2,1)} %fusion.12), channel_id=1, source_target_pairs={{0,4},{1,5},{2,6},{3,7},{4,0},{5,1},{6,2},{7,3},{8,12},{9,13},{10,... | collective-permute-start | bytes 3538952 | tf_op jit(solution)/shard_map/ppermute | solution.py:367
  159.5 28.3 %collective-permute-start.25 = (bf16[2,4,96,768]{3,2,1,0:T(8,128)(2,1)}, bf16[2,4,96,768]{3,2,1,0:T(8,128)(2,1)}, u32[]{:S(2)}, u32[]{:S(2)}) collective-permute-start(bf16[2,4,96,768]{3,2,1,0:T(8,128)(2,1)} %fusion.13), channel_id=1, source_target_pairs={{0,1},{1,0},{2,3},{3,2},{4,5},{5,4},{6,7},{7,6},{8,9},{9,8},{10,11... | collective-permute-start | bytes 3538952 | tf_op jit(solution)/shard_map/ppermute | solution.py:367
  191.1 15.2 %collective-permute-start.26 = (bf16[4,4,24,768]{3,2,1,0:T(8,128)(2,1)S(1)}, bf16[4,4,24,768]{3,2,1,0:T(8,128)(2,1)S(1)}, u32[]{:S(2)}, u32[]{:S(2)}) collective-permute-start(bf16[4,4,24,768]{3,2,1,0:T(8,128)(2,1)S(1)} %fusion.20), channel_id=1, source_target_pairs={{0,1},{1,0},{2,3},{3,2},{4,5},{5,4},{6,7},{7,6},{8,9},{9,8},{10,11... | collective-permute-start | bytes 1769480 | tf_op jit(solution)/shard_map/ppermute | solution.py:367
  192.7 14.2 %collective-permute-start.27 = (bf16[4,96,768]{2,1,0:T(8,128)(2,1)S(1)}, bf16[4,96,768]{2,1,0:T(8,128)(2,1)S(1)}, u32[]{:S(2)}, u32[]{:S(2)}) collective-permute-start(bf16[4,96,768]{2,1,0:T(8,128)(2,1)S(1)} %fusion.19), channel_id=1, source_target_pairs={{0,4},{1,5},{2,6},{3,7},{4,0},{5,1},{6,2},{7,3},{8,12},{9,13},{10,... | collective-permute-start | bytes 1769480 | tf_op jit(solution)/shard_map/ppermute | solution.py:367
  230.4 10.2 %collective-permute-start.30 = (bf16[2,2,4,56,768]{4,3,2,1,0:T(8,128)(2,1)}, bf16[2,2,4,56,768]{4,3,2,1,0:T(8,128)(2,1)}, u32[]{:S(2)}, u32[]{:S(2)}) collective-permute-start(bf16[2,2,4,56,768]{4,3,2,1,0:T(8,128)(2,1)} %get-tuple-element.191), channel_id=1, source_target_pairs={{0,2},{1,3},{2,0},{3,1},{4,6},{5,7},{6,4},{7,5},{8,10},{9,11},{10,... | collective-permute-start | bytes 4128776 | tf_op jit(solution)/shard_map/ppermute | solution.py:367
  231.9 12.7 %collective-permute-start.23 = (bf16[256,768]{1,0:T(8,128)(2,1)S(1)}, bf16[256,768]{1,0:T(8,128)(2,1)S(1)}, u32[]{:S(2)}, u32[]{:S(2)}) collective-permute-start(bf16[256,768]{1,0:T(8,128)(2,1)S(1)} %constant_dynamic-slice_fusion.1), channel_id=1, source_target_pairs={{0,1},{1,0},{2,3},{3,2},{4,5},{5,4},{6,7},{7,6},{8,9},{9,8},{10,11... | collective-permute-start | bytes 1179656 | tf_op jit(solution)/shard_map/ppermute | solution.py:360
  232.5 14.5 %collective-permute-start.41 = (bf16[4,24,768]{2,1,0:T(8,128)(2,1)}, bf16[4,24,768]{2,1,0:T(8,128)(2,1)S(1)}, u32[]{:S(2)}, u32[]{:S(2)}) collective-permute-start(bf16[4,24,768]{2,1,0:T(8,128)(2,1)} %get-tuple-element.209), channel_id=1, source_target_pairs={{0,8},{1,9},{2,10},{3,11},{4,12},{5,13},{6,14},{7,15},{8,0},{9,1},... | collective-permute-start | bytes 442376 | tf_op jit(solution)/shard_map/ppermute | solution.py:367
  234.5 13.8 %collective-permute-start.42 = (bf16[4,24,768]{2,1,0:T(8,128)(2,1)S(1)}, bf16[4,24,768]{2,1,0:T(8,128)(2,1)S(1)}, u32[]{:S(2)}, u32[]{:S(2)}) collective-permute-start(bf16[4,24,768]{2,1,0:T(8,128)(2,1)S(1)} %copy-done.34), channel_id=1, source_target_pairs={{0,16},{1,17},{2,18},{3,19},{4,20},{5,21},{6,22},{7,23},{8,24},{9,... | collective-permute-start | bytes 442376 | tf_op jit(solution)/shard_map/ppermute | solution.py:367
  240.1 11.2 %collective-permute-start.43 = (bf16[4,24,768]{2,1,0:T(8,128)(2,1)S(1)}, bf16[4,24,768]{2,1,0:T(8,128)(2,1)S(1)}, u32[]{:S(2)}, u32[]{:S(2)}) collective-permute-start(bf16[4,24,768]{2,1,0:T(8,128)(2,1)S(1)} %copy-done.33), channel_id=1, source_target_pairs={{0,24},{1,25},{2,26},{3,27},{4,28},{5,29},{6,30},{7,31},{8,16},{9,... | collective-permute-start | bytes 442376 | tf_op jit(solution)/shard_map/ppermute | solution.py:367
  243.1 15.2 %collective-permute-start.31 = (bf16[2,4,48,768]{3,2,1,0:T(8,128)(2,1)S(1)}, bf16[2,4,48,768]{3,2,1,0:T(8,128)(2,1)S(1)}, u32[]{:S(2)}, u32[]{:S(2)}) collective-permute-start(bf16[2,4,48,768]{3,2,1,0:T(8,128)(2,1)S(1)} %fusion.23), channel_id=1, source_target_pairs={{0,4},{1,5},{2,6},{3,7},{4,0},{5,1},{6,2},{7,3},{8,12},{9,13},{10,... | collective-permute-start | bytes 1769480 | tf_op jit(solution)/shard_map/ppermute | solution.py:367
  244.6 18.4 %collective-permute-start.32 = (bf16[2,4,56,768]{3,2,1,0:T(8,128)(2,1)S(1)}, bf16[2,4,56,768]{3,2,1,0:T(8,128)(2,1)S(1)}, u32[]{:S(2)}, u32[]{:S(2)}) collective-permute-start(bf16[2,4,56,768]{3,2,1,0:T(8,128)(2,1)S(1)} %fusion.21), channel_id=1, source_target_pairs={{0,1},{1,0},{2,3},{3,2},{4,5},{5,4},{6,7},{7,6},{8,9},{9,8},{10,11... | collective-permute-start | bytes 2064392 | tf_op jit(solution)/shard_map/ppermute | solution.py:367
  247.0 19.2 %collective-permute-start.44 = (bf16[96,768]{1,0:T(8,128)(2,1)S(1)}, bf16[96,768]{1,0:T(8,128)(2,1)S(1)}, u32[]{:S(2)}, u32[]{:S(2)}) collective-permute-start(bf16[96,768]{1,0:T(8,128)(2,1)S(1)} %copy-done.32), channel_id=1, source_target_pairs={{0,8},{1,9},{2,10},{3,11},{4,12},{5,13},{6,14},{7,15},{8,0},{9,1},... | collective-permute-start | bytes 442376 | tf_op jit(solution)/shard_map/ppermute | solution.py:367
  248.3 17.9 %collective-permute-start.45 = (bf16[96,768]{1,0:T(8,128)(2,1)S(1)}, bf16[96,768]{1,0:T(8,128)(2,1)S(1)}, u32[]{:S(2)}, u32[]{:S(2)}) collective-permute-start(bf16[96,768]{1,0:T(8,128)(2,1)S(1)} %get-tuple-element.213), channel_id=1, source_target_pairs={{0,16},{1,17},{2,18},{3,19},{4,20},{5,21},{6,22},{7,23},{8,24},{9,... | collective-permute-start | bytes 442376 | tf_op jit(solution)/shard_map/ppermute | solution.py:367
  251.3 15.0 %collective-permute-start.46 = (bf16[96,768]{1,0:T(8,128)(2,1)S(1)}, bf16[96,768]{1,0:T(8,128)(2,1)S(1)}, u32[]{:S(2)}, u32[]{:S(2)}) collective-permute-start(bf16[96,768]{1,0:T(8,128)(2,1)S(1)} %get-tuple-element.214), channel_id=1, source_target_pairs={{0,24},{1,25},{2,26},{3,27},{4,28},{5,29},{6,30},{7,31},{8,16},{9,... | collective-permute-start | bytes 442376 | tf_op jit(solution)/shard_map/ppermute | solution.py:367
  258.3 13.1 %collective-permute-start.29 = (bf16[256,768]{1,0:T(8,128)(2,1)S(1)}, bf16[256,768]{1,0:T(8,128)(2,1)S(1)}, u32[]{:S(2)}, u32[]{:S(2)}) collective-permute-start(bf16[256,768]{1,0:T(8,128)(2,1)S(1)} %constant_dynamic-slice_fusion), channel_id=1, source_target_pairs={{0,1},{1,0},{2,3},{3,2},{4,5},{5,4},{6,7},{7,6},{8,9},{9,8},{10,11... | collective-permute-start | bytes 1179656 | tf_op jit(solution)/shard_map/ppermute | solution.py:360
  265.2 11.1 %collective-permute-start.33 = (bf16[4,48,768]{2,1,0:T(8,128)(2,1)S(1)}, bf16[4,48,768]{2,1,0:T(8,128)(2,1)S(1)}, u32[]{:S(2)}, u32[]{:S(2)}) collective-permute-start(bf16[4,48,768]{2,1,0:T(8,128)(2,1)S(1)} %fusion.24), channel_id=1, source_target_pairs={{0,1},{1,0},{2,3},{3,2},{4,5},{5,4},{6,7},{7,6},{8,9},{9,8},{10,11... | collective-permute-start | bytes 884744 | tf_op jit(solution)/shard_map/ppermute | solution.py:367
  283.9 10.1 %collective-permute-start.39 = (bf16[56,768]{1,0:T(8,128)(2,1)S(1)}, bf16[56,768]{1,0:T(8,128)(2,1)S(1)}, u32[]{:S(2)}, u32[]{:S(2)}) collective-permute-start(bf16[56,768]{1,0:T(8,128)(2,1)S(1)} %get-tuple-element.207), channel_id=1, source_target_pairs={{0,16},{1,17},{2,18},{3,19},{4,20},{5,21},{6,22},{7,23},{8,24},{9,... | collective-permute-start | bytes 258056 | tf_op jit(solution)/shard_map/ppermute | solution.py:367
  (62 other events, 515.0 us)
Sparse Core Ops, SparseCore 0:
  14.8 79.1 all-gather.1

commit v3 on v1

v3 whole, which is shorter than its diff:
```python
import jax
import jax.numpy as jnp
from jax import lax
from jax.experimental import pallas as pl
from jax.experimental.pallas import tpu as pltpu
from jax.sharding import PartitionSpec as P

HD = 64
RB = 128
epsilon = 1e-06


SMALL_COST = pl.CostEstimate(flops=1 << 20, bytes_accessed=1 << 10, transcendentals=0)


def dot_nt(a, b):
    return lax.dot_general(a, b, (((1,), (1,)), ((), ())), preferred_element_type=jnp.float32)


def dot_nn(a, b):
    return lax.dot_general(a, b, (((1,), (0,)), ((), ())), preferred_element_type=jnp.float32)


def dot_tn(a, b):
    return lax.dot_general(a, b, (((0,), (0,)), ((), ())), preferred_element_type=jnp.float32)


def diag_sums(slab):
    rows = slab.shape[0]
    while rows > 1:
        rows //= 2
        slab = pltpu.roll(slab[:rows], rows, 1) + slab[rows:]
    return slab
def bias_columns(vec):
    wide = jnp.broadcast_to(vec, (RB, vec.shape[1]))
    return pltpu.roll(wide, vec.shape[1] - RB + 1, 1, stride=1, stride_axis=0).T

def attend_kernel(q_ref, k_ref, v_ref, vec_ref, o_ref, lse_ref, slab_ref, out_ref):
    length = q_ref.shape[0]
    for head in range(2):
        cols = slice(head * HD, (head + 1) * HD)
        k = k_ref[:, cols]
        vt = v_ref[:, cols].T
        slab_ref[...] = bias_columns(vec_ref[0, head:head+1, :])
        for first in range(0, length, RB):
            at = length - RB - first
            s = dot_nt(k, q_ref[first:first+RB, cols]) + slab_ref[at:at+length, :]
            peak = jnp.max(s, axis=0, keepdims=True)
            e = jnp.exp(s - peak)
            total = jnp.sum(e, axis=0, keepdims=True)
            lse_ref[0, head:head+1, first:first+RB] = peak + jnp.log(total)
            p = e * (1.0 / total)
            out_ref[head*HD:(head+1)*HD, first:first+RB] = dot_nn(vt, p.astype(jnp.bfloat16))
    o_ref[...] = out_ref[...].T.astype(jnp.bfloat16)

def attend(qk, v, vec):
    length, width = v.shape[0], qk.shape[1] // 2
    steps = width // (2 * HD)
    spec = lambda at: pl.BlockSpec((length, 2 * HD), lambda h: (0, at + h))
    row = lambda columns: pl.BlockSpec((1, 2, columns), lambda h: (h, 0, 0))
    return pl.pallas_call(
        attend_kernel,
        grid=(steps,),
        in_specs=[spec(0), spec(steps), spec(0), row(vec.shape[2])],
        out_specs=[spec(0), row(length)],
        out_shape=[
            jax.ShapeDtypeStruct((length, width), jnp.bfloat16),
            jax.ShapeDtypeStruct((steps, 2, length), jnp.float32),
        ],
        scratch_shapes=[
            pltpu.VMEM((vec.shape[2], RB), jnp.float32),
            pltpu.VMEM((2 * HD, length), jnp.float32),
        ],
        cost_estimate=SMALL_COST,
        compiler_params=pltpu.CompilerParams(vmem_limit_bytes=48 << 20),
    )(qk, qk, v, vec)


def attend_back_kernel(q_ref, k_ref, v_ref, go_ref, lse_ref, vec_ref, dq_ref, dk_ref, dv_ref, dvec_ref, slab_ref, dslab_ref, dqt_ref):
    length = q_ref.shape[0]
    for head in range(2):
        cols = slice(head * HD, (head + 1) * HD)
        k = k_ref[:, cols]
        v = v_ref[:, cols]
        kt = k.T
        slab_ref[...] = bias_columns(vec_ref[0, head:head+1, :])
        lse = lse_ref[0, head:head+1, :]
        dslab_ref[...] = jnp.zeros(dslab_ref.shape, jnp.float32)
        dk = jnp.zeros((length, HD), jnp.float32)
        dv = jnp.zeros((length, HD), jnp.float32)
        for first in range(0, length, RB):
            at = length - RB - first
            rows = slice(first, first + RB)
            q = q_ref[rows, cols]
            go = go_ref[rows, cols]
            p = jnp.exp(dot_nt(k, q) + slab_ref[at:at+length, :] - lse[:, rows])
            gp = dot_nt(v, go)
            ds = (p * (gp - jnp.sum(p * gp, axis=0, keepdims=True))).astype(jnp.bfloat16)
            dslab_ref[at:at+length, :] += ds.astype(jnp.float32)
            dqt_ref[head*HD:(head+1)*HD, rows] = dot_nn(kt, ds)
            dk += dot_nn(ds, q)
            dv += dot_nn(p.astype(jnp.bfloat16), go)
        dk_ref[:, cols] = dk.astype(jnp.bfloat16)
        dv_ref[:, cols] = dv.astype(jnp.bfloat16)
        dvec_ref[0, head:head+1, :] = diag_sums(dslab_ref[...].T)
    dq_ref[...] = dqt_ref[...].T.astype(jnp.bfloat16)

def attend_back(qk, v, go, lse, vec, start, count):
    length, width = go.shape
    steps = width // (2 * HD)
    spec = lambda at: pl.BlockSpec((length, 2 * HD), lambda h: (0, at + h))
    row = lambda at, columns: pl.BlockSpec((1, 2, columns), lambda h: (at + h, 0, 0))
    span = vec.shape[2]
    o = jax.ShapeDtypeStruct((length, count * 2 * HD), jnp.bfloat16)
    return pl.pallas_call(
        attend_back_kernel,
        grid=(count,),
        in_specs=[
            spec(start),
            spec(steps + start),
            spec(start),
            spec(start),
            row(start, length),
            row(start, span),
        ],
        out_specs=[spec(0), spec(0), spec(0), row(0, span)],
        out_shape=[o, o, o, jax.ShapeDtypeStruct((count, 2, span), jnp.float32)],
        scratch_shapes=[
            pltpu.VMEM((span, RB), jnp.float32),
            pltpu.VMEM((span, RB), jnp.float32),
            pltpu.VMEM((2 * HD, length), jnp.float32),
        ],
        cost_estimate=SMALL_COST,
        compiler_params=pltpu.CompilerParams(vmem_limit_bytes=48 << 20),
    )(qk, qk, v, go, lse, vec)


def ffn_step(x_ref, top_ref, win_ref, wout, middle_ref, gain_ref, wo_ref, outs, scratch):
    layer_ref, grad_ref, grad_low_ref, grad_attended_ref = outs
    out_ref, gx_ref, xt_ref = scratch
    x = x_ref[...]
    top = top_ref[...]
    pre = dot_nn(x, win_ref[...])
    sig = 1.0 / (1.0 + jnp.exp(-pre))
    hid = (pre * sig).astype(jnp.bfloat16)
    gact = dot_nt(top, wout)
    gpre = (gact * (sig * (1.0 + pre * (1.0 - sig)))).astype(jnp.bfloat16)

    @pl.when(pl.program_id(0) == 0)
    def _():
        xt_ref[...] = x.T
        out_ref[...] = middle_ref[...]
        gx_ref[...] = jnp.zeros(gx_ref.shape, jnp.float32)

    out_ref[...] += dot_nn(hid, wout)
    gx_ref[...] += dot_nt(gpre, win_ref[...])

    @pl.when(pl.program_id(0) == pl.num_programs(0) - 1)
    def _():
        layer_ref[...] = out_ref[...].astype(jnp.bfloat16)
        middle = middle_ref[...]
        grad = norm_back(gx_ref[...], middle, rms_scale(middle), gain_ref[...])
        grad = grad + top.astype(jnp.float32)
        low = grad.astype(jnp.bfloat16)
        grad_ref[...] = grad
        grad_low_ref[...] = low
        grad_attended_ref[...] = dot_nt(low, wo_ref[...]).astype(jnp.bfloat16)

    return dot_nn(xt_ref[...], gpre).astype(jnp.bfloat16), dot_tn(hid, top).astype(jnp.bfloat16)


def turn_kernel(a_ref, b_ref, a_out_ref, b_out_ref):
    a_out_ref[...] = a_ref[...].T
    b_out_ref[...] = b_ref[...].T


def turn(a, b):
    shape = jax.ShapeDtypeStruct(a.shape[::-1], a.dtype)
    return pl.pallas_call(turn_kernel, out_shape=[shape, shape])(a, b)


def store_blocks(seat_ref, value, rows, blocks, keep_ref, send_ref, put):
    ranks_far = max(blocks // 8, 1)
    for core in range(2):

        @pl.when(seat_ref[0] == core)
        def _():
            for block in range(blocks):
                ref = keep_ref if (block >> 1 & 1) == core else send_ref
                x = (block >> 2 & 1) ^ seat_ref[1]
                y = (block & 1) ^ seat_ref[2]
                put(ref, x, y, turn_bits(block >> 3, ranks_far), value[block * rows : (block + 1) * rows])


def ffn_kernel(
    seat_ref, x_ref, top_ref, win_ref, wout_ref, middle_ref, gain_ref, wo_ref, *outs
):
    in_keep_ref, in_send_ref, out_keep_ref, out_send_ref = outs[4:8]
    own = wout_ref.shape[0] // 8
    tall = out_keep_ref.shape[3]
    width = x_ref.shape[1]
    wout = jnp.concatenate(
        [
            wout_ref[block * own : (block + 1) * own, at * width : (at + 1) * width]
            for block in range(8)
            for at in range(tall // own)
        ]
    )
    d_in, d_out = ffn_step(
        x_ref, top_ref, win_ref, wout, middle_ref, gain_ref, wo_ref, outs[:4], outs[8:]
    )

    def put_in(ref, x, y, far, block):
        ref[x, y, far ^ seat_ref[3]] = block

    def put_out(ref, x, y, far, block):
        ref[x, y, 0] = block

    store_blocks(seat_ref, d_in, own, d_in.shape[0] // own, in_keep_ref, in_send_ref, put_in)
    store_blocks(seat_ref, d_out, tall, 8, out_keep_ref, out_send_ref, put_out)


def ffn_plain_kernel(
    x_ref, top_ref, win_ref, wout_ref, middle_ref, gain_ref, wo_ref, *outs
):
    outs[4][...], outs[5][...] = ffn_step(
        x_ref, top_ref, win_ref, wout_ref[...], middle_ref, gain_ref, wo_ref, outs[:4], outs[6:]
    )


def ffn(x, top, gathered, middle, gain, w_o, ranks):
    length, width = x.shape
    hidden = gathered.shape[1] // 2
    chunks = hidden // width
    own = width // ranks.devices
    far = ranks.devices // 8
    tall = own * chunks
    low = jax.ShapeDtypeStruct((length, width), jnp.bfloat16)
    firsts = [low, jax.ShapeDtypeStruct((length, width), jnp.float32), low, low]
    keep = dict(
        cost_estimate=SMALL_COST,
        compiler_params=pltpu.CompilerParams(vmem_limit_bytes=60 << 20),
    )
    scratch = [
        pltpu.VMEM((length, width), jnp.float32),
        pltpu.VMEM((length, width), jnp.float32),
        pltpu.VMEM((width, length), jnp.bfloat16),
    ]
    fixed = lambda shape: pl.BlockSpec(shape, lambda j, *seat: (0, 0))
    full, square = fixed((length, width)), fixed((width, width))
    column = pl.BlockSpec((width, width), lambda j, *seat: (0, j))
    ends = [full, fixed((1, width)), square]
    if own % 8 or far != chunks:
        row = pl.BlockSpec((width, width), lambda j: (j, 0))
        w_out = gathered[:, hidden:].reshape(ranks.devices, own, chunks, width)
        w_out = w_out.transpose(0, 2, 1, 3).reshape(hidden, width)
        outs = pl.pallas_call(
            ffn_plain_kernel,
            grid=(chunks,),
            in_specs=[full, full, column, row] + ends,
            out_specs=[full] * 4 + [column, row],
            out_shape=firsts
            + [
                jax.ShapeDtypeStruct((width, hidden), jnp.bfloat16),
                jax.ShapeDtypeStruct((hidden, width), jnp.bfloat16),
            ],
            scratch_shapes=scratch,
            **keep,
        )(x, top, gathered, w_out, middle, gain, w_o)
        d_in = outs[4].reshape(ranks.devices, own, chunks, width).transpose(0, 2, 1, 3)
        d_in = d_in.reshape(ranks.devices, tall, width)
        d_out = outs[5].reshape(ranks.devices, tall, width)
        return outs[:4], [ranks.by_seat(d_in), ranks.by_seat(d_out)]
    rows = pl.BlockSpec((8 * own, hidden), lambda j, seat: (j, 1))
    bits = far.bit_length() - 1
    turned = lambda j: sum((j >> at & 1) << (bits - 1 - at) for at in range(bits))
    in_spec = pl.BlockSpec((2, 2, far, own, width), lambda j, seat: (0, 0, 0, j, 0))
    out_spec = pl.BlockSpec((2, 2, 1, tall, width), lambda j, seat: (0, 0, turned(j) ^ seat[3], 0, 0))
    grad = jax.ShapeDtypeStruct((2, 2, far, tall, width), jnp.bfloat16)
    outs = pl.pallas_call(
        ffn_kernel,
        grid_spec=pltpu.PrefetchScalarGridSpec(
            num_scalar_prefetch=1,
            grid=(chunks,),
            in_specs=[full, full, column, rows] + ends,
            out_specs=[full] * 4 + [in_spec, in_spec, out_spec, out_spec],
            scratch_shapes=scratch,
        ),
        out_shape=firsts + [grad] * 4,
        **keep,
    )(ranks.seat, x, top, gathered, gathered, middle, gain, w_o)
    return outs[:4], [outs[4:6], outs[6:8]]


def weight_grads(ranks, left, rights, left_last, right_last):
    width = left.shape[0]
    own = width // ranks.devices
    far = ranks.devices // 8
    if own % 8:
        block = lambda a, b: dot_nn(a, b).astype(jnp.bfloat16).reshape(ranks.devices, own, width)
        blocks = [block(left, right) for right in rights] + [block(left_last, right_last)]
        pairs = blocks[:2], blocks[2:]
        return [ranks.by_seat(jnp.concatenate(pair, axis=1)) for pair in pairs]
    args = [left, left_last, *rights, right_last]

    def kernel(seat_ref, *refs):
        ins, outs = refs[: len(args)], refs[len(args) :]

        def put(ref, x, y, far_at, block):
            ref[x, y, far_at ^ seat_ref[3]] = block

        for step in range(4):

            @pl.when(pl.program_id(0) == step)
            def _():
                value = dot_nn(ins[step == 3][...], ins[2 + step][...]).astype(jnp.bfloat16)
                lane = 2 * (step // 2)
                store_blocks(
                    seat_ref, value, own, ranks.devices, outs[lane], outs[lane + 1], put
                )

    whole = lambda a: pl.BlockSpec(a.shape, lambda i, seat: (0,) * len(a.shape))
    spec = lambda at: pl.BlockSpec((2, 2, far, own, width), lambda i, seat: (0, 0, 0, at(i), 0))
    early, late = spec(lambda i: jnp.minimum(i, 1)), spec(lambda i: jnp.maximum(i - 2, 0))
    outs = pl.pallas_call(
        kernel,
        grid_spec=pltpu.PrefetchScalarGridSpec(
            num_scalar_prefetch=1,
            grid=(4,),
            in_specs=[whole(a) for a in args],
            out_specs=[early, early, late, late],
        ),
        out_shape=[jax.ShapeDtypeStruct((2, 2, far, 2 * own, width), jnp.bfloat16)] * 4,
        cost_estimate=SMALL_COST,
        compiler_params=pltpu.CompilerParams(vmem_limit_bytes=56 << 20),
    )(ranks.seat, *args)
    return [outs[:2], outs[2:]]


def rms_scale(values):
    return lax.rsqrt(jnp.mean(values * values, axis=-1, keepdims=True) + epsilon)


def norm_back(grad_out, values, inv_rms, gain):
    scaled = grad_out * gain
    inner = jnp.mean(scaled * values, axis=-1, keepdims=True)
    return inv_rms * scaled - values * (inv_rms * inv_rms * inv_rms) * inner


def bucket_picker(buckets, bucket_count):
    padded = jnp.pad(buckets, (0, 1), constant_values=-1)
    rows = jnp.arange(bucket_count, dtype=jnp.int32)[:, None]
    return (padded[None, :] == rows).astype(jnp.float32)


def whole_sequences(arrays, half):
    mine = [lax.dynamic_index_in_dim(a, half, 0, keepdims=False)[0] for a in arrays]
    other = [lax.dynamic_index_in_dim(a, 1 - half, 0, keepdims=False)[0] for a in arrays]
    received = lax.ppermute(jnp.stack(other), "seq", [(0, 1), (1, 0)])
    return [
        jnp.concatenate([jnp.where(half == 0, a, b), jnp.where(half == 0, b, a)])
        for a, b in zip(mine, received)
    ]


def split_sequence(array, half):
    rows = array.shape[0] // 2
    mine = lax.dynamic_slice_in_dim(array, half * rows, rows, 0)
    other = lax.dynamic_slice_in_dim(array, (1 - half) * rows, rows, 0)
    received = lax.ppermute(other, "seq", [(0, 1), (1, 0)])
    first = jnp.where(half == 0, mine, received)
    second = jnp.where(half == 0, received, mine)
    return jnp.stack([first, second])[:, None]


def bf16_parts(values, count):
    parts = []
    for _ in range(count):
        part = lax.reduce_precision(values, 8, 7)
        values = values - part
        parts.append(part.astype(jnp.bfloat16))
    return parts


def partner_sends(array, mask, devices):
    return lax.ppermute(array, ("rows", "seq"), [(b, b ^ mask) for b in range(devices)])


def together(first, second):
    return lax.optimization_barrier((first, second))


def turn_bits(value, size):
    bits = size.bit_length() - 1
    return sum((value >> at & 1) << (bits - 1 - at) for at in range(bits))


class Ranks:
    def __init__(self):
        self.devices = lax.axis_size("rows") * lax.axis_size("seq")
        self.count = self.devices.bit_length() - 1
        rank = lax.axis_index("rows") * lax.axis_size("seq") + lax.axis_index("seq")
        rank = rank.astype(jnp.int32)
        self.bits = [(rank >> b) & 1 for b in range(self.count)]
        self.far_bits = list(range(3, self.count))
        self.far_groups = [self.far_bits[at : at + 2] for at in range(0, len(self.far_bits), 2)]
        turned = [self.bits[bit] << (self.count - 1 - bit) for bit in self.far_bits]
        self.seat = jnp.stack([self.bits[1], self.bits[2], self.bits[0], sum(turned)])

    def by_seat(self, array):
        far = self.devices // 8
        grid = array.reshape((far, 2, 2, 2) + array.shape[1:])
        for axis, bit in ((1, 2), (2, 1), (3, 0)):
            grid = jnp.where(self.bits[bit] == 0, grid, jnp.flip(grid, axis))
        turned = jnp.array([turn_bits(at, far) for at in range(far)], dtype=jnp.int32)
        order = jnp.arange(far, dtype=jnp.int32) ^ self.seat[3]
        grid = jnp.take(grid, jnp.take(turned, order), axis=0)
        grid = jnp.moveaxis(grid, 0, 3)
        return grid[:, 0], grid[:, 1]


def group_masks(group):
    for code in range(1, 1 << len(group)):
        yield sum(1 << bit for at, bit in enumerate(group) if code >> at & 1)


class Gather:
    def __init__(self, ranks, shard, held=()):
        self.ranks, self.value, self.held = ranks, shard, list(held)

    def send(self, group):
        self.group = group
        self.arrived = {
            mask: partner_sends(self.value, mask, self.ranks.devices) for mask in group_masks(group)
        }

    def merge(self):
        by_mask = {0: self.value, **self.arrived}
        for bit in self.group:
            self.held = sorted(self.held + [bit], reverse=True)
            axis = self.held.index(bit)
            flag = self.ranks.bits[bit] == 0
            merged = {}
            for mask in by_mask:
                if mask >> bit & 1:
                    continue
                here, there = by_mask[mask], by_mask[mask | 1 << bit]
                merged[mask] = jnp.stack(
                    [jnp.where(flag, here, there), jnp.where(flag, there, here)], axis=axis
                )
            by_mask = merged
        self.value = by_mask[0]

    def blocks(self):
        return self.value.reshape((-1,) + self.value.shape[-2:])


def summed(terms, pick):
    return sum(pick(term).astype(jnp.float32) for term in terms)


def side(at, axis):
    return lambda term: lax.index_in_dim(term, at, axis, keepdims=False)


def far_half(at):
    return lambda term: jnp.split(term, 2, axis=0)[at]


class Scatter:
    def __init__(self, ranks, halves, steps):
        self.ranks = ranks
        self.terms = [[kept] for kept, _ in halves]
        self.outgoing = [leaving for _, leaving in halves]
        everything = sorted(lane for _, lanes in steps[0] for lane in lanes)
        core = [(1, [lane]) for lane in range(len(halves))]
        self.steps = [core] + steps + [[(bit, everything)] for bit in ranks.far_bits]
        self.step = 0

    def send(self):
        self.arrived = [
            partner_sends(array, 1 << bit, self.ranks.devices)
            for array, (bit, _) in zip(self.outgoing, self.steps[self.step])
        ]
        self.step += 1

    def join(self, kept, leaving):
        self.steps[0].append((1, [len(self.terms)]))
        self.terms.append([kept])
        self.arrived = self.arrived + [partner_sends(leaving, 2, self.ranks.devices)]

    def receive(self):
        for got, (_, lanes) in zip(self.arrived, self.steps[self.step - 1]):
            at = 0
            for lane in lanes:
                rows = self.terms[lane][0].shape[-2]
                self.terms[lane].append(lax.slice_in_dim(got, at, at + rows, axis=got.ndim - 2))
                at += rows

    def prepare(self):
        self.receive()
        self.outgoing = []
        for bit, lanes in self.steps[self.step]:
            axis = 1 if bit == 0 and self.step == 1 else 0
            pick = far_half if bit > 2 else lambda at, axis=axis: side(at, axis)
            sums = [summed(self.terms[lane], pick(1)) for lane in lanes]
            total = jnp.concatenate(sums, axis=-2) if len(sums) > 1 else sums[0]
            self.outgoing.append(total.astype(jnp.bfloat16))
            for lane in lanes:
                self.terms[lane] = [pick(0)(term) for term in self.terms[lane]]

    def advance(self, waited=()):
        self.arrived, waited = together(self.arrived, waited)
        self.prepare()
        self.outgoing, waited = together(self.outgoing, waited)
        self.send()
        return waited

    def done(self):
        return self.step == len(self.steps)

    def finish(self):
        self.receive()
        return [summed(terms, lambda term: term[0]) for terms in self.terms]


def shards(
    tokens,
    cotangent,
    w_query,
    w_key,
    w_value,
    w_output,
    w_in,
    w_out,
    gain_attn,
    gain_ffn,
    bias_table,
    buckets,
):
    ranks = Ranks()
    devices = ranks.devices
    half = lax.axis_index("seq")
    own, width = w_query.shape
    head_pairs = width // (2 * HD)
    bf16, f32 = jnp.bfloat16, jnp.float32

    parts = [part.reshape(own, -1) for part in bf16_parts(bias_table, 3)]
    little = jnp.concatenate([gain_attn[:, None], gain_ffn[:, None]] + parts, axis=1)
    used = little.shape[1]
    little = jnp.pad(little, ((0, 0), (0, -used % 128)))
    packed = jnp.concatenate([w_query, w_key, w_value, w_output, little], axis=1)
    groups = w_out.reshape(-1, own, width).transpose(1, 0, 2).reshape(own, -1)
    gathered = lax.all_gather(
        jnp.concatenate([w_in, groups], axis=1), ("rows", "seq"), axis=0, tiled=True
    )
    first = Gather(ranks, packed)
    for group in ranks.far_groups:
        first.send(group)
        first.merge()
    cut = 2 * width
    pair = [
        Gather(ranks, first.value[..., :cut], first.held),
        Gather(ranks, first.value[..., cut:], first.held),
    ]
    pair[0].send([2])
    pair[1].send([0])
    for part in pair:
        part.merge()
    pair[0].send([0])
    pair[1].send([2])
    for part in pair:
        part.merge()
        part.send([1])
    inputs, top = whole_sequences([tokens, cotangent], half)
    for part in pair:
        part.merge()
    low, high = [part.value.reshape(width, -1) for part in pair]
    w_parts = [low[:, :width], low[:, width:], high[:, :width]]
    w_o = high[:, width : 2 * width]
    g_attn = high[:, 2 * width].astype(f32)
    g_ffn = high[:, 2 * width + 1].astype(f32)
    tables = high[: 2 * own, 2 * width + 2 : 2 * width + used].astype(f32)
    tables = tables.reshape(2, own, 3, -1).sum(axis=2).reshape(2 * head_pairs, -1)
    picker = bucket_picker(buckets, bias_table.shape[1])
    vec = jnp.dot(tables, picker, precision=lax.Precision.HIGHEST, preferred_element_type=f32)
    vec = vec.reshape(head_pairs, 2, -1)

    inputs = inputs.astype(f32)
    attn_scale = rms_scale(inputs)
    attn_input = (inputs * attn_scale * g_attn).astype(bf16)
    qk = jnp.dot(attn_input, low, preferred_element_type=f32).astype(bf16)
    v = jnp.dot(attn_input, w_parts[2], preferred_element_type=f32).astype(bf16)
    attended, lse = attend(qk, v, vec)
    middle = inputs + jnp.dot(attended, w_o, preferred_element_type=f32)
    ffn_scale = rms_scale(middle)
    ffn_input = (middle * ffn_scale * g_ffn).astype(bf16)
    attn_turned, attended_turned = turn(attn_input, attended)
    gathered, (ffn_input, top, attn_turned, attended_turned) = together(
        gathered, (ffn_input, top, attn_turned, attended_turned)
    )
    (layer_low, grad_middle, grad_middle_low, grad_attended), d_ffn = ffn(
        ffn_input, top, gathered, middle, g_ffn[None], w_o, ranks
    )
    big = Scatter(ranks, d_ffn, [[(2, [0]), (0, [1])], [(0, [0]), (2, [1])]])
    big.send()

    layer_out = split_sequence(layer_low, half)
    each = head_pairs // 3
    piece_0 = attend_back(qk, v, grad_attended, lse, vec, 0, each)
    piece_0, grad_attended, layer_out = big.advance((piece_0, grad_attended, layer_out))
    piece_1 = attend_back(qk, v, grad_attended, lse, vec, each, head_pairs - each)
    d_vec = jnp.concatenate([piece_0[3], piece_1[3]])
    grads = [jnp.concatenate([piece_0[at], piece_1[at]], axis=1) for at in range(3)]
    small = Scatter(
        ranks,
        weight_grads(ranks, attn_turned, grads, attended_turned, grad_middle_low),
        [[(2, [0]), (0, [1, 2])], [(0, [0]), (2, [1, 2])]],
    )
    small.outgoing, (grads, d_vec) = together(small.outgoing, (grads, d_vec))
    small.send()
    grads, d_vec = big.advance((grads, d_vec))
    d_table = jnp.dot(
        d_vec.reshape(2 * head_pairs, -1),
        picker.T,
        precision=lax.Precision.HIGHEST,
        preferred_element_type=f32,
    )
    extra = jnp.concatenate(bf16_parts(d_table.reshape(2, bias_table.size), 2), axis=1)
    extra = jnp.pad(extra[:, None], ((0, 0), (0, 7), (0, width - 2 * bias_table.size)))
    small.join(*ranks.by_seat(jnp.tile(extra, (devices // 2, 1, 1))))
    grads = small.advance(grads)
    grad_attn_in = sum(dot_nt(grad, w) for grad, w in zip(grads, w_parts))
    grad_inputs = norm_back(grad_attn_in, inputs, attn_scale, g_attn)
    token_low = (grad_inputs + grad_middle).astype(bf16)
    token_low = big.advance(token_low)
    token_low = small.advance(token_low)
    grad_tokens = split_sequence(token_low, half)
    while not (big.done() and small.done()):
        for scatter in (big, small):
            if not scatter.done():
                scatter.advance()
    own_w_in, own_w_out = big.finish()
    own_qk, own_vo, rest = small.finish()
    own_w_in = own_w_in.reshape(-1, own, width).transpose(1, 0, 2).reshape(w_in.shape)
    d_w = [own_qk[:own], own_qk[own:], own_vo[:own]]
    own_gain_attn = sum(
        jnp.sum(w.astype(f32) * d, axis=1) for w, d in zip((w_query, w_key, w_value), d_w)
    ) / gain_attn.astype(f32)
    own_gain_ffn = jnp.sum(w_in.astype(f32) * own_w_in, axis=1) / gain_ffn.astype(f32)
    own_table = rest[0, : bias_table.size] + rest[0, bias_table.size : 2 * bias_table.size]
    return (
        layer_out,
        grad_tokens,
        d_w[0],
        d_w[1],
        d_w[2],
        own_vo[own:],
        own_w_in,
        own_w_out,
        own_gain_attn,
        own_gain_ffn,
        own_table.reshape(bias_table.shape),
    )


def solution(mesh):
    in_specs = (
        P(None, "rows", "seq", None),
        P(None, "rows", "seq", None),
        P(("rows", "seq"), None),
        P(("rows", "seq"), None),
        P(("rows", "seq"), None),
        P(("rows", "seq"), None),
        P(("rows", "seq"), None),
        P(("rows", "seq"), None),
        P(("rows", "seq")),
        P(("rows", "seq")),
        P("seq", None),
        P(),
    )
    out_specs = (
        P(None, "rows", "seq", None),
        P(None, "rows", "seq", None),
        P(("rows", "seq"), None),
        P(("rows", "seq"), None),
        P(("rows", "seq"), None),
        P(("rows", "seq"), None),
        P(("rows", "seq"), None),
        P(("rows", "seq"), None),
        P(("rows", "seq")),
        P(("rows", "seq")),
        P("seq", None),
    )
    return jax.shard_map(shards, mesh=mesh, in_specs=in_specs, out_specs=out_specs, check_vma=False)
```

time: 413 us -> 269 us (0.65)
  waiting for transfers between devices: 237 us -> 74.5 us
  other arithmetic: 14.4 us -> 44.9 us
  starting transfers between devices: 5.37 us -> 31.1 us
  blocking collectives: 20.8 us -> 0 us
  matrix products: 20.4 us -> 8.88 us
  local copies, waits for them, and re-layouts: 26.1 us -> 16 us
    unnamed x3 -> x1, waiting for transfers between devices: 136 us -> 0.02 us
    all_gather x1, waiting for transfers between devices: 82.9 us -> 1.9 us  [shards(): lax.all_gather(jnp.concatenate([w_in, groups], axis=1), ('rows', 'seq'),...]
    ppermute x2 -> x27, waiting for transfers between devices: 0.01 us -> 68.5 us  [the longest x26 68.5 us: partner_sends(): lax.ppermute(array, ('rows', 'seq'), [(b, b ^ mask) for b in range(device...]
    ppermute x2 -> x27, starting transfers between devices: 3.13 us -> 28.1 us  [the longest x26 26.3 us: partner_sends(): lax.ppermute(array, ('rows', 'seq'), [(b, b ^ mask) for b in range(device...]
    all_gather x1 -> x0, blocking collectives: 20.8 us -> none  [shards(): tables = lax.all_gather(bias_table, 'seq', axis=0, tiled=True)]
    another operation x1 -> x28, other arithmetic: 0.01 us -> 14.3 us  [shards(): jnp.stack([gain_attn, gain_ffn], axis=1)]
    ppermute x2, waiting for transfers between devices: 17.6 us -> 4.04 us  [split_sequence(): received = lax.ppermute(other, 'seq', [(0, 1), (1, 0)])]
    convert_element_type x4 -> x11, other arithmetic: 4.37 us -> 14.1 us  [the longest x6 12.5 us: prepare(): self.outgoing.append(total.astype(jnp.bfloat16))]
  transfers between devices with their start and end apart: 6 -> 30, of which waited for: 4 -> 17; matrix products, arithmetic and copies ran while one was open for 2% -> 19% of each run, Pallas kernels for 0% -> 19%
where the time goes in v3:
time: 269 us; the launch traced here: 268 us
  Pallas kernels  77.4 us (29%)
  waiting for transfers between devices  74.5 us (28%)
  other arithmetic  44.9 us (17%)
  starting transfers between devices  31.1 us (12%)
  local copies, waits for them, and re-layouts  16 us (6%)
  between operations  15.1 us (6%)
  matrix products  8.88 us (3%)
    ppermute x26, waiting for transfers between devices, partner_sends(): lax.ppermute(array, ('rows', 'seq'), [(b, b ^ mask) for b in range(device...  68.5 us
    pallas_call x1, Pallas kernels, ffn(): pl.pallas_call(ffn_kernel, grid_spec=pltpu.PrefetchScalarGridSpec(num_sca...  27 us
    ppermute x26, starting transfers between devices, partner_sends(): lax.ppermute(array, ('rows', 'seq'), [(b, b ^ mask) for b in range(device...  26.3 us
    pallas_call x2, Pallas kernels, attend_back(): pl.pallas_call(attend_back_kernel, grid=(count,), in_specs=[spec(start),...  24.6 us
    pallas_call x1, Pallas kernels, attend(): pl.pallas_call(attend_kernel, grid=(steps,), in_specs=[spec(0), spec(step...  14.4 us
    convert_element_type x6, other arithmetic, prepare(): self.outgoing.append(total.astype(jnp.bfloat16))  12.5 us
    another operation x10, other arithmetic  8.43 us
    pallas_call x1, Pallas kernels, weight_grads(): pl.pallas_call(kernel, grid_spec=pltpu.PrefetchScalarGridSpec(num_scalar_...  8.4 us
  transfers between devices with their start and end apart: 30, of which 17 were waited for; matrix products, arithmetic and copies ran while one was open for 19% of the time, Pallas kernels for 19%

profile of v3, /device:TPU:0, one launch (start us, length us, event | category | flops | bytes accessed | tf_op | source)
XLA Modules:
  0.0 267.9 jit_solution(8224855132372181687)
XLA Ops:
  12.7 3.1 %collective-permute-start.1 = (bf16[24,3200]{1,0:T(8,128)(2,1)S(1)}, bf16[24,3200]{1,0:T(8,128)(2,1)}, u32[]{:S(2)}, u32[]{:S(2)}) collective-permute-start(bf16[24,3200]{1,0:T(8,128)(2,1)S(1)} %constant_dynamic-update-slice_fusion), channel_id=1, source_target_pairs={{0,8},{1,9},{2,10},{3,11},{4,12},{5,13},{6,14},{7,15},{8,0},{9,1},... | collective-permute-start | bytes 460808 | tf_op jit(solution)/shard_map/ppermute | solution.py:386
  15.8 2.6 collective-permute-start.2
  18.6 1.8 collective-permute-start
  20.4 1.7 collective-permute-done.1
  23.0 10.2 %collective-permute-done.2 = bf16[24,3200]{1,0:T(8,128)(2,1)S(1)} collective-permute-done((bf16[24,3200]{1,0:T(8,128)(2,1)S(1)}, bf16[24,3200]{1,0:T(8,128)(2,1)S(1)}, u32[]{:S(2)}, u32[]{:S(2)}) %collective-permute-start.2) | collective-permute-done | bytes 153632 | tf_op jit(solution)/shard_map/ppermute | solution.py:386
  38.1 3.0 %collective-permute-done.7 = bf16[2,2,24,1536]{3,2,1,0:T(8,128)(2,1)S(1)} collective-permute-done((bf16[2,2,24,1536]{3,2,1,0:T(8,128)(2,1)S(1)}, bf16[2,2,24,1536]{3,2,1,0:T(8,128)(2,1)S(1)}, u32[]{:S(2)}, u32[]{:S(2)}) %collective-permute-start.7) | collective-permute-done | bytes 294944 | tf_op jit(solution)/shard_map/ppermute | solution.py:386
  42.9 7.5 %collective-permute-done.4 = bf16[2,2,24,1664]{3,2,1,0:T(8,128)(2,1)S(1)} collective-permute-done((bf16[2,2,24,1664]{3,2,1,0:T(8,128)(2,1)S(1)}, bf16[2,2,24,1664]{3,2,1,0:T(8,128)(2,1)S(1)}, u32[]{:S(2)}, u32[]{:S(2)}) %collective-permute-start.4) | collective-permute-done | bytes 319520 | tf_op jit(solution)/shard_map/ppermute | solution.py:386
  51.8 11.4 %collective-permute-done.8 = bf16[2,2,2,24,1536]{4,3,2,1,0:T(8,128)(2,1)S(1)} collective-permute-done((bf16[2,2,2,24,1536]{4,3,2,1,0:T(8,128)(2,1)S(1)}, bf16[2,2,2,24,1536]{4,3,2,1,0:T(8,128)(2,1)S(1)}, u32[]{:S(2)}, u32[]{:S(2)}) %collective-permute-start.8) | collective-permute-done | bytes 589856 | tf_op jit(solution)/shard_map/ppermute | solution.py:386
  63.5 5.0 %collective-permute-done.5 = bf16[2,2,2,24,1664]{4,3,1,0,2:T(8,128)(2,1)S(1)} collective-permute-done((bf16[2,2,2,24,1664]{4,3,1,0,2:T(8,128)(2,1)S(1)}, bf16[2,2,2,24,1664]{4,3,1,0,2:T(8,128)(2,1)S(1)}, u32[]{:S(2)}, u32[]{:S(2)}) %collective-permute-start.5) | collective-permute-done | bytes 639008 | tf_op jit(solution)/shard_map/ppermute | solution.py:386
  70.3 1.8 pad_maximum_fusion.1
  78.6 14.4 %shard_map.212 = (bf16[512,768]{1,0:T(8,128)(2,1)S(1)}, f32[6,2,512]{2,1,0:T(2,128)S(1)}) custom-call(bf16[512,1536]{1,0:T(8,128)(2,1)S(1)} %convolution_convert_fusion.q_ref.k_ref, bf16[512,1536]{1,0:T(8,128)(2,1)S(1)} %convolution_convert_fusion.q_ref.k_ref, bf16[512,768]{1,0:T(8,128)(2,1)S(1)} %convolution_convert_fusion.1.v_ref, ...), custom_call_target="tpu_custom_call" | custom-call | flops 1048576 | bytes 1024 | tf_op jit(solution)/shard_map/pallas_call | solution.py:61
  94.0 2.9 %shard_map.213 = (bf16[768,512]{1,0:T(8,128)(2,1)}, bf16[768,512]{1,0:T(8,128)(2,1)}) custom-call(bf16[512,768]{1,0:T(8,128)(2,1)} %copy-done.12, bf16[512,768]{1,0:T(8,128)(2,1)} %copy-done.1), custom_call_target="tpu_custom_call" | custom-call | tf_op jit(solution)/shard_map/pallas_call | solution.py:179
  97.5 2.5 multiply_reduce_fusion
  102.2 1.9 all-gather.2.cloned.1.call-done.win_ref.wout_ref
  104.1 27.0 %shard_map.214 = (bf16[512,768]{1,0:T(8,128)(2,1)}, f32[512,768]{1,0:T(8,128)}, bf16[512,768]{1,0:T(8,128)(2,1)}, bf16[512,768]{1,0:T(8,128)(2,1)}, bf16[2,2,4,9...) custom-call(s32[4]{0:T(128)} %pad_add_fusion.seat_ref, ...), custom_call_target="tpu_custom_call" | custom-call | flops 1048576 | bytes 1024 | tf_op jit(solution)/shard_map/pallas_call | solution.py:280
  131.7 1.8 constant_dynamic-slice_fusion.1
  135.6 8.4 %shard_map.215 = (bf16[512,256]{1,0:T(8,128)(2,1)S(1)}, bf16[512,256]{1,0:T(8,128)(2,1)S(1)}, bf16[512,256]{1,0:T(8,128)(2,1)S(1)}, f32[2,2,1024]{2,1,0:T(2,128)S(1)}) custom-call(bf16[512,1536]{1,0:T(8,128)(2,1)S(1)} %convolution_convert_fusion.q_ref.k_ref, bf16[512,1536]{1,0:T(8,128)(2,1)S(1)} %convolution_convert_fusion.q_ref.k_ref, ...), custom_call_target="tpu_custom_call" | custom-call | flops 1048576 | bytes 1024 | tf_op jit(solution)/shard_map/pallas_call | solution.py:115
  147.2 2.8 %fusion.9 = bf16[2,4,96,768]{3,2,1,0:T(8,128)(2,1)} fusion(bf16[2,2,4,96,768]{4,3,2,1,0:T(8,128)(2,1)S(1)} %copy-done.13, bf16[2,2,4,96,768]{4,3,2,1,0:T(8,128)(2,1)} %collective-permute-done.11), kind=kLoop, calls=%fused_computation.28 | loop fusion | flops 2359296 | bytes 3538944 | tf_op jit(solution)/shard_map/convert_element_type | solution.py:508
  149.9 2.6 fusion.8
  154.6 16.3 %shard_map.216 = (bf16[512,512]{1,0:T(8,128)(2,1)S(1)}, bf16[512,512]{1,0:T(8,128)(2,1)S(1)}, bf16[512,512]{1,0:T(8,128)(2,1)S(1)}, f32[4,2,1024]{2,1,0:T(2,128)S(1)}) custom-call(bf16[512,1536]{1,0:T(8,128)(2,1)S(1)} %convolution_convert_fusion.q_ref.k_ref, bf16[512,1536]{1,0:T(8,128)(2,1)S(1)} %convolution_convert_fusion.q_ref.k_ref, ...), custom_call_target="tpu_custom_call" | custom-call | flops 1048576 | bytes 1024 | tf_op jit(solution)/shard_map/pallas_call | solution.py:115
  172.4 8.4 %shard_map.217 = (bf16[2,2,4,48,768]{4,3,2,1,0:T(8,128)(2,1)}, bf16[2,2,4,48,768]{4,3,2,1,0:T(8,128)(2,1)}, bf16[2,2,4,48,768]{4,3,2,1,0:T(8,128)(2,1)}, bf16[2,2,4,48,768]{4,3,2,1,0:T(8,128)(2,1)}) custom-call(s32[4]{0:T(128)} %pad_add_fusion.seat_ref, bf16[768,512]{1,0:T(8,128)(2,1)} %get-tuple-element.124.refs_0_, ...), custom_call_target="tpu_custom_call" | custom-call | flops 1048576 | bytes 1024 | tf_op jit(solution)/shard_map/pallas_call | solution.py:325
  181.4 2.4 fusion.14
  183.8 2.3 fusion.15
  199.2 2.3 fusion.7
  201.9 3.9 %collective-permute-done.20 = bf16[4,96,768]{2,1,0:T(8,128)(2,1)S(1)} collective-permute-done((bf16[4,96,768]{2,1,0:T(8,128)(2,1)S(1)}, bf16[4,96,768]{2,1,0:T(8,128)(2,1)S(1)}, u32[]{:S(2)}, u32[]{:S(2)}) %collective-permute-start.20) | collective-permute-done | bytes 589856 | tf_op jit(solution)/shard_map/ppermute | solution.py:386
  211.3 7.8 %collective-permute-done.18 = bf16[2,4,48,768]{3,2,1,0:T(8,128)(2,1)S(1)} collective-permute-done((bf16[2,4,48,768]{3,2,1,0:T(8,128)(2,1)S(1)}, bf16[2,4,48,768]{3,2,1,0:T(8,128)(2,1)S(1)}, u32[]{:S(2)}, u32[]{:S(2)}) %collective-permute-start.18) | collective-permute-done | bytes 589856 | tf_op jit(solution)/shard_map/ppermute | solution.py:386
  227.6 2.0 collective-permute-start.28
  229.6 4.4 %collective-permute-done.23 = bf16[4,48,768]{2,1,0:T(8,128)(2,1)S(1)} collective-permute-done((bf16[4,48,768]{2,1,0:T(8,128)(2,1)S(1)}, bf16[4,48,768]{2,1,0:T(8,128)(2,1)S(1)}, u32[]{:S(2)}, u32[]{:S(2)}) %collective-permute-start.23) | collective-permute-done | bytes 294944 | tf_op jit(solution)/shard_map/ppermute | solution.py:386
  237.6 3.0 %collective-permute-done.22 = bf16[256,768]{1,0:T(8,128)(2,1)S(1)} collective-permute-done((bf16[256,768]{1,0:T(8,128)(2,1)S(1)}, bf16[256,768]{1,0:T(8,128)(2,1)S(1)}, u32[]{:S(2)}, u32[]{:S(2)}) %collective-permute-start.22) | collective-permute-done | bytes 393248 | tf_op jit(solution)/shard_map/ppermute | solution.py:370
  243.0 1.9 convert_add_fusion.7
  244.9 3.0 %collective-permute-done.25 = bf16[2,104,768]{2,1,0:T(8,128)(2,1)S(1)} collective-permute-done((bf16[2,104,768]{2,1,0:T(8,128)(2,1)S(1)}, bf16[2,104,768]{2,1,0:T(8,128)(2,1)S(1)}, u32[]{:S(2)}, u32[]{:S(2)}) %collective-permute-start.25) | collective-permute-done | bytes 319520 | tf_op jit(solution)/shard_map/ppermute | solution.py:386
  249.5 7.4 %collective-permute-done.26 = bf16[1,104,768]{2,1,0:T(8,128)(2,1)S(1)} collective-permute-done((bf16[1,104,768]{2,1,0:T(8,128)(2,1)S(1)}, bf16[1,104,768]{2,1,0:T(8,128)(2,1)S(1)}, u32[]{:S(2)}, u32[]{:S(2)}) %collective-permute-start.26) | collective-permute-done | bytes 159776 | tf_op jit(solution)/shard_map/ppermute | solution.py:386
  (267 shorter events, 75.5 us)
Async XLA Ops:
  7.2 96.9 %all-gather.2.cloned.1.call-start = ((), (), s32[]{:S(2)}) async-start(), calls=%async_computation | async-start | bytes 9732096 | tf_op jit(solution)/shard_map/all_gather | solution.py:554
  12.7 9.4 %collective-permute-start.1 = (bf16[24,3200]{1,0:T(8,128)(2,1)S(1)}, bf16[24,3200]{1,0:T(8,128)(2,1)}, u32[]{:S(2)}, u32[]{:S(2)}) collective-permute-start(bf16[24,3200]{1,0:T(8,128)(2,1)S(1)} %constant_dynamic-update-slice_fusion), channel_id=1, source_target_pairs={{0,8},{1,9},{2,10},{3,11},{4,12},{5,13},{6,14},{7,15},{8,0},{9,1},... | collective-permute-start | bytes 460808 | tf_op jit(solution)/shard_map/ppermute | solution.py:386
  15.8 17.4 %collective-permute-start.2 = (bf16[24,3200]{1,0:T(8,128)(2,1)S(1)}, bf16[24,3200]{1,0:T(8,128)(2,1)S(1)}, u32[]{:S(2)}, u32[]{:S(2)}) collective-permute-start(bf16[24,3200]{1,0:T(8,128)(2,1)S(1)} %constant_dynamic-update-slice_fusion), channel_id=1, source_target_pairs={{0,16},{1,17},{2,18},{3,19},{4,20},{5,21},{6,22},{7,23},{8,24},{9,... | collective-permute-start | bytes 460808 | tf_op jit(solution)/shard_map/ppermute | solution.py:386
  18.4 14.8 %collective-permute-start.3 = (bf16[24,3200]{1,0:T(8,128)(2,1)S(1)}, bf16[24,3200]{1,0:T(8,128)(2,1)}, u32[]{:S(2)}, u32[]{:S(2)}) collective-permute-start(bf16[24,3200]{1,0:T(8,128)(2,1)S(1)} %constant_dynamic-update-slice_fusion), channel_id=1, source_target_pairs={{0,24},{1,25},{2,26},{3,27},{4,28},{5,29},{6,30},{7,31},{8,16},{9,... | collective-permute-start | bytes 460808 | tf_op jit(solution)/shard_map/ppermute | solution.py:386
  18.6 50.3 %collective-permute-start = (bf16[2,256,768]{2,1,0:T(8,128)(2,1)S(1)}, bf16[2,256,768]{2,1,0:T(8,128)(2,1)S(1)}, u32[]{:S(2)}, u32[]{:S(2)}) collective-permute-start(bf16[2,256,768]{2,1,0:T(8,128)(2,1)S(1)} %pad_maximum_fusion.4), channel_id=1, source_target_pairs={{0,1},{1,0},{2,3},{3,2},{4,5},{5,4},{6,7},{7,6},{8,9},{9,8},{10,11... | collective-permute-start | bytes 2359304 | tf_op jit(solution)/shard_map/ppermute | solution.py:359
  34.3 6.8 %collective-permute-start.7 = (bf16[2,2,24,1536]{3,2,1,0:T(8,128)(2,1)S(1)}, bf16[2,2,24,1536]{3,2,1,0:T(8,128)(2,1)S(1)}, u32[]{:S(2)}, u32[]{:S(2)}) collective-permute-start(bf16[2,2,24,1536]{3,2,1,0:T(8,128)(2,1)S(1)} %pad_maximum_fusion.15), channel_id=1, source_target_pairs={{0,4},{1,5},{2,6},{3,7},{4,0},{5,1},{6,2},{7,3},{8,12},{9,13},{10,... | collective-permute-start | bytes 884744 | tf_op jit(solution)/shard_map/ppermute | solution.py:386
  36.5 13.8 %collective-permute-start.4 = (bf16[2,2,24,1664]{3,2,1,0:T(8,128)(2,1)S(1)}, bf16[2,2,24,1664]{3,2,1,0:T(8,128)(2,1)S(1)}, u32[]{:S(2)}, u32[]{:S(2)}) collective-permute-start(bf16[2,2,24,1664]{3,2,1,0:T(8,128)(2,1)S(1)} %fusion.27), channel_id=1, source_target_pairs={{0,1},{1,0},{2,3},{3,2},{4,5},{5,4},{6,7},{7,6},{8,9},{9,8},{10,11... | collective-permute-start | bytes 958472 | tf_op jit(solution)/shard_map/ppermute | solution.py:386
  41.3 21.9 %collective-permute-start.8 = (bf16[2,2,2,24,1536]{4,3,2,1,0:T(8,128)(2,1)S(1)}, bf16[2,2,2,24,1536]{4,3,2,1,0:T(8,128)(2,1)S(1)}, u32[]{:S(2)}, u32[]{:S(2)}) collective-permute-start(bf16[2,2,2,24,1536]{4,3,2,1,0:T(8,128)(2,1)S(1)} %pad_maximum_fusion.9), channel_id=1, source_target_pairs={{0,1},{1,0},{2,3},{3,2},{4,5},{5,4},{6,7},{7,6},{8,9},{9,8},{10,11... | collective-permute-start | bytes 1769480 | tf_op jit(solution)/shard_map/ppermute | solution.py:386
  50.5 18.0 %collective-permute-start.5 = (bf16[2,2,2,24,1664]{4,3,1,0,2:T(8,128)(2,1)S(1)}, bf16[2,2,2,24,1664]{4,3,1,0,2:T(8,128)(2,1)S(1)}, u32[]{:S(2)}, u32[]{:S(2)}) collective-permute-start(bf16[2,2,2,24,1664]{4,3,1,0,2:T(8,128)(2,1)S(1)} %pad_maximum_fusion.8), channel_id=1, source_target_pairs={{0,4},{1,5},{2,6},{3,7},{4,0},{5,1},{6,2},{7,3},{8,12},{9,13},{10,... | collective-permute-start | bytes 1916936 | tf_op jit(solution)/shard_map/ppermute | solution.py:386
  63.4 6.8 %collective-permute-start.9 = (bf16[2,2,2,2,24,1536]{5,4,3,2,1,0:T(8,128)(2,1)S(1)}, bf16[2,2,2,2,24,1536]{5,4,3,2,1,0:T(8,128)(2,1)S(1)}, u32[]{:S(2)}, u32[]{:S(2)}) collective-permute-start(bf16[2,2,2,2,24,1536]{5,4,3,2,1,0:T(8,128)(2,1)S(1)} %pad_maximum_fusion.3), channel_id=1, source_target_pairs={{0,2},{1,3},{2,0},{3,1},{4,6},{5,7},{6,4},{7,5},{8,10},{9,11},{10,... | collective-permute-start | bytes 3538952 | tf_op jit(solution)/shard_map/ppermute | solution.py:386
  68.8 3.4 %collective-permute-start.6 = (bf16[2,2,2,2,24,1664]{5,4,1,0,3,2:T(8,128)(2,1)S(1)}, bf16[2,2,2,2,24,1664]{5,4,1,0,3,2:T(8,128)(2,1)S(1)}, u32[]{:S(2)}, u32[]{:S(2)}) collective-permute-start(bf16[2,2,2,2,24,1664]{5,4,1,0,3,2:T(8,128)(2,1)S(1)} %pad_maximum_fusion.2), channel_id=1, source_target_pairs={{0,2},{1,3},{2,0},{3,1},{4,6},{5,7},{6,4},{7,5},{8,10},{9,11},{10,... | collective-permute-start | bytes 3833864 | tf_op jit(solution)/shard_map/ppermute | solution.py:386
  104.1 30.9 %copy-start.3 = (s32[4]{0:T(128)S(1)}, s32[4]{0:T(128)}, u32[]{:S(2)}) copy-start(s32[4]{0:T(128)} %constant.74.clone) | copy-start | bytes 52
  131.1 16.0 %collective-permute-start.10 = (bf16[2,2,4,96,768]{4,3,2,1,0:T(8,128)(2,1)}, bf16[2,2,4,96,768]{4,3,2,1,0:T(8,128)(2,1)}, u32[]{:S(2)}, u32[]{:S(2)}) collective-permute-start(bf16[2,2,4,96,768]{4,3,2,1,0:T(8,128)(2,1)} %get-tuple-element.105), channel_id=1, source_target_pairs={{0,2},{1,3},{2,0},{3,1},{4,6},{5,7},{6,4},{7,5},{8,10},{9,11},{10,... | collective-permute-start | bytes 7077896 | tf_op jit(solution)/shard_map/ppermute | solution.py:386
  131.4 15.7 %collective-permute-start.11 = (bf16[2,2,4,96,768]{4,3,2,1,0:T(8,128)(2,1)}, bf16[2,2,4,96,768]{4,3,2,1,0:T(8,128)(2,1)}, u32[]{:S(2)}, u32[]{:S(2)}) collective-permute-start(bf16[2,2,4,96,768]{4,3,2,1,0:T(8,128)(2,1)} %get-tuple-element.106), channel_id=1, source_target_pairs={{0,2},{1,3},{2,0},{3,1},{4,6},{5,7},{6,4},{7,5},{8,10},{9,11},{10,... | collective-permute-start | bytes 7077896 | tf_op jit(solution)/shard_map/ppermute | solution.py:386
  133.5 11.6 %collective-permute-start.12 = (bf16[256,768]{1,0:T(8,128)(2,1)}, bf16[256,768]{1,0:T(8,128)(2,1)}, u32[]{:S(2)}, u32[]{:S(2)}) collective-permute-start(bf16[256,768]{1,0:T(8,128)(2,1)} %constant_dynamic-slice_fusion.1), channel_id=1, source_target_pairs={{0,1},{1,0},{2,3},{3,2},{4,5},{5,4},{6,7},{7,6},{8,9},{9,8},{10,11... | collective-permute-start | bytes 1179656 | tf_op jit(solution)/shard_map/ppermute | solution.py:370
  152.5 28.9 %collective-permute-start.15 = (bf16[2,4,96,768]{3,2,1,0:T(8,128)(2,1)}, bf16[2,4,96,768]{3,2,1,0:T(8,128)(2,1)}, u32[]{:S(2)}, u32[]{:S(2)}) collective-permute-start(bf16[2,4,96,768]{3,2,1,0:T(8,128)(2,1)} %fusion.8), channel_id=1, source_target_pairs={{0,4},{1,5},{2,6},{3,7},{4,0},{5,1},{6,2},{7,3},{8,12},{9,13},{10,... | collective-permute-start | bytes 3538952 | tf_op jit(solution)/shard_map/ppermute | solution.py:386
  153.9 27.5 %collective-permute-start.16 = (bf16[2,4,96,768]{3,2,1,0:T(8,128)(2,1)}, bf16[2,4,96,768]{3,2,1,0:T(8,128)(2,1)}, u32[]{:S(2)}, u32[]{:S(2)}) collective-permute-start(bf16[2,4,96,768]{3,2,1,0:T(8,128)(2,1)} %fusion.9), channel_id=1, source_target_pairs={{0,1},{1,0},{2,3},{3,2},{4,5},{5,4},{6,7},{7,6},{8,9},{9,8},{10,11... | collective-permute-start | bytes 3538952 | tf_op jit(solution)/shard_map/ppermute | solution.py:386
  180.8 10.9 %collective-permute-start.13 = (bf16[2,2,4,48,768]{4,3,2,1,0:T(8,128)(2,1)}, bf16[2,2,4,48,768]{4,3,2,1,0:T(8,128)(2,1)}, u32[]{:S(2)}, u32[]{:S(2)}) collective-permute-start(bf16[2,2,4,48,768]{4,3,2,1,0:T(8,128)(2,1)} %get-tuple-element.139), channel_id=1, source_target_pairs={{0,2},{1,3},{2,0},{3,1},{4,6},{5,7},{6,4},{7,5},{8,10},{9,11},{10,... | collective-permute-start | bytes 3538952 | tf_op jit(solution)/shard_map/ppermute | solution.py:386
  180.9 10.8 %collective-permute-start.14 = (bf16[2,2,4,48,768]{4,3,2,1,0:T(8,128)(2,1)}, bf16[2,2,4,48,768]{4,3,2,1,0:T(8,128)(2,1)}, u32[]{:S(2)}, u32[]{:S(2)}) collective-permute-start(bf16[2,2,4,48,768]{4,3,2,1,0:T(8,128)(2,1)} %get-tuple-element.140), channel_id=1, source_target_pairs={{0,2},{1,3},{2,0},{3,1},{4,6},{5,7},{6,4},{7,5},{8,10},{9,11},{10,... | collective-permute-start | bytes 3538952 | tf_op jit(solution)/shard_map/ppermute | solution.py:386
  187.6 4.2 %collective-permute-start.17 = (bf16[2,2,4,8,768]{4,3,2,1,0:T(8,128)(2,1)S(1)}, bf16[2,2,4,8,768]{4,3,2,1,0:T(8,128)(2,1)S(1)}, u32[]{:S(2)}, u32[]{:S(2)}) collective-permute-start(bf16[2,2,4,8,768]{4,3,2,1,0:T(8,128)(2,1)S(1)} %get-tuple-element.266), channel_id=1, source_target_pairs={{0,2},{1,3},{2,0},{3,1},{4,6},{5,7},{6,4},{7,5},{8,10},{9,11},{10,... | collective-permute-start | bytes 589832 | tf_op jit(solution)/shard_map/ppermute | solution.py:386
  189.6 16.2 %collective-permute-start.20 = (bf16[4,96,768]{2,1,0:T(8,128)(2,1)S(1)}, bf16[4,96,768]{2,1,0:T(8,128)(2,1)S(1)}, u32[]{:S(2)}, u32[]{:S(2)}) collective-permute-start(bf16[4,96,768]{2,1,0:T(8,128)(2,1)S(1)} %copy-done.33), channel_id=1, source_target_pairs={{0,1},{1,0},{2,3},{3,2},{4,5},{5,4},{6,7},{7,6},{8,9},{9,8},{10,11... | collective-permute-start | bytes 1769480 | tf_op jit(solution)/shard_map/ppermute | solution.py:386
  191.1 16.2 %collective-permute-start.21 = (bf16[4,96,768]{2,1,0:T(8,128)(2,1)S(1)}, bf16[4,96,768]{2,1,0:T(8,128)(2,1)S(1)}, u32[]{:S(2)}, u32[]{:S(2)}) collective-permute-start(bf16[4,96,768]{2,1,0:T(8,128)(2,1)S(1)} %copy-done.32), channel_id=1, source_target_pairs={{0,4},{1,5},{2,6},{3,7},{4,0},{5,1},{6,2},{7,3},{8,12},{9,13},{10,... | collective-permute-start | bytes 1769480 | tf_op jit(solution)/shard_map/ppermute | solution.py:386
  197.1 23.0 %collective-permute-start.19 = (bf16[2,4,56,768]{3,2,1,0:T(8,128)(2,1)S(1)}, bf16[2,4,56,768]{3,2,1,0:T(8,128)(2,1)S(1)}, u32[]{:S(2)}, u32[]{:S(2)}) collective-permute-start(bf16[2,4,56,768]{3,2,1,0:T(8,128)(2,1)S(1)} %pad_maximum_fusion.7), channel_id=1, source_target_pairs={{0,1},{1,0},{2,3},{3,2},{4,5},{5,4},{6,7},{7,6},{8,9},{9,8},{10,11... | collective-permute-start | bytes 2064392 | tf_op jit(solution)/shard_map/ppermute | solution.py:386
  198.6 20.4 %collective-permute-start.18 = (bf16[2,4,48,768]{3,2,1,0:T(8,128)(2,1)S(1)}, bf16[2,4,48,768]{3,2,1,0:T(8,128)(2,1)S(1)}, u32[]{:S(2)}, u32[]{:S(2)}) collective-permute-start(bf16[2,4,48,768]{3,2,1,0:T(8,128)(2,1)S(1)} %fusion.18), channel_id=1, source_target_pairs={{0,4},{1,5},{2,6},{3,7},{4,0},{5,1},{6,2},{7,3},{8,12},{9,13},{10,... | collective-permute-start | bytes 1769480 | tf_op jit(solution)/shard_map/ppermute | solution.py:386
  209.9 16.3 %collective-permute-start.27 = (bf16[2,192,768]{2,1,0:T(8,128)(2,1)S(1)}, bf16[2,192,768]{2,1,0:T(8,128)(2,1)S(1)}, u32[]{:S(2)}, u32[]{:S(2)}) collective-permute-start(bf16[2,192,768]{2,1,0:T(8,128)(2,1)S(1)} %pad_maximum_fusion.10), channel_id=1, source_target_pairs={{0,8},{1,9},{2,10},{3,11},{4,12},{5,13},{6,14},{7,15},{8,0},{9,1},... | collective-permute-start | bytes 1769480 | tf_op jit(solution)/shard_map/ppermute | solution.py:386
  220.1 36.8 %copy-start.29 = (bf16[2,4,56,768]{3,2,1,0:T(8,128)(2,1)}, bf16[2,4,56,768]{3,2,1,0:T(8,128)(2,1)S(1)}, u32[]{:S(2)}) copy-start(bf16[2,4,56,768]{3,2,1,0:T(8,128)(2,1)S(1)} %collective-permute-done.19) | copy-start | bytes 2064388
  222.5 11.5 %collective-permute-start.24 = (bf16[4,56,768]{2,1,0:T(8,128)(2,1)S(1)}, bf16[4,56,768]{2,1,0:T(8,128)(2,1)S(1)}, u32[]{:S(2)}, u32[]{:S(2)}) collective-permute-start(bf16[4,56,768]{2,1,0:T(8,128)(2,1)S(1)} %pad_maximum_fusion.11), channel_id=1, source_target_pairs={{0,4},{1,5},{2,6},{3,7},{4,0},{5,1},{6,2},{7,3},{8,12},{9,13},{10,... | collective-permute-start | bytes 1032200 | tf_op jit(solution)/shard_map/ppermute | solution.py:386
  224.0 9.9 %collective-permute-start.23 = (bf16[4,48,768]{2,1,0:T(8,128)(2,1)S(1)}, bf16[4,48,768]{2,1,0:T(8,128)(2,1)S(1)}, u32[]{:S(2)}, u32[]{:S(2)}) collective-permute-start(bf16[4,48,768]{2,1,0:T(8,128)(2,1)S(1)} %fusion.21), channel_id=1, source_target_pairs={{0,1},{1,0},{2,3},{3,2},{4,5},{5,4},{6,7},{7,6},{8,9},{9,8},{10,11... | collective-permute-start | bytes 884744 | tf_op jit(solution)/shard_map/ppermute | solution.py:386
  224.6 16.0 %collective-permute-start.22 = (bf16[256,768]{1,0:T(8,128)(2,1)S(1)}, bf16[256,768]{1,0:T(8,128)(2,1)S(1)}, u32[]{:S(2)}, u32[]{:S(2)}) collective-permute-start(bf16[256,768]{1,0:T(8,128)(2,1)S(1)} %constant_dynamic-slice_fusion), channel_id=1, source_target_pairs={{0,1},{1,0},{2,3},{3,2},{4,5},{5,4},{6,7},{7,6},{8,9},{9,8},{10,11... | collective-permute-start | bytes 1179656 | tf_op jit(solution)/shard_map/ppermute | solution.py:370
  227.6 15.0 %collective-permute-start.28 = (bf16[1,192,768]{2,1,0:T(8,128)(2,1)S(1)}, bf16[1,192,768]{2,1,0:T(8,128)(2,1)S(1)}, u32[]{:S(2)}, u32[]{:S(2)}) collective-permute-start(bf16[1,192,768]{2,1,0:T(8,128)(2,1)S(1)} %pad_maximum_fusion.17), channel_id=1, source_target_pairs={{0,16},{1,17},{2,18},{3,19},{4,20},{5,21},{6,22},{7,23},{8,24},{9,... | collective-permute-start | bytes 884744 | tf_op jit(solution)/shard_map/ppermute | solution.py:386
  236.2 11.7 %collective-permute-start.25 = (bf16[2,104,768]{2,1,0:T(8,128)(2,1)S(1)}, bf16[2,104,768]{2,1,0:T(8,128)(2,1)S(1)}, u32[]{:S(2)}, u32[]{:S(2)}) collective-permute-start(bf16[2,104,768]{2,1,0:T(8,128)(2,1)S(1)} %pad_maximum_fusion.12), channel_id=1, source_target_pairs={{0,8},{1,9},{2,10},{3,11},{4,12},{5,13},{6,14},{7,15},{8,0},{9,1},... | collective-permute-start | bytes 958472 | tf_op jit(solution)/shard_map/ppermute | solution.py:386
  248.9 8.0 %collective-permute-start.26 = (bf16[1,104,768]{2,1,0:T(8,128)(2,1)S(1)}, bf16[1,104,768]{2,1,0:T(8,128)(2,1)S(1)}, u32[]{:S(2)}, u32[]{:S(2)}) collective-permute-start(bf16[1,104,768]{2,1,0:T(8,128)(2,1)S(1)} %pad_maximum_fusion.18), channel_id=1, source_target_pairs={{0,16},{1,17},{2,18},{3,19},{4,20},{5,21},{6,22},{7,23},{8,24},{9,... | collective-permute-start | bytes 479240 | tf_op jit(solution)/shard_map/ppermute | solution.py:386
  (46 other events, 300.5 us)
Sparse Core Ops, SparseCore 0:
  11.6 92.4 all-gather.1

commit v4 on v3

--- a/solution.py
+++ b/solution.py
@@ -6,7 +6,6 @@
 from jax.sharding import PartitionSpec as P
 
 HD = 64
-RB = 128
 epsilon = 1e-06
 
 
@@ -25,92 +24,77 @@
     return lax.dot_general(a, b, (((0,), (0,)), ((), ())), preferred_element_type=jnp.float32)
 
 
-def diag_sums(slab):
-    rows = slab.shape[0]
-    while rows > 1:
-        rows //= 2
-        slab = pltpu.roll(slab[:rows], rows, 1) + slab[rows:]
-    return slab
-def bias_columns(vec):
-    wide = jnp.broadcast_to(vec, (RB, vec.shape[1]))
-    return pltpu.roll(wide, vec.shape[1] - RB + 1, 1, stride=1, stride_axis=0).T
-
-def attend_kernel(q_ref, k_ref, v_ref, vec_ref, o_ref, lse_ref, slab_ref, out_ref):
-    length = q_ref.shape[0]
+def biased_scores(k, q, bias_row):
+    length = k.shape[0]
+    wide = jnp.broadcast_to(bias_row, (length, 2 * length))
+    bias = pltpu.roll(wide, length, 1, stride=1, stride_axis=0)[:, :length]
+    return dot_nt(k, q) + bias
+
+
+def diagonal_sums(grads):
+    length = grads.shape[0]
+    rows = jnp.concatenate([grads, jnp.zeros_like(grads)], axis=1)
+    while rows.shape[0] > 1:
+        half = rows.shape[0] // 2
+        rows = pltpu.roll(rows[:half], half, 1) + rows[half:]
+    return pltpu.roll(rows, 1, 1)
+
+
+def attend_kernel(q_ref, k_ref, v_ref, bias_ref, o_ref, turned_ref, lse_ref):
     for head in range(2):
         cols = slice(head * HD, (head + 1) * HD)
-        k = k_ref[:, cols]
-        vt = v_ref[:, cols].T
-        slab_ref[...] = bias_columns(vec_ref[0, head:head+1, :])
-        for first in range(0, length, RB):
-            at = length - RB - first
-            s = dot_nt(k, q_ref[first:first+RB, cols]) + slab_ref[at:at+length, :]
-            peak = jnp.max(s, axis=0, keepdims=True)
-            e = jnp.exp(s - peak)
-            total = jnp.sum(e, axis=0, keepdims=True)
-            lse_ref[0, head:head+1, first:first+RB] = peak + jnp.log(total)
-            p = e * (1.0 / total)
-            out_ref[head*HD:(head+1)*HD, first:first+RB] = dot_nn(vt, p.astype(jnp.bfloat16))
-    o_ref[...] = out_ref[...].T.astype(jnp.bfloat16)
-
-def attend(qk, v, vec):
-    length, width = v.shape[0], qk.shape[1] // 2
+        s = biased_scores(k_ref[:, cols], q_ref[:, cols], bias_ref[0, head : head + 1, :])
+        peak = jnp.max(s, axis=0, keepdims=True)
+        e = jnp.exp(s - peak)
+        total = jnp.sum(e, axis=0, keepdims=True)
+        lse_ref[0, head : head + 1, :] = peak + jnp.log(total)
+        p = (e * (1.0 / total)).astype(jnp.bfloat16)
+        turned_ref[cols, :] = dot_nn(v_ref[:, cols].T, p).astype(jnp.bfloat16)
+    o_ref[...] = turned_ref[...].T
+
+
+def attend(qk, v, bias_rows):
+    length, width = v.shape
     steps = width // (2 * HD)
     spec = lambda at: pl.BlockSpec((length, 2 * HD), lambda h: (0, at + h))
     row = lambda columns: pl.BlockSpec((1, 2, columns), lambda h: (h, 0, 0))
     return pl.pallas_call(
         attend_kernel,
         grid=(steps,),
-        in_specs=[spec(0), spec(steps), spec(0), row(vec.shape[2])],
-        out_specs=[spec(0), row(length)],
+        in_specs=[spec(0), spec(steps), spec(0), row(2 * length)],
+        out_specs=[spec(0), pl.BlockSpec((2 * HD, length), lambda h: (h, 0)), row(length)],
         out_shape=[
             jax.ShapeDtypeStruct((length, width), jnp.bfloat16),
+            jax.ShapeDtypeStruct((width, length), jnp.bfloat16),
             jax.ShapeDtypeStruct((steps, 2, length), jnp.float32),
-        ],
-        scratch_shapes=[
-            pltpu.VMEM((vec.shape[2], RB), jnp.float32),
-            pltpu.VMEM((2 * HD, length), jnp.float32),
         ],
         cost_estimate=SMALL_COST,
         compiler_params=pltpu.CompilerParams(vmem_limit_bytes=48 << 20),
-    )(qk, qk, v, vec)
-
-
-def attend_back_kernel(q_ref, k_ref, v_ref, go_ref, lse_ref, vec_ref, dq_ref, dk_ref, dv_ref, dvec_ref, slab_ref, dslab_ref, dqt_ref):
-    length = q_ref.shape[0]
+    )(qk, qk, v, bias_rows)
+
+
+def attend_back_kernel(
+    q_ref, k_ref, v_ref, go_ref, lse_ref, bias_ref, dq_ref, dk_ref, dv_ref, db_ref, dqt_ref
+):
     for head in range(2):
         cols = slice(head * HD, (head + 1) * HD)
-        k = k_ref[:, cols]
-        v = v_ref[:, cols]
-        kt = k.T
-        slab_ref[...] = bias_columns(vec_ref[0, head:head+1, :])
-        lse = lse_ref[0, head:head+1, :]
-        dslab_ref[...] = jnp.zeros(dslab_ref.shape, jnp.float32)
-        dk = jnp.zeros((length, HD), jnp.float32)
-        dv = jnp.zeros((length, HD), jnp.float32)
-        for first in range(0, length, RB):
-            at = length - RB - first
-            rows = slice(first, first + RB)
-            q = q_ref[rows, cols]
-            go = go_ref[rows, cols]
-            p = jnp.exp(dot_nt(k, q) + slab_ref[at:at+length, :] - lse[:, rows])
-            gp = dot_nt(v, go)
-            ds = (p * (gp - jnp.sum(p * gp, axis=0, keepdims=True))).astype(jnp.bfloat16)
-            dslab_ref[at:at+length, :] += ds.astype(jnp.float32)
-            dqt_ref[head*HD:(head+1)*HD, rows] = dot_nn(kt, ds)
-            dk += dot_nn(ds, q)
-            dv += dot_nn(p.astype(jnp.bfloat16), go)
-        dk_ref[:, cols] = dk.astype(jnp.bfloat16)
-        dv_ref[:, cols] = dv.astype(jnp.bfloat16)
-        dvec_ref[0, head:head+1, :] = diag_sums(dslab_ref[...].T)
+        q, k, v, go = q_ref[:, cols], k_ref[:, cols], v_ref[:, cols], go_ref[:, cols]
+        s = biased_scores(k, q, bias_ref[0, head : head + 1, :])
+        p = jnp.exp(s - lse_ref[0, head : head + 1, :])
+        gp = dot_nt(v, go)
+        ds = (p * (gp - jnp.sum(p * gp, axis=0, keepdims=True))).astype(jnp.bfloat16)
+        dqt_ref[cols, :] = dot_nn(k.T, ds)
+        dk_ref[:, cols] = dot_nn(ds, q).astype(jnp.bfloat16)
+        dv_ref[:, cols] = dot_nn(p.astype(jnp.bfloat16), go).astype(jnp.bfloat16)
+        db_ref[0, head : head + 1, :] = diagonal_sums(ds.astype(jnp.float32))
     dq_ref[...] = dqt_ref[...].T.astype(jnp.bfloat16)
 
-def attend_back(qk, v, go, lse, vec, start, count):
+
+def attend_back(qk, v, go, lse, bias_rows, start, count):
     length, width = go.shape
     steps = width // (2 * HD)
     spec = lambda at: pl.BlockSpec((length, 2 * HD), lambda h: (0, at + h))
     row = lambda at, columns: pl.BlockSpec((1, 2, columns), lambda h: (at + h, 0, 0))
-    span = vec.shape[2]
     o = jax.ShapeDtypeStruct((length, count * 2 * HD), jnp.bfloat16)
     return pl.pallas_call(
         attend_back_kernel,
@@ -121,18 +105,14 @@
             spec(start),
             spec(start),
             row(start, length),
-            row(start, span),
+            row(start, 2 * length),
         ],
-        out_specs=[spec(0), spec(0), spec(0), row(0, span)],
-        out_shape=[o, o, o, jax.ShapeDtypeStruct((count, 2, span), jnp.float32)],
-        scratch_shapes=[
-            pltpu.VMEM((span, RB), jnp.float32),
-            pltpu.VMEM((span, RB), jnp.float32),
-            pltpu.VMEM((2 * HD, length), jnp.float32),
-        ],
+        out_specs=[spec(0), spec(0), spec(0), row(0, 2 * length)],
+        out_shape=[o, o, o, jax.ShapeDtypeStruct((count, 2, 2 * length), jnp.float32)],
+        scratch_shapes=[pltpu.VMEM((2 * HD, length), jnp.float32)],
         cost_estimate=SMALL_COST,
         compiler_params=pltpu.CompilerParams(vmem_limit_bytes=48 << 20),
-    )(qk, qk, v, go, lse, vec)
+    )(qk, qk, v, go, lse, bias_rows)
 
 
 def ffn_step(x_ref, top_ref, win_ref, wout, middle_ref, gain_ref, wo_ref, outs, scratch):
@@ -152,6 +132,8 @@
         out_ref[...] = middle_ref[...]
         gx_ref[...] = jnp.zeros(gx_ref.shape, jnp.float32)
 
+    d_in = dot_nn(xt_ref[...], gpre).astype(jnp.bfloat16)
+    d_out = dot_tn(hid, top).astype(jnp.bfloat16)
     out_ref[...] += dot_nn(hid, wout)
     gx_ref[...] += dot_nt(gpre, win_ref[...])
 
@@ -166,17 +148,7 @@
         grad_low_ref[...] = low
         grad_attended_ref[...] = dot_nt(low, wo_ref[...]).astype(jnp.bfloat16)
 
-    return dot_nn(xt_ref[...], gpre).astype(jnp.bfloat16), dot_tn(hid, top).astype(jnp.bfloat16)
-
-
-def turn_kernel(a_ref, b_ref, a_out_ref, b_out_ref):
-    a_out_ref[...] = a_ref[...].T
-    b_out_ref[...] = b_ref[...].T
-
-
-def turn(a, b):
-    shape = jax.ShapeDtypeStruct(a.shape[::-1], a.dtype)
-    return pl.pallas_call(turn_kernel, out_shape=[shape, shape])(a, b)
+    return d_in, d_out
 
 
 def store_blocks(seat_ref, value, rows, blocks, keep_ref, send_ref, put):
@@ -293,18 +265,22 @@
 
 
 def weight_grads(ranks, left, rights, left_last, right_last):
-    width = left.shape[0]
+    width = left.shape[1]
     own = width // ranks.devices
     far = ranks.devices // 8
     if own % 8:
         block = lambda a, b: dot_nn(a, b).astype(jnp.bfloat16).reshape(ranks.devices, own, width)
-        blocks = [block(left, right) for right in rights] + [block(left_last, right_last)]
+        blocks = [block(left.T, right) for right in rights] + [block(left_last, right_last)]
         pairs = blocks[:2], blocks[2:]
         return [ranks.by_seat(jnp.concatenate(pair, axis=1)) for pair in pairs]
     args = [left, left_last, *rights, right_last]
 
     def kernel(seat_ref, *refs):
-        ins, outs = refs[: len(args)], refs[len(args) :]
+        ins, outs, turned_ref = refs[: len(args)], refs[len(args) : -1], refs[-1]
+
+        @pl.when(pl.program_id(0) == 0)
+        def _():
+            turned_ref[...] = ins[0][...].T
 
         def put(ref, x, y, far_at, block):
             ref[x, y, far_at ^ seat_ref[3]] = block
@@ -313,7 +289,8 @@
 
             @pl.when(pl.program_id(0) == step)
             def _():
-                value = dot_nn(ins[step == 3][...], ins[2 + step][...]).astype(jnp.bfloat16)
+                lhs = ins[1] if step == 3 else turned_ref
+                value = dot_nn(lhs[...], ins[2 + step][...]).astype(jnp.bfloat16)
                 lane = 2 * (step // 2)
                 store_blocks(
                     seat_ref, value, own, ranks.devices, outs[lane], outs[lane + 1], put
@@ -329,6 +306,7 @@
             grid=(4,),
             in_specs=[whole(a) for a in args],
             out_specs=[early, early, late, late],
+            scratch_shapes=[pltpu.VMEM(left.shape[::-1], left.dtype)],
         ),
         out_shape=[jax.ShapeDtypeStruct((2, 2, far, 2 * own, width), jnp.bfloat16)] * 4,
         cost_estimate=SMALL_COST,
@@ -348,7 +326,7 @@
 
 
 def bucket_picker(buckets, bucket_count):
-    padded = jnp.pad(buckets, (0, 1), constant_values=-1)
+    padded = jnp.pad(buckets[::-1], (1, 0), constant_values=-1)
     rows = jnp.arange(bucket_count, dtype=jnp.int32)[:, None]
     return (padded[None, :] == rows).astype(jnp.float32)
 
@@ -583,22 +561,19 @@
     tables = high[: 2 * own, 2 * width + 2 : 2 * width + used].astype(f32)
     tables = tables.reshape(2, own, 3, -1).sum(axis=2).reshape(2 * head_pairs, -1)
     picker = bucket_picker(buckets, bias_table.shape[1])
-    vec = jnp.dot(tables, picker, precision=lax.Precision.HIGHEST, preferred_element_type=f32)
-    vec = vec.reshape(head_pairs, 2, -1)
+    bias_rows = jnp.dot(tables, picker, precision=lax.Precision.HIGHEST, preferred_element_type=f32)
+    bias_rows = bias_rows.reshape(head_pairs, 2, -1)
 
     inputs = inputs.astype(f32)
     attn_scale = rms_scale(inputs)
     attn_input = (inputs * attn_scale * g_attn).astype(bf16)
     qk = jnp.dot(attn_input, low, preferred_element_type=f32).astype(bf16)
     v = jnp.dot(attn_input, w_parts[2], preferred_element_type=f32).astype(bf16)
-    attended, lse = attend(qk, v, vec)
+    attended, turned_attended, lse = attend(qk, v, bias_rows)
     middle = inputs + jnp.dot(attended, w_o, preferred_element_type=f32)
     ffn_scale = rms_scale(middle)
     ffn_input = (middle * ffn_scale * g_ffn).astype(bf16)
-    attn_turned, attended_turned = turn(attn_input, attended)
-    gathered, (ffn_input, top, attn_turned, attended_turned) = together(
-        gathered, (ffn_input, top, attn_turned, attended_turned)
-    )
+    gathered, (ffn_input, top) = together(gathered, (ffn_input, top))
     (layer_low, grad_middle, grad_middle_low, grad_attended), d_ffn = ffn(
         ffn_input, top, gathered, middle, g_ffn[None], w_o, ranks
     )
@@ -607,14 +582,15 @@
 
     layer_out = split_sequence(layer_low, half)
     each = head_pairs // 3
-    piece_0 = attend_back(qk, v, grad_attended, lse, vec, 0, each)
-    piece_0, grad_attended, layer_out = big.advance((piece_0, grad_attended, layer_out))
-    piece_1 = attend_back(qk, v, grad_attended, lse, vec, each, head_pairs - each)
+    piece_0 = attend_back(qk, v, grad_attended, lse, bias_rows, 0, each)
+    piece_0, grad_attended = big.advance((piece_0, grad_attended))
+    piece_1 = attend_back(qk, v, grad_attended, lse, bias_rows, each, head_pairs - each)
+    piece_1, layer_out = together(piece_1, layer_out)
     d_vec = jnp.concatenate([piece_0[3], piece_1[3]])
     grads = [jnp.concatenate([piece_0[at], piece_1[at]], axis=1) for at in range(3)]
     small = Scatter(
         ranks,
-        weight_grads(ranks, attn_turned, grads, attended_turned, grad_middle_low),
+        weight_grads(ranks, attn_input, grads, turned_attended, grad_middle_low),
         [[(2, [0]), (0, [1, 2])], [(0, [0]), (2, [1, 2])]],
     )
     small.outgoing, (grads, d_vec) = together(small.outgoing, (grads, d_vec))
@@ -627,8 +603,10 @@
         preferred_element_type=f32,
     )
     extra = jnp.concatenate(bf16_parts(d_table.reshape(2, bias_table.size), 2), axis=1)
-    extra = jnp.pad(extra[:, None], ((0, 0), (0, 7), (0, width - 2 * bias_table.size)))
-    small.join(*ranks.by_seat(jnp.tile(extra, (devices // 2, 1, 1))))
+    extra = jnp.where(half == 0, extra, extra[::-1])
+    extra = jnp.pad(extra[None, :, None, None], ((0, 0),) * 4 + ((0, width - 2 * bias_table.size),))
+    extra = jnp.broadcast_to(extra, (2, 2, devices // 8, 8, width))
+    small.join(extra, extra)
     grads = small.advance(grads)
     grad_attn_in = sum(dot_nt(grad, w) for grad, w in zip(grads, w_parts))
     grad_inputs = norm_back(grad_attn_in, inputs, attn_scale, g_attn)

time: 269 us -> 264 us (0.981)
  Pallas kernels: 77.4 us -> 62.2 us
  waiting for transfers between devices: 74.5 us -> 87.3 us
    all_gather x1, waiting for transfers between devices: 1.9 us -> 12.6 us  [shards(): lax.all_gather(jnp.concatenate([w_in, groups], axis=1), ('rows', 'seq'),...]
    pallas_call x2, Pallas kernels: 24.6 us -> 18.7 us  [attend_back(): pl.pallas_call(attend_back_kernel, grid=(count,), in_specs=[spec(start),...]
    pallas_call x1, Pallas kernels: 14.4 us -> 8.92 us  [attend(): pl.pallas_call(attend_kernel, grid=(steps,), in_specs=[spec(0), spec(step...]
    ppermute x26, waiting for transfers between devices: 68.5 us -> 72.1 us  [partner_sends(): lax.ppermute(array, ('rows', 'seq'), [(b, b ^ mask) for b in range(device...]
    pallas_call x1 -> x0, Pallas kernels: 2.9 us -> none  [turn(): return pl.pallas_call(turn_kernel, out_shape=[shape, shape])(a, b)]
    another operation x10 -> x11, other arithmetic: 8.43 us -> 8.08 us
    unnamed x103 -> x86, local copies, waits for them, and re-layouts: 5.69 us -> 5.4 us
    add x6 -> x5, other arithmetic: 5.51 us -> 5.39 us  [summed(): return sum((pick(term).astype(jnp.float32) for term in terms))]
  transfers between devices with their start and end apart: 30 -> 30, of which waited for: 17 -> 18; matrix products, arithmetic and copies ran while one was open for 19% -> 20% of each run, Pallas kernels for 19% -> 14%
where the time goes in v4:
time: 264 us; the launch traced here: 263 us
  waiting for transfers between devices  87.3 us (33%)
  Pallas kernels  62.2 us (24%)
  other arithmetic  43 us (16%)
  starting transfers between devices  32.9 us (12%)
  between operations  15.1 us (6%)
  local copies, waits for them, and re-layouts  14.1 us (5%)
  matrix products  8.95 us (3%)
    ppermute x26, waiting for transfers between devices, partner_sends(): lax.ppermute(array, ('rows', 'seq'), [(b, b ^ mask) for b in range(device...  72.1 us
    ppermute x26, starting transfers between devices, partner_sends(): lax.ppermute(array, ('rows', 'seq'), [(b, b ^ mask) for b in range(device...  28.2 us
    pallas_call x1, Pallas kernels, ffn(): pl.pallas_call(ffn_kernel, grid_spec=pltpu.PrefetchScalarGridSpec(num_sca...  26.2 us
    pallas_call x2, Pallas kernels, attend_back(): pl.pallas_call(attend_back_kernel, grid=(count,), in_specs=[spec(start),...  18.7 us
    all_gather x1, waiting for transfers between devices, shards(): lax.all_gather(jnp.concatenate([w_in, groups], axis=1), ('rows', 'seq'),...  12.6 us
    convert_element_type x6, other arithmetic, prepare(): self.outgoing.append(total.astype(jnp.bfloat16))  12.5 us
    pallas_call x1, Pallas kernels, attend(): pl.pallas_call(attend_kernel, grid=(steps,), in_specs=[spec(0), spec(step...  8.92 us
    pallas_call x1, Pallas kernels, weight_grads(): pl.pallas_call(kernel, grid_spec=pltpu.PrefetchScalarGridSpec(num_scalar_...  8.39 us
  transfers between devices with their start and end apart: 30, of which 18 were waited for; matrix products, arithmetic and copies ran while one was open for 20% of the time, Pallas kernels for 14%

profile of v4, /device:TPU:0, one launch (start us, length us, event | category | flops | bytes accessed | tf_op | source)
XLA Modules:
  0.0 263.5 jit_solution(5506788892822669762)
XLA Ops:
  8.4 1.6 pad_maximum_fusion.16
  12.7 4.1 %collective-permute-start.2 = (bf16[24,3200]{1,0:T(8,128)(2,1)S(1)}, bf16[24,3200]{1,0:T(8,128)(2,1)S(1)}, u32[]{:S(2)}, u32[]{:S(2)}) collective-permute-start(bf16[24,3200]{1,0:T(8,128)(2,1)S(1)} %constant_dynamic-update-slice_fusion), channel_id=1, source_target_pairs={{0,16},{1,17},{2,18},{3,19},{4,20},{5,21},{6,22},{7,23},{8,24},{9,... | collective-permute-start | bytes 460808 | tf_op jit(solution)/shard_map/ppermute | solution.py:364
  20.4 11.3 %collective-permute-done.1 = bf16[24,3200]{1,0:T(8,128)(2,1)} collective-permute-done((bf16[24,3200]{1,0:T(8,128)(2,1)S(1)}, bf16[24,3200]{1,0:T(8,128)(2,1)}, u32[]{:S(2)}, u32[]{:S(2)}) %collective-permute-start.1) | collective-permute-done | bytes 153632 | tf_op jit(solution)/shard_map/ppermute | solution.py:364
  33.7 1.8 collective-permute-start.7
  36.1 2.2 collective-permute-start.4
  38.3 2.2 collective-permute-done.7
  40.7 2.4 collective-permute-start.8
  43.1 6.3 %collective-permute-done.4 = bf16[2,2,24,1664]{3,2,1,0:T(8,128)(2,1)S(1)} collective-permute-done((bf16[2,2,24,1664]{3,2,1,0:T(8,128)(2,1)S(1)}, bf16[2,2,24,1664]{3,2,1,0:T(8,128)(2,1)S(1)}, u32[]{:S(2)}, u32[]{:S(2)}) %collective-permute-start.4) | collective-permute-done | bytes 319520 | tf_op jit(solution)/shard_map/ppermute | solution.py:364
  50.9 12.3 %collective-permute-done.8 = bf16[2,2,2,24,1536]{4,3,2,1,0:T(8,128)(2,1)S(1)} collective-permute-done((bf16[2,2,2,24,1536]{4,3,2,1,0:T(8,128)(2,1)S(1)}, bf16[2,2,2,24,1536]{4,3,2,1,0:T(8,128)(2,1)S(1)}, u32[]{:S(2)}, u32[]{:S(2)}) %collective-permute-start.8) | collective-permute-done | bytes 589856 | tf_op jit(solution)/shard_map/ppermute | solution.py:364
  63.4 5.6 %collective-permute-done.5 = bf16[2,2,2,24,1664]{4,3,1,0,2:T(8,128)(2,1)S(1)} collective-permute-done((bf16[2,2,2,24,1664]{4,3,1,0,2:T(8,128)(2,1)S(1)}, bf16[2,2,2,24,1664]{4,3,1,0,2:T(8,128)(2,1)S(1)}, u32[]{:S(2)}, u32[]{:S(2)}) %collective-permute-start.5) | collective-permute-done | bytes 639008 | tf_op jit(solution)/shard_map/ppermute | solution.py:364
  79.5 8.9 %shard_map.203 = (bf16[512,768]{1,0:T(8,128)(2,1)S(1)}, bf16[768,512]{1,0:T(8,128)(2,1)S(1)}, f32[6,2,512]{2,1,0:T(2,128)S(1)}) custom-call(bf16[512,1536]{1,0:T(8,128)(2,1)S(1)} %convolution_convert_fusion.q_ref.k_ref, bf16[512,1536]{1,0:T(8,128)(2,1)S(1)} %convolution_convert_fusion.q_ref.k_ref, bf16[512,768]{1,0:T(8,128)(2,1)S(1)} %convolution_convert_fusion.1.v_ref, ...), custom_call_target="tpu_custom_call" | custom-call | flops 1048576 | bytes 1024 | tf_op jit(solution)/shard_map/pallas_call | solution.py:61
  88.5 2.5 multiply_reduce_fusion
  93.2 12.6 %all-gather.2.cloned.1.call-done.win_ref.wout_ref = bf16[768,6144]{1,0:T(8,128)(2,1)} async-done(((bf16[24,6144]{1,0:T(8,128)(2,1)}), bf16[768,6144]{1,0:T(8,128)(2,1)}) %all-gather.2.cloned.1.call-update) | async-done | bytes 9437200 | tf_op jit(solution)/shard_map/all_gather | solution.py:532
  105.7 26.2 %shard_map.204 = (bf16[512,768]{1,0:T(8,128)(2,1)}, f32[512,768]{1,0:T(8,128)}, bf16[512,768]{1,0:T(8,128)(2,1)}, bf16[512,768]{1,0:T(8,128)(2,1)}, bf16[2,2,4,9...) custom-call(s32[4]{0:T(128)} %pad_add_fusion.seat_ref, ...), custom_call_target="tpu_custom_call" | custom-call | flops 1048576 | bytes 1024 | tf_op jit(solution)/shard_map/pallas_call | solution.py:252
  136.2 6.2 %shard_map.205 = (bf16[512,256]{1,0:T(8,128)(2,1)S(1)}, bf16[512,256]{1,0:T(8,128)(2,1)S(1)}, bf16[512,256]{1,0:T(8,128)(2,1)S(1)}, f32[2,2,1024]{2,1,0:T(2,128)S(1)}) custom-call(bf16[512,1536]{1,0:T(8,128)(2,1)S(1)} %convolution_convert_fusion.q_ref.k_ref, bf16[512,1536]{1,0:T(8,128)(2,1)S(1)} %convolution_convert_fusion.q_ref.k_ref, ...), custom_call_target="tpu_custom_call" | custom-call | flops 1048576 | bytes 1024 | tf_op jit(solution)/shard_map/pallas_call | solution.py:99
  142.5 2.7 %fusion.8 = bf16[2,4,96,768]{3,2,1,0:T(8,128)(2,1)} fusion(bf16[2,2,4,96,768]{4,3,2,1,0:T(8,128)(2,1)} %collective-permute-done.10, bf16[2,2,4,96,768]{4,3,2,1,0:T(8,128)(2,1)S(1)} %copy-done.13), kind=kLoop, calls=%fused_computation.25 | loop fusion | flops 2359296 | bytes 3538944 | tf_op jit(solution)/shard_map/convert_element_type | solution.py:486
  145.2 2.7 %fusion.9 = bf16[2,4,96,768]{3,2,1,0:T(8,128)(2,1)} fusion(bf16[2,2,4,96,768]{4,3,2,1,0:T(8,128)(2,1)S(1)} %copy-done.11, bf16[2,2,4,96,768]{4,3,2,1,0:T(8,128)(2,1)} %collective-permute-done.11), kind=kLoop, calls=%fused_computation.26 | loop fusion | flops 2359296 | bytes 3538944 | tf_op jit(solution)/shard_map/convert_element_type | solution.py:486
  151.0 12.5 %shard_map.206 = (bf16[512,512]{1,0:T(8,128)(2,1)S(1)}, bf16[512,512]{1,0:T(8,128)(2,1)S(1)}, bf16[512,512]{1,0:T(8,128)(2,1)S(1)}, f32[4,2,1024]{2,1,0:T(2,128)S(1)}) custom-call(bf16[512,1536]{1,0:T(8,128)(2,1)S(1)} %convolution_convert_fusion.q_ref.k_ref, bf16[512,1536]{1,0:T(8,128)(2,1)S(1)} %convolution_convert_fusion.q_ref.k_ref, ...), custom_call_target="tpu_custom_call" | custom-call | flops 1048576 | bytes 1024 | tf_op jit(solution)/shard_map/pallas_call | solution.py:99
  165.0 8.4 %shard_map.207 = (bf16[2,2,4,48,768]{4,3,2,1,0:T(8,128)(2,1)}, bf16[2,2,4,48,768]{4,3,2,1,0:T(8,128)(2,1)}, bf16[2,2,4,48,768]{4,3,2,1,0:T(8,128)(2,1)}, bf16[2,2,4,48,768]{4,3,2,1,0:T(8,128)(2,1)}) custom-call(s32[4]{0:T(128)} %pad_add_fusion.seat_ref, bf16[512,768]{1,0:T(8,128)(2,1)} %copy-done.10, bf16[768,512]{1,0:T(8,128)(2,1)} %copy-done.1, ...), custom_call_target="tpu_custom_call" | custom-call | flops 1048576 | bytes 1024 | tf_op jit(solution)/shard_map/pallas_call | solution.py:302
  174.0 2.1 collective-permute-done.15
  176.3 2.5 fusion.15
  178.8 2.3 fusion.14
  193.0 2.4 fusion.7
  195.9 4.7 %collective-permute-done.20 = bf16[4,96,768]{2,1,0:T(8,128)(2,1)S(1)} collective-permute-done((bf16[4,96,768]{2,1,0:T(8,128)(2,1)}, bf16[4,96,768]{2,1,0:T(8,128)(2,1)S(1)}, u32[]{:S(2)}, u32[]{:S(2)}) %collective-permute-start.20) | collective-permute-done | bytes 589856 | tf_op jit(solution)/shard_map/ppermute | solution.py:364
  206.1 7.6 %collective-permute-done.18 = bf16[2,4,48,768]{3,2,1,0:T(8,128)(2,1)S(1)} collective-permute-done((bf16[2,4,48,768]{3,2,1,0:T(8,128)(2,1)S(1)}, bf16[2,4,48,768]{3,2,1,0:T(8,128)(2,1)S(1)}, u32[]{:S(2)}, u32[]{:S(2)}) %collective-permute-start.18) | collective-permute-done | bytes 589856 | tf_op jit(solution)/shard_map/ppermute | solution.py:364
  222.1 2.0 collective-permute-start.28
  224.1 2.9 %collective-permute-done.23 = bf16[4,48,768]{2,1,0:T(8,128)(2,1)S(1)} collective-permute-done((bf16[4,48,768]{2,1,0:T(8,128)(2,1)S(1)}, bf16[4,48,768]{2,1,0:T(8,128)(2,1)S(1)}, u32[]{:S(2)}, u32[]{:S(2)}) %collective-permute-start.23) | collective-permute-done | bytes 294944 | tf_op jit(solution)/shard_map/ppermute | solution.py:364
  231.3 2.6 %collective-permute-done.22 = bf16[256,768]{1,0:T(8,128)(2,1)S(1)} collective-permute-done((bf16[256,768]{1,0:T(8,128)(2,1)S(1)}, bf16[256,768]{1,0:T(8,128)(2,1)S(1)}, u32[]{:S(2)}, u32[]{:S(2)}) %collective-permute-start.22) | collective-permute-done | bytes 393248 | tf_op jit(solution)/shard_map/ppermute | solution.py:348
  235.1 2.0 collective-permute-done.28
  237.5 1.8 convert_add_fusion.7
  239.3 3.6 %collective-permute-done.25 = bf16[2,104,768]{2,1,0:T(8,128)(2,1)S(1)} collective-permute-done((bf16[2,104,768]{2,1,0:T(8,128)(2,1)S(1)}, bf16[2,104,768]{2,1,0:T(8,128)(2,1)S(1)}, u32[]{:S(2)}, u32[]{:S(2)}) %collective-permute-start.25) | collective-permute-done | bytes 319520 | tf_op jit(solution)/shard_map/ppermute | solution.py:364
  244.6 8.1 %collective-permute-done.26 = bf16[1,104,768]{2,1,0:T(8,128)(2,1)S(1)} collective-permute-done((bf16[1,104,768]{2,1,0:T(8,128)(2,1)S(1)}, bf16[1,104,768]{2,1,0:T(8,128)(2,1)S(1)}, u32[]{:S(2)}, u32[]{:S(2)}) %collective-permute-start.26) | collective-permute-done | bytes 159776 | tf_op jit(solution)/shard_map/ppermute | solution.py:364
  (240 shorter events, 71.4 us)
Async XLA Ops:
  7.2 98.5 %all-gather.2.cloned.1.call-start = ((), (), s32[]{:S(2)}) async-start(), calls=%async_computation | async-start | bytes 9732096 | tf_op jit(solution)/shard_map/all_gather | solution.py:532
  12.7 19.9 %collective-permute-start.2 = (bf16[24,3200]{1,0:T(8,128)(2,1)S(1)}, bf16[24,3200]{1,0:T(8,128)(2,1)S(1)}, u32[]{:S(2)}, u32[]{:S(2)}) collective-permute-start(bf16[24,3200]{1,0:T(8,128)(2,1)S(1)} %constant_dynamic-update-slice_fusion), channel_id=1, source_target_pairs={{0,16},{1,17},{2,18},{3,19},{4,20},{5,21},{6,22},{7,23},{8,24},{9,... | collective-permute-start | bytes 460808 | tf_op jit(solution)/shard_map/ppermute | solution.py:364
  16.8 15.8 %collective-permute-start.3 = (bf16[24,3200]{1,0:T(8,128)(2,1)S(1)}, bf16[24,3200]{1,0:T(8,128)(2,1)}, u32[]{:S(2)}, u32[]{:S(2)}) collective-permute-start(bf16[24,3200]{1,0:T(8,128)(2,1)S(1)} %constant_dynamic-update-slice_fusion), channel_id=1, source_target_pairs={{0,24},{1,25},{2,26},{3,27},{4,28},{5,29},{6,30},{7,31},{8,16},{9,... | collective-permute-start | bytes 460808 | tf_op jit(solution)/shard_map/ppermute | solution.py:364
  18.2 13.5 %collective-permute-start.1 = (bf16[24,3200]{1,0:T(8,128)(2,1)S(1)}, bf16[24,3200]{1,0:T(8,128)(2,1)}, u32[]{:S(2)}, u32[]{:S(2)}) collective-permute-start(bf16[24,3200]{1,0:T(8,128)(2,1)S(1)} %constant_dynamic-update-slice_fusion), channel_id=1, source_target_pairs={{0,8},{1,9},{2,10},{3,11},{4,12},{5,13},{6,14},{7,15},{8,0},{9,1},... | collective-permute-start | bytes 460808 | tf_op jit(solution)/shard_map/ppermute | solution.py:364
  18.5 50.8 %collective-permute-start = (bf16[2,256,768]{2,1,0:T(8,128)(2,1)S(1)}, bf16[2,256,768]{2,1,0:T(8,128)(2,1)S(1)}, u32[]{:S(2)}, u32[]{:S(2)}) collective-permute-start(bf16[2,256,768]{2,1,0:T(8,128)(2,1)S(1)} %pad_maximum_fusion.4), channel_id=1, source_target_pairs={{0,1},{1,0},{2,3},{3,2},{4,5},{5,4},{6,7},{7,6},{8,9},{9,8},{10,11... | collective-permute-start | bytes 2359304 | tf_op jit(solution)/shard_map/ppermute | solution.py:337
  33.7 6.8 %collective-permute-start.7 = (bf16[2,2,24,1536]{3,2,1,0:T(8,128)(2,1)S(1)}, bf16[2,2,24,1536]{3,2,1,0:T(8,128)(2,1)S(1)}, u32[]{:S(2)}, u32[]{:S(2)}) collective-permute-start(bf16[2,2,24,1536]{3,2,1,0:T(8,128)(2,1)S(1)} %pad_maximum_fusion.15), channel_id=1, source_target_pairs={{0,4},{1,5},{2,6},{3,7},{4,0},{5,1},{6,2},{7,3},{8,12},{9,13},{10,... | collective-permute-start | bytes 884744 | tf_op jit(solution)/shard_map/ppermute | solution.py:364
  36.1 13.2 %collective-permute-start.4 = (bf16[2,2,24,1664]{3,2,1,0:T(8,128)(2,1)S(1)}, bf16[2,2,24,1664]{3,2,1,0:T(8,128)(2,1)S(1)}, u32[]{:S(2)}, u32[]{:S(2)}) collective-permute-start(bf16[2,2,24,1664]{3,2,1,0:T(8,128)(2,1)S(1)} %fusion.26), channel_id=1, source_target_pairs={{0,1},{1,0},{2,3},{3,2},{4,5},{5,4},{6,7},{7,6},{8,9},{9,8},{10,11... | collective-permute-start | bytes 958472 | tf_op jit(solution)/shard_map/ppermute | solution.py:364
  40.7 22.4 %collective-permute-start.8 = (bf16[2,2,2,24,1536]{4,3,2,1,0:T(8,128)(2,1)S(1)}, bf16[2,2,2,24,1536]{4,3,2,1,0:T(8,128)(2,1)S(1)}, u32[]{:S(2)}, u32[]{:S(2)}) collective-permute-start(bf16[2,2,2,24,1536]{4,3,2,1,0:T(8,128)(2,1)S(1)} %pad_maximum_fusion.9), channel_id=1, source_target_pairs={{0,1},{1,0},{2,3},{3,2},{4,5},{5,4},{6,7},{7,6},{8,9},{9,8},{10,11... | collective-permute-start | bytes 1769480 | tf_op jit(solution)/shard_map/ppermute | solution.py:364
  49.5 19.5 %collective-permute-start.5 = (bf16[2,2,2,24,1664]{4,3,1,0,2:T(8,128)(2,1)S(1)}, bf16[2,2,2,24,1664]{4,3,1,0,2:T(8,128)(2,1)S(1)}, u32[]{:S(2)}, u32[]{:S(2)}) collective-permute-start(bf16[2,2,2,24,1664]{4,3,1,0,2:T(8,128)(2,1)S(1)} %pad_maximum_fusion.8), channel_id=1, source_target_pairs={{0,4},{1,5},{2,6},{3,7},{4,0},{5,1},{6,2},{7,3},{8,12},{9,13},{10,... | collective-permute-start | bytes 1916936 | tf_op jit(solution)/shard_map/ppermute | solution.py:364
  63.3 7.3 %collective-permute-start.9 = (bf16[2,2,2,2,24,1536]{5,4,3,2,1,0:T(8,128)(2,1)S(1)}, bf16[2,2,2,2,24,1536]{5,4,3,2,1,0:T(8,128)(2,1)S(1)}, u32[]{:S(2)}, u32[]{:S(2)}) collective-permute-start(bf16[2,2,2,2,24,1536]{5,4,3,2,1,0:T(8,128)(2,1)S(1)} %pad_maximum_fusion.3), channel_id=1, source_target_pairs={{0,2},{1,3},{2,0},{3,1},{4,6},{5,7},{6,4},{7,5},{8,10},{9,11},{10,... | collective-permute-start | bytes 3538952 | tf_op jit(solution)/shard_map/ppermute | solution.py:364
  69.3 3.2 %collective-permute-start.6 = (bf16[2,2,2,2,24,1664]{5,4,1,0,3,2:T(8,128)(2,1)S(1)}, bf16[2,2,2,2,24,1664]{5,4,1,0,3,2:T(8,128)(2,1)S(1)}, u32[]{:S(2)}, u32[]{:S(2)}) collective-permute-start(bf16[2,2,2,2,24,1664]{5,4,1,0,3,2:T(8,128)(2,1)S(1)} %pad_maximum_fusion.2), channel_id=1, source_target_pairs={{0,2},{1,3},{2,0},{3,1},{4,6},{5,7},{6,4},{7,5},{8,10},{9,11},{10,... | collective-permute-start | bytes 3833864 | tf_op jit(solution)/shard_map/ppermute | solution.py:364
  131.9 10.5 %collective-permute-start.10 = (bf16[2,2,4,96,768]{4,3,2,1,0:T(8,128)(2,1)}, bf16[2,2,4,96,768]{4,3,2,1,0:T(8,128)(2,1)}, u32[]{:S(2)}, u32[]{:S(2)}) collective-permute-start(bf16[2,2,4,96,768]{4,3,2,1,0:T(8,128)(2,1)} %get-tuple-element.103), channel_id=1, source_target_pairs={{0,2},{1,3},{2,0},{3,1},{4,6},{5,7},{6,4},{7,5},{8,10},{9,11},{10,... | collective-permute-start | bytes 7077896 | tf_op jit(solution)/shard_map/ppermute | solution.py:364
  132.2 10.2 %collective-permute-start.11 = (bf16[2,2,4,96,768]{4,3,2,1,0:T(8,128)(2,1)}, bf16[2,2,4,96,768]{4,3,2,1,0:T(8,128)(2,1)}, u32[]{:S(2)}, u32[]{:S(2)}) collective-permute-start(bf16[2,2,4,96,768]{4,3,2,1,0:T(8,128)(2,1)} %get-tuple-element.104), channel_id=1, source_target_pairs={{0,2},{1,3},{2,0},{3,1},{4,6},{5,7},{6,4},{7,5},{8,10},{9,11},{10,... | collective-permute-start | bytes 7077896 | tf_op jit(solution)/shard_map/ppermute | solution.py:364
  133.5 16.4 %collective-permute-start.12 = (bf16[256,768]{1,0:T(8,128)(2,1)S(1)}, bf16[256,768]{1,0:T(8,128)(2,1)S(1)}, u32[]{:S(2)}, u32[]{:S(2)}) collective-permute-start(bf16[256,768]{1,0:T(8,128)(2,1)S(1)} %constant_dynamic-slice_fusion.1), channel_id=1, source_target_pairs={{0,1},{1,0},{2,3},{3,2},{4,5},{5,4},{6,7},{7,6},{8,9},{9,8},{10,11... | collective-permute-start | bytes 1179656 | tf_op jit(solution)/shard_map/ppermute | solution.py:348
  147.9 28.2 %collective-permute-start.15 = (bf16[2,4,96,768]{3,2,1,0:T(8,128)(2,1)}, bf16[2,4,96,768]{3,2,1,0:T(8,128)(2,1)}, u32[]{:S(2)}, u32[]{:S(2)}) collective-permute-start(bf16[2,4,96,768]{3,2,1,0:T(8,128)(2,1)} %fusion.8), channel_id=1, source_target_pairs={{0,4},{1,5},{2,6},{3,7},{4,0},{5,1},{6,2},{7,3},{8,12},{9,13},{10,... | collective-permute-start | bytes 3538952 | tf_op jit(solution)/shard_map/ppermute | solution.py:364
  148.4 27.9 %collective-permute-start.16 = (bf16[2,4,96,768]{3,2,1,0:T(8,128)(2,1)}, bf16[2,4,96,768]{3,2,1,0:T(8,128)(2,1)}, u32[]{:S(2)}, u32[]{:S(2)}) collective-permute-start(bf16[2,4,96,768]{3,2,1,0:T(8,128)(2,1)} %fusion.9), channel_id=1, source_target_pairs={{0,1},{1,0},{2,3},{3,2},{4,5},{5,4},{6,7},{7,6},{8,9},{9,8},{10,11... | collective-permute-start | bytes 3538952 | tf_op jit(solution)/shard_map/ppermute | solution.py:364
  173.4 12.8 %collective-permute-start.13 = (bf16[2,2,4,48,768]{4,3,2,1,0:T(8,128)(2,1)}, bf16[2,2,4,48,768]{4,3,2,1,0:T(8,128)(2,1)}, u32[]{:S(2)}, u32[]{:S(2)}) collective-permute-start(bf16[2,2,4,48,768]{4,3,2,1,0:T(8,128)(2,1)} %get-tuple-element.139), channel_id=1, source_target_pairs={{0,2},{1,3},{2,0},{3,1},{4,6},{5,7},{6,4},{7,5},{8,10},{9,11},{10,... | collective-permute-start | bytes 3538952 | tf_op jit(solution)/shard_map/ppermute | solution.py:364
  173.5 12.7 %collective-permute-start.14 = (bf16[2,2,4,48,768]{4,3,2,1,0:T(8,128)(2,1)}, bf16[2,2,4,48,768]{4,3,2,1,0:T(8,128)(2,1)}, u32[]{:S(2)}, u32[]{:S(2)}) collective-permute-start(bf16[2,2,4,48,768]{4,3,2,1,0:T(8,128)(2,1)} %get-tuple-element.140), channel_id=1, source_target_pairs={{0,2},{1,3},{2,0},{3,1},{4,6},{5,7},{6,4},{7,5},{8,10},{9,11},{10,... | collective-permute-start | bytes 3538952 | tf_op jit(solution)/shard_map/ppermute | solution.py:364
  182.0 4.3 %collective-permute-start.17 = (bf16[2,2,4,8,768]{4,3,2,1,0:T(8,128)(2,1)S(1)}, bf16[2,2,4,8,768]{4,3,2,1,0:T(8,128)(2,1)S(1)}, u32[]{:S(2)}, u32[]{:S(2)}) collective-permute-start(bf16[2,2,4,8,768]{4,3,2,1,0:T(8,128)(2,1)S(1)} %broadcast_in_dim.38), channel_id=1, source_target_pairs={{0,2},{1,3},{2,0},{3,1},{4,6},{5,7},{6,4},{7,5},{8,10},{9,11},{10,... | collective-permute-start | bytes 589832 | tf_op jit(solution)/shard_map/ppermute | solution.py:364
  184.1 16.4 %collective-permute-start.20 = (bf16[4,96,768]{2,1,0:T(8,128)(2,1)}, bf16[4,96,768]{2,1,0:T(8,128)(2,1)S(1)}, u32[]{:S(2)}, u32[]{:S(2)}) collective-permute-start(bf16[4,96,768]{2,1,0:T(8,128)(2,1)} %fusion.15), channel_id=1, source_target_pairs={{0,1},{1,0},{2,3},{3,2},{4,5},{5,4},{6,7},{7,6},{8,9},{9,8},{10,11... | collective-permute-start | bytes 1769480 | tf_op jit(solution)/shard_map/ppermute | solution.py:364
  185.6 16.4 %collective-permute-start.21 = (bf16[4,96,768]{2,1,0:T(8,128)(2,1)}, bf16[4,96,768]{2,1,0:T(8,128)(2,1)S(1)}, u32[]{:S(2)}, u32[]{:S(2)}) collective-permute-start(bf16[4,96,768]{2,1,0:T(8,128)(2,1)} %fusion.14), channel_id=1, source_target_pairs={{0,4},{1,5},{2,6},{3,7},{4,0},{5,1},{6,2},{7,3},{8,12},{9,13},{10,... | collective-permute-start | bytes 1769480 | tf_op jit(solution)/shard_map/ppermute | solution.py:364
  189.0 24.8 %collective-permute-start.18 = (bf16[2,4,48,768]{3,2,1,0:T(8,128)(2,1)S(1)}, bf16[2,4,48,768]{3,2,1,0:T(8,128)(2,1)S(1)}, u32[]{:S(2)}, u32[]{:S(2)}) collective-permute-start(bf16[2,4,48,768]{3,2,1,0:T(8,128)(2,1)S(1)} %fusion.18), channel_id=1, source_target_pairs={{0,4},{1,5},{2,6},{3,7},{4,0},{5,1},{6,2},{7,3},{8,12},{9,13},{10,... | collective-permute-start | bytes 1769480 | tf_op jit(solution)/shard_map/ppermute | solution.py:364
  190.4 24.3 %collective-permute-start.19 = (bf16[2,4,56,768]{3,2,1,0:T(8,128)(2,1)S(1)}, bf16[2,4,56,768]{3,2,1,0:T(8,128)(2,1)S(1)}, u32[]{:S(2)}, u32[]{:S(2)}) collective-permute-start(bf16[2,4,56,768]{3,2,1,0:T(8,128)(2,1)S(1)} %pad_maximum_fusion.7), channel_id=1, source_target_pairs={{0,1},{1,0},{2,3},{3,2},{4,5},{5,4},{6,7},{7,6},{8,9},{9,8},{10,11... | collective-permute-start | bytes 2064392 | tf_op jit(solution)/shard_map/ppermute | solution.py:364
  200.6 20.1 %copy-start.27 = (bf16[4,96,768]{2,1,0:T(8,128)(2,1)}, bf16[4,96,768]{2,1,0:T(8,128)(2,1)S(1)}, u32[]{:S(2)}) copy-start(bf16[4,96,768]{2,1,0:T(8,128)(2,1)S(1)} %collective-permute-done.20) | copy-start | bytes 1769476
  204.5 16.1 %collective-permute-start.27 = (bf16[2,192,768]{2,1,0:T(8,128)(2,1)S(1)}, bf16[2,192,768]{2,1,0:T(8,128)(2,1)S(1)}, u32[]{:S(2)}, u32[]{:S(2)}) collective-permute-start(bf16[2,192,768]{2,1,0:T(8,128)(2,1)S(1)} %pad_maximum_fusion.10), channel_id=1, source_target_pairs={{0,8},{1,9},{2,10},{3,11},{4,12},{5,13},{6,14},{7,15},{8,0},{9,1},... | collective-permute-start | bytes 1769480 | tf_op jit(solution)/shard_map/ppermute | solution.py:364
  217.0 10.0 %collective-permute-start.23 = (bf16[4,48,768]{2,1,0:T(8,128)(2,1)S(1)}, bf16[4,48,768]{2,1,0:T(8,128)(2,1)S(1)}, u32[]{:S(2)}, u32[]{:S(2)}) collective-permute-start(bf16[4,48,768]{2,1,0:T(8,128)(2,1)S(1)} %fusion.21), channel_id=1, source_target_pairs={{0,1},{1,0},{2,3},{3,2},{4,5},{5,4},{6,7},{7,6},{8,9},{9,8},{10,11... | collective-permute-start | bytes 884744 | tf_op jit(solution)/shard_map/ppermute | solution.py:364
  218.4 9.2 %collective-permute-start.24 = (bf16[4,56,768]{2,1,0:T(8,128)(2,1)S(1)}, bf16[4,56,768]{2,1,0:T(8,128)(2,1)S(1)}, u32[]{:S(2)}, u32[]{:S(2)}) collective-permute-start(bf16[4,56,768]{2,1,0:T(8,128)(2,1)S(1)} %pad_maximum_fusion.11), channel_id=1, source_target_pairs={{0,4},{1,5},{2,6},{3,7},{4,0},{5,1},{6,2},{7,3},{8,12},{9,13},{10,... | collective-permute-start | bytes 1032200 | tf_op jit(solution)/shard_map/ppermute | solution.py:364
  219.1 14.9 %collective-permute-start.22 = (bf16[256,768]{1,0:T(8,128)(2,1)S(1)}, bf16[256,768]{1,0:T(8,128)(2,1)S(1)}, u32[]{:S(2)}, u32[]{:S(2)}) collective-permute-start(bf16[256,768]{1,0:T(8,128)(2,1)S(1)} %constant_dynamic-slice_fusion), channel_id=1, source_target_pairs={{0,1},{1,0},{2,3},{3,2},{4,5},{5,4},{6,7},{7,6},{8,9},{9,8},{10,11... | collective-permute-start | bytes 1179656 | tf_op jit(solution)/shard_map/ppermute | solution.py:348
  222.1 15.0 %collective-permute-start.28 = (bf16[1,192,768]{2,1,0:T(8,128)(2,1)S(1)}, bf16[1,192,768]{2,1,0:T(8,128)(2,1)S(1)}, u32[]{:S(2)}, u32[]{:S(2)}) collective-permute-start(bf16[1,192,768]{2,1,0:T(8,128)(2,1)S(1)} %pad_maximum_fusion.17), channel_id=1, source_target_pairs={{0,16},{1,17},{2,18},{3,19},{4,20},{5,21},{6,22},{7,23},{8,24},{9,... | collective-permute-start | bytes 884744 | tf_op jit(solution)/shard_map/ppermute | solution.py:364
  229.7 13.2 %collective-permute-start.25 = (bf16[2,104,768]{2,1,0:T(8,128)(2,1)S(1)}, bf16[2,104,768]{2,1,0:T(8,128)(2,1)S(1)}, u32[]{:S(2)}, u32[]{:S(2)}) collective-permute-start(bf16[2,104,768]{2,1,0:T(8,128)(2,1)S(1)} %pad_maximum_fusion.12), channel_id=1, source_target_pairs={{0,8},{1,9},{2,10},{3,11},{4,12},{5,13},{6,14},{7,15},{8,0},{9,1},... | collective-permute-start | bytes 958472 | tf_op jit(solution)/shard_map/ppermute | solution.py:364
  237.3 16.6 %copy-start.23 = (f32[4,3,8,768]{3,2,0,1:T(8,128)}, f32[4,3,8,768]{3,2,0,1:T(8,128)S(1)}, u32[]{:S(2)}) copy-start(f32[4,3,8,768]{3,2,0,1:T(8,128)S(1)} %copy.96) | copy-start | bytes 884740
  244.0 8.7 %collective-permute-start.26 = (bf16[1,104,768]{2,1,0:T(8,128)(2,1)S(1)}, bf16[1,104,768]{2,1,0:T(8,128)(2,1)S(1)}, u32[]{:S(2)}, u32[]{:S(2)}) collective-permute-start(bf16[1,104,768]{2,1,0:T(8,128)(2,1)S(1)} %pad_maximum_fusion.18), channel_id=1, source_target_pairs={{0,16},{1,17},{2,18},{3,19},{4,20},{5,21},{6,22},{7,23},{8,24},{9,... | collective-permute-start | bytes 479240 | tf_op jit(solution)/shard_map/ppermute | solution.py:364
  (37 other events, 196.4 us)
Sparse Core Ops, SparseCore 0:
  11.6 94.1 all-gather.1

commit v5 on v4

--- a/solution.py
+++ b/solution.py
@@ -341,14 +341,15 @@
     ]
 
 
-def split_sequence(array, half):
-    rows = array.shape[0] // 2
-    mine = lax.dynamic_slice_in_dim(array, half * rows, rows, 0)
-    other = lax.dynamic_slice_in_dim(array, (1 - half) * rows, rows, 0)
-    received = lax.ppermute(other, "seq", [(0, 1), (1, 0)])
-    first = jnp.where(half == 0, mine, received)
-    second = jnp.where(half == 0, received, mine)
-    return jnp.stack([first, second])[:, None]
+def split_sequences(arrays, half):
+    rows = arrays[0].shape[0] // 2
+    mine = [lax.dynamic_slice_in_dim(a, half * rows, rows, 0) for a in arrays]
+    other = [lax.dynamic_slice_in_dim(a, (1 - half) * rows, rows, 0) for a in arrays]
+    received = lax.ppermute(jnp.stack(other), "seq", [(0, 1), (1, 0)])
+    return [
+        jnp.stack([jnp.where(half == 0, a, b), jnp.where(half == 0, b, a)])[:, None]
+        for a, b in zip(mine, received)
+    ]
 
 
 def bf16_parts(values, count):
@@ -580,12 +581,10 @@
     big = Scatter(ranks, d_ffn, [[(2, [0]), (0, [1])], [(0, [0]), (2, [1])]])
     big.send()
 
-    layer_out = split_sequence(layer_low, half)
     each = head_pairs // 3
     piece_0 = attend_back(qk, v, grad_attended, lse, bias_rows, 0, each)
     piece_0, grad_attended = big.advance((piece_0, grad_attended))
     piece_1 = attend_back(qk, v, grad_attended, lse, bias_rows, each, head_pairs - each)
-    piece_1, layer_out = together(piece_1, layer_out)
     d_vec = jnp.concatenate([piece_0[3], piece_1[3]])
     grads = [jnp.concatenate([piece_0[at], piece_1[at]], axis=1) for at in range(3)]
     small = Scatter(
@@ -602,10 +601,11 @@
         precision=lax.Precision.HIGHEST,
         preferred_element_type=f32,
     )
-    extra = jnp.concatenate(bf16_parts(d_table.reshape(2, bias_table.size), 2), axis=1)
+    extra = bf16_parts(d_table.reshape((2,) + bias_table.shape), 2)
+    extra = jnp.concatenate(extra, axis=2)
     extra = jnp.where(half == 0, extra, extra[::-1])
-    extra = jnp.pad(extra[None, :, None, None], ((0, 0),) * 4 + ((0, width - 2 * bias_table.size),))
-    extra = jnp.broadcast_to(extra, (2, 2, devices // 8, 8, width))
+    extra = jnp.pad(extra, ((0, 0), (0, 8 - extra.shape[1]), (0, width - extra.shape[2])))
+    extra = jnp.broadcast_to(extra[None, :, None], (2, 2, devices // 8, 8, width))
     small.join(extra, extra)
     grads = small.advance(grads)
     grad_attn_in = sum(dot_nt(grad, w) for grad, w in zip(grads, w_parts))
@@ -613,7 +613,7 @@
     token_low = (grad_inputs + grad_middle).astype(bf16)
     token_low = big.advance(token_low)
     token_low = small.advance(token_low)
-    grad_tokens = split_sequence(token_low, half)
+    layer_out, grad_tokens = split_sequences([layer_low, token_low], half)
     while not (big.done() and small.done()):
         for scatter in (big, small):
             if not scatter.done():
@@ -626,7 +626,8 @@
         jnp.sum(w.astype(f32) * d, axis=1) for w, d in zip((w_query, w_key, w_value), d_w)
     ) / gain_attn.astype(f32)
     own_gain_ffn = jnp.sum(w_in.astype(f32) * own_w_in, axis=1) / gain_ffn.astype(f32)
-    own_table = rest[0, : bias_table.size] + rest[0, bias_table.size : 2 * bias_table.size]
+    heads, buckets_count = bias_table.shape
+    own_table = rest[:heads, :buckets_count] + rest[:heads, buckets_count : 2 * buckets_count]
     return (
         layer_out,
         grad_tokens,
@@ -638,7 +639,7 @@
         own_w_out,
         own_gain_attn,
         own_gain_ffn,
-        own_table.reshape(bias_table.shape),
+        own_table,
     )
 
 

time: 264 us -> 263 us (level)
  starting transfers between devices: 32.9 us -> 30 us
    ppermute x2 -> x1, waiting for transfers between devices: 2.65 us -> 0.01 us  [split_sequences(): received = lax.ppermute(jnp.stack(other), 'seq', [(0, 1), (1, 0)])]
    unnamed x86 -> x102, local copies, waits for them, and re-layouts: 5.4 us -> 5.43 us
  transfers between devices with their start and end apart: 30 -> 29, of which waited for: 18 -> 18; matrix products, arithmetic and copies ran while one was open for 20% -> 20% of each run, Pallas kernels for 14% -> 14%
where the time goes in v5:
time: 263 us; the launch traced here: 262 us
  waiting for transfers between devices  86.1 us (33%)
  Pallas kernels  62.4 us (24%)
  other arithmetic  45.1 us (17%)
  starting transfers between devices  30 us (11%)
  between operations  15.1 us (6%)
  local copies, waits for them, and re-layouts  14.2 us (5%)
  matrix products  9 us (3%)
    ppermute x26, waiting for transfers between devices, partner_sends(): lax.ppermute(array, ('rows', 'seq'), [(b, b ^ mask) for b in range(device...  74.1 us
    ppermute x26, starting transfers between devices, partner_sends(): lax.ppermute(array, ('rows', 'seq'), [(b, b ^ mask) for b in range(device...  27.7 us
    pallas_call x1, Pallas kernels, ffn(): pl.pallas_call(ffn_kernel, grid_spec=pltpu.PrefetchScalarGridSpec(num_sca...  26.3 us
    pallas_call x2, Pallas kernels, attend_back(): pl.pallas_call(attend_back_kernel, grid=(count,), in_specs=[spec(start),...  18.7 us
    convert_element_type x6, other arithmetic, prepare(): self.outgoing.append(total.astype(jnp.bfloat16))  12.7 us
    all_gather x1, waiting for transfers between devices, shards(): lax.all_gather(jnp.concatenate([w_in, groups], axis=1), ('rows', 'seq'),...  12 us
    pallas_call x1, Pallas kernels, attend(): pl.pallas_call(attend_kernel, grid=(steps,), in_specs=[spec(0), spec(step...  8.92 us
    pallas_call x1, Pallas kernels, weight_grads(): pl.pallas_call(kernel, grid_spec=pltpu.PrefetchScalarGridSpec(num_scalar_...  8.45 us
  transfers between devices with their start and end apart: 29, of which 18 were waited for; matrix products, arithmetic and copies ran while one was open for 20% of the time, Pallas kernels for 14%

profile of v5, /device:TPU:0, one launch (start us, length us, event | category | flops | bytes accessed | tf_op | source)
XLA Modules:
  0.0 261.9 jit_solution(66953651297058961)
XLA Ops:
  8.4 1.6 pad_maximum_fusion.17
  12.7 4.1 %collective-permute-start.2 = (bf16[24,3200]{1,0:T(8,128)(2,1)S(1)}, bf16[24,3200]{1,0:T(8,128)(2,1)S(1)}, u32[]{:S(2)}, u32[]{:S(2)}) collective-permute-start(bf16[24,3200]{1,0:T(8,128)(2,1)S(1)} %constant_dynamic-update-slice_fusion), channel_id=1, source_target_pairs={{0,16},{1,17},{2,18},{3,19},{4,20},{5,21},{6,22},{7,23},{8,24},{9,... | collective-permute-start | bytes 460808 | tf_op jit(solution)/shard_map/ppermute | solution.py:365
  20.4 11.3 %collective-permute-done.1 = bf16[24,3200]{1,0:T(8,128)(2,1)} collective-permute-done((bf16[24,3200]{1,0:T(8,128)(2,1)S(1)}, bf16[24,3200]{1,0:T(8,128)(2,1)}, u32[]{:S(2)}, u32[]{:S(2)}) %collective-permute-start.1) | collective-permute-done | bytes 153632 | tf_op jit(solution)/shard_map/ppermute | solution.py:365
  33.7 1.8 collective-permute-start.7
  36.1 2.2 collective-permute-start.4
  38.3 2.2 collective-permute-done.7
  40.7 2.4 collective-permute-start.8
  43.1 6.3 %collective-permute-done.4 = bf16[2,2,24,1664]{3,2,1,0:T(8,128)(2,1)S(1)} collective-permute-done((bf16[2,2,24,1664]{3,2,1,0:T(8,128)(2,1)S(1)}, bf16[2,2,24,1664]{3,2,1,0:T(8,128)(2,1)S(1)}, u32[]{:S(2)}, u32[]{:S(2)}) %collective-permute-start.4) | collective-permute-done | bytes 319520 | tf_op jit(solution)/shard_map/ppermute | solution.py:365
  50.9 12.3 %collective-permute-done.8 = bf16[2,2,2,24,1536]{4,3,2,1,0:T(8,128)(2,1)S(1)} collective-permute-done((bf16[2,2,2,24,1536]{4,3,2,1,0:T(8,128)(2,1)S(1)}, bf16[2,2,2,24,1536]{4,3,2,1,0:T(8,128)(2,1)S(1)}, u32[]{:S(2)}, u32[]{:S(2)}) %collective-permute-start.8) | collective-permute-done | bytes 589856 | tf_op jit(solution)/shard_map/ppermute | solution.py:365
  63.4 5.6 %collective-permute-done.5 = bf16[2,2,2,24,1664]{4,3,1,0,2:T(8,128)(2,1)S(1)} collective-permute-done((bf16[2,2,2,24,1664]{4,3,1,0,2:T(8,128)(2,1)S(1)}, bf16[2,2,2,24,1664]{4,3,1,0,2:T(8,128)(2,1)S(1)}, u32[]{:S(2)}, u32[]{:S(2)}) %collective-permute-start.5) | collective-permute-done | bytes 639008 | tf_op jit(solution)/shard_map/ppermute | solution.py:365
  71.4 1.6 pad_maximum_fusion.1
  80.1 8.9 %shard_map.203 = (bf16[512,768]{1,0:T(8,128)(2,1)S(1)}, bf16[768,512]{1,0:T(8,128)(2,1)S(1)}, f32[6,2,512]{2,1,0:T(2,128)S(1)}) custom-call(bf16[512,1536]{1,0:T(8,128)(2,1)S(1)} %convolution_convert_fusion.q_ref.k_ref, bf16[512,1536]{1,0:T(8,128)(2,1)S(1)} %convolution_convert_fusion.q_ref.k_ref, bf16[512,768]{1,0:T(8,128)(2,1)S(1)} %convolution_convert_fusion.1.v_ref, ...), custom_call_target="tpu_custom_call" | custom-call | flops 1048576 | bytes 1024 | tf_op jit(solution)/shard_map/pallas_call | solution.py:61
  89.1 2.4 multiply_reduce_fusion
  93.7 12.0 %all-gather.2.cloned.1.call-done.win_ref.wout_ref = bf16[768,6144]{1,0:T(8,128)(2,1)} async-done(((bf16[24,6144]{1,0:T(8,128)(2,1)}), bf16[768,6144]{1,0:T(8,128)(2,1)}) %all-gather.2.cloned.1.call-update) | async-done | bytes 9437200 | tf_op jit(solution)/shard_map/all_gather | solution.py:533
  105.7 26.3 %shard_map.204 = (bf16[512,768]{1,0:T(8,128)(2,1)}, f32[512,768]{1,0:T(8,128)}, bf16[512,768]{1,0:T(8,128)(2,1)}, bf16[512,768]{1,0:T(8,128)(2,1)}, bf16[2,2,4,9...) custom-call(s32[4]{0:T(128)} %pad_add_fusion.seat_ref, ...), custom_call_target="tpu_custom_call" | custom-call | flops 1048576 | bytes 1024 | tf_op jit(solution)/shard_map/pallas_call | solution.py:252
  133.7 6.2 %shard_map.205 = (bf16[512,256]{1,0:T(8,128)(2,1)S(1)}, bf16[512,256]{1,0:T(8,128)(2,1)S(1)}, bf16[512,256]{1,0:T(8,128)(2,1)S(1)}, f32[2,2,1024]{2,1,0:T(2,128)S(1)}) custom-call(bf16[512,1536]{1,0:T(8,128)(2,1)S(1)} %convolution_convert_fusion.q_ref.k_ref, bf16[512,1536]{1,0:T(8,128)(2,1)S(1)} %convolution_convert_fusion.q_ref.k_ref, ...), custom_call_target="tpu_custom_call" | custom-call | flops 1048576 | bytes 1024 | tf_op jit(solution)/shard_map/pallas_call | solution.py:99
  140.3 2.7 %fusion.8 = bf16[2,4,96,768]{3,2,1,0:T(8,128)(2,1)} fusion(bf16[2,2,4,96,768]{4,3,2,1,0:T(8,128)(2,1)} %collective-permute-done.10, bf16[2,2,4,96,768]{4,3,2,1,0:T(8,128)(2,1)S(1)} %copy-done.13), kind=kLoop, calls=%fused_computation.25 | loop fusion | flops 2359296 | bytes 3538944 | tf_op jit(solution)/shard_map/convert_element_type | solution.py:487
  143.1 2.7 %fusion.9 = bf16[2,4,96,768]{3,2,1,0:T(8,128)(2,1)} fusion(bf16[2,2,4,96,768]{4,3,2,1,0:T(8,128)(2,1)S(1)} %copy-done.11, bf16[2,2,4,96,768]{4,3,2,1,0:T(8,128)(2,1)} %collective-permute-done.11), kind=kLoop, calls=%fused_computation.26 | loop fusion | flops 2359296 | bytes 3538944 | tf_op jit(solution)/shard_map/convert_element_type | solution.py:487
  148.6 12.5 %shard_map.206 = (bf16[512,512]{1,0:T(8,128)(2,1)S(1)}, bf16[512,512]{1,0:T(8,128)(2,1)S(1)}, bf16[512,512]{1,0:T(8,128)(2,1)S(1)}, f32[4,2,1024]{2,1,0:T(2,128)S(1)}) custom-call(bf16[512,1536]{1,0:T(8,128)(2,1)S(1)} %convolution_convert_fusion.q_ref.k_ref, bf16[512,1536]{1,0:T(8,128)(2,1)S(1)} %convolution_convert_fusion.q_ref.k_ref, ...), custom_call_target="tpu_custom_call" | custom-call | flops 1048576 | bytes 1024 | tf_op jit(solution)/shard_map/pallas_call | solution.py:99
  162.6 8.5 %shard_map.207 = (bf16[2,2,4,48,768]{4,3,2,1,0:T(8,128)(2,1)}, bf16[2,2,4,48,768]{4,3,2,1,0:T(8,128)(2,1)}, bf16[2,2,4,48,768]{4,3,2,1,0:T(8,128)(2,1)}, bf16[2,2,4,48,768]{4,3,2,1,0:T(8,128)(2,1)}) custom-call(s32[4]{0:T(128)} %pad_add_fusion.seat_ref, bf16[512,768]{1,0:T(8,128)(2,1)} %copy-done.10, bf16[768,512]{1,0:T(8,128)(2,1)} %copy-done.1, ...), custom_call_target="tpu_custom_call" | custom-call | flops 1048576 | bytes 1024 | tf_op jit(solution)/shard_map/pallas_call | solution.py:302
  176.9 2.5 fusion.15
  179.4 2.3 fusion.14
  192.0 2.4 fusion.7
  194.9 4.5 %collective-permute-done.19 = bf16[4,96,768]{2,1,0:T(8,128)(2,1)S(1)} collective-permute-done((bf16[4,96,768]{2,1,0:T(8,128)(2,1)}, bf16[4,96,768]{2,1,0:T(8,128)(2,1)S(1)}, u32[]{:S(2)}, u32[]{:S(2)}) %collective-permute-start.19) | collective-permute-done | bytes 589856 | tf_op jit(solution)/shard_map/ppermute | solution.py:365
  204.0 8.0 %collective-permute-done.17 = bf16[2,4,48,768]{3,2,1,0:T(8,128)(2,1)S(1)} collective-permute-done((bf16[2,4,48,768]{3,2,1,0:T(8,128)(2,1)S(1)}, bf16[2,4,48,768]{3,2,1,0:T(8,128)(2,1)S(1)}, u32[]{:S(2)}, u32[]{:S(2)}) %collective-permute-start.17) | collective-permute-done | bytes 589856 | tf_op jit(solution)/shard_map/ppermute | solution.py:365
  211.9 1.8 collective-permute-done.18
  220.3 2.0 collective-permute-start.27
  222.3 3.6 %collective-permute-done.22 = bf16[4,48,768]{2,1,0:T(8,128)(2,1)S(1)} collective-permute-done((bf16[4,48,768]{2,1,0:T(8,128)(2,1)S(1)}, bf16[4,48,768]{2,1,0:T(8,128)(2,1)S(1)}, u32[]{:S(2)}, u32[]{:S(2)}) %collective-permute-start.22) | collective-permute-done | bytes 294944 | tf_op jit(solution)/shard_map/ppermute | solution.py:365
  229.4 6.1 %collective-permute-done.27 = bf16[1,192,768]{2,1,0:T(8,128)(2,1)S(1)} collective-permute-done((bf16[1,192,768]{2,1,0:T(8,128)(2,1)S(1)}, bf16[1,192,768]{2,1,0:T(8,128)(2,1)S(1)}, u32[]{:S(2)}, u32[]{:S(2)}) %collective-permute-start.27) | collective-permute-done | bytes 294944 | tf_op jit(solution)/shard_map/ppermute | solution.py:365
  235.7 1.9 convert_add_fusion.7
  238.3 3.2 %collective-permute-done.24 = bf16[2,104,768]{2,1,0:T(8,128)(2,1)S(1)} collective-permute-done((bf16[2,104,768]{2,1,0:T(8,128)(2,1)S(1)}, bf16[2,104,768]{2,1,0:T(8,128)(2,1)S(1)}, u32[]{:S(2)}, u32[]{:S(2)}) %collective-permute-start.24) | collective-permute-done | bytes 319520 | tf_op jit(solution)/shard_map/ppermute | solution.py:365
  244.9 6.3 %collective-permute-done.25 = bf16[1,104,768]{2,1,0:T(8,128)(2,1)S(1)} collective-permute-done((bf16[1,104,768]{2,1,0:T(8,128)(2,1)S(1)}, bf16[1,104,768]{2,1,0:T(8,128)(2,1)S(1)}, u32[]{:S(2)}, u32[]{:S(2)}) %collective-permute-start.25) | collective-permute-done | bytes 159776 | tf_op jit(solution)/shard_map/ppermute | solution.py:365
  (251 shorter events, 68.8 us)
Async XLA Ops:
  7.2 98.5 %all-gather.2.cloned.1.call-start = ((), (), s32[]{:S(2)}) async-start(), calls=%async_computation | async-start | bytes 9732096 | tf_op jit(solution)/shard_map/all_gather | solution.py:533
  12.7 19.9 %collective-permute-start.2 = (bf16[24,3200]{1,0:T(8,128)(2,1)S(1)}, bf16[24,3200]{1,0:T(8,128)(2,1)S(1)}, u32[]{:S(2)}, u32[]{:S(2)}) collective-permute-start(bf16[24,3200]{1,0:T(8,128)(2,1)S(1)} %constant_dynamic-update-slice_fusion), channel_id=1, source_target_pairs={{0,16},{1,17},{2,18},{3,19},{4,20},{5,21},{6,22},{7,23},{8,24},{9,... | collective-permute-start | bytes 460808 | tf_op jit(solution)/shard_map/ppermute | solution.py:365
  16.8 15.8 %collective-permute-start.3 = (bf16[24,3200]{1,0:T(8,128)(2,1)S(1)}, bf16[24,3200]{1,0:T(8,128)(2,1)}, u32[]{:S(2)}, u32[]{:S(2)}) collective-permute-start(bf16[24,3200]{1,0:T(8,128)(2,1)S(1)} %constant_dynamic-update-slice_fusion), channel_id=1, source_target_pairs={{0,24},{1,25},{2,26},{3,27},{4,28},{5,29},{6,30},{7,31},{8,16},{9,... | collective-permute-start | bytes 460808 | tf_op jit(solution)/shard_map/ppermute | solution.py:365
  18.2 13.5 %collective-permute-start.1 = (bf16[24,3200]{1,0:T(8,128)(2,1)S(1)}, bf16[24,3200]{1,0:T(8,128)(2,1)}, u32[]{:S(2)}, u32[]{:S(2)}) collective-permute-start(bf16[24,3200]{1,0:T(8,128)(2,1)S(1)} %constant_dynamic-update-slice_fusion), channel_id=1, source_target_pairs={{0,8},{1,9},{2,10},{3,11},{4,12},{5,13},{6,14},{7,15},{8,0},{9,1},... | collective-permute-start | bytes 460808 | tf_op jit(solution)/shard_map/ppermute | solution.py:365
  18.5 50.8 %collective-permute-start = (bf16[2,256,768]{2,1,0:T(8,128)(2,1)S(1)}, bf16[2,256,768]{2,1,0:T(8,128)(2,1)S(1)}, u32[]{:S(2)}, u32[]{:S(2)}) collective-permute-start(bf16[2,256,768]{2,1,0:T(8,128)(2,1)S(1)} %pad_maximum_fusion.4), channel_id=1, source_target_pairs={{0,1},{1,0},{2,3},{3,2},{4,5},{5,4},{6,7},{7,6},{8,9},{9,8},{10,11... | collective-permute-start | bytes 2359304 | tf_op jit(solution)/shard_map/ppermute | solution.py:337
  20.4 55.8 %copy-start.37 = (s32[1024]{0:T(1024)}, s32[1024]{0:T(1024)S(1)}, u32[]{:S(2)}) copy-start(s32[1024]{0:T(1024)S(1)} %pad.13) | copy-start | bytes 12292
  33.7 6.8 %collective-permute-start.7 = (bf16[2,2,24,1536]{3,2,1,0:T(8,128)(2,1)S(1)}, bf16[2,2,24,1536]{3,2,1,0:T(8,128)(2,1)S(1)}, u32[]{:S(2)}, u32[]{:S(2)}) collective-permute-start(bf16[2,2,24,1536]{3,2,1,0:T(8,128)(2,1)S(1)} %pad_maximum_fusion.16), channel_id=1, source_target_pairs={{0,4},{1,5},{2,6},{3,7},{4,0},{5,1},{6,2},{7,3},{8,12},{9,13},{10,... | collective-permute-start | bytes 884744 | tf_op jit(solution)/shard_map/ppermute | solution.py:365
  36.1 13.2 %collective-permute-start.4 = (bf16[2,2,24,1664]{3,2,1,0:T(8,128)(2,1)S(1)}, bf16[2,2,24,1664]{3,2,1,0:T(8,128)(2,1)S(1)}, u32[]{:S(2)}, u32[]{:S(2)}) collective-permute-start(bf16[2,2,24,1664]{3,2,1,0:T(8,128)(2,1)S(1)} %fusion.26), channel_id=1, source_target_pairs={{0,1},{1,0},{2,3},{3,2},{4,5},{5,4},{6,7},{7,6},{8,9},{9,8},{10,11... | collective-permute-start | bytes 958472 | tf_op jit(solution)/shard_map/ppermute | solution.py:365
  40.7 22.4 %collective-permute-start.8 = (bf16[2,2,2,24,1536]{4,3,2,1,0:T(8,128)(2,1)S(1)}, bf16[2,2,2,24,1536]{4,3,2,1,0:T(8,128)(2,1)S(1)}, u32[]{:S(2)}, u32[]{:S(2)}) collective-permute-start(bf16[2,2,2,24,1536]{4,3,2,1,0:T(8,128)(2,1)S(1)} %pad_maximum_fusion.10), channel_id=1, source_target_pairs={{0,1},{1,0},{2,3},{3,2},{4,5},{5,4},{6,7},{7,6},{8,9},{9,8},{10,11... | collective-permute-start | bytes 1769480 | tf_op jit(solution)/shard_map/ppermute | solution.py:365
  49.5 19.5 %collective-permute-start.5 = (bf16[2,2,2,24,1664]{4,3,1,0,2:T(8,128)(2,1)S(1)}, bf16[2,2,2,24,1664]{4,3,1,0,2:T(8,128)(2,1)S(1)}, u32[]{:S(2)}, u32[]{:S(2)}) collective-permute-start(bf16[2,2,2,24,1664]{4,3,1,0,2:T(8,128)(2,1)S(1)} %pad_maximum_fusion.9), channel_id=1, source_target_pairs={{0,4},{1,5},{2,6},{3,7},{4,0},{5,1},{6,2},{7,3},{8,12},{9,13},{10,... | collective-permute-start | bytes 1916936 | tf_op jit(solution)/shard_map/ppermute | solution.py:365
  63.3 7.9 %collective-permute-start.9 = (bf16[2,2,2,2,24,1536]{5,4,3,2,1,0:T(8,128)(2,1)S(1)}, bf16[2,2,2,2,24,1536]{5,4,3,2,1,0:T(8,128)(2,1)S(1)}, u32[]{:S(2)}, u32[]{:S(2)}) collective-permute-start(bf16[2,2,2,2,24,1536]{5,4,3,2,1,0:T(8,128)(2,1)S(1)} %pad_maximum_fusion.3), channel_id=1, source_target_pairs={{0,2},{1,3},{2,0},{3,1},{4,6},{5,7},{6,4},{7,5},{8,10},{9,11},{10,... | collective-permute-start | bytes 3538952 | tf_op jit(solution)/shard_map/ppermute | solution.py:365
  69.3 3.8 %collective-permute-start.6 = (bf16[2,2,2,2,24,1664]{5,4,1,0,3,2:T(8,128)(2,1)S(1)}, bf16[2,2,2,2,24,1664]{5,4,1,0,3,2:T(8,128)(2,1)S(1)}, u32[]{:S(2)}, u32[]{:S(2)}) collective-permute-start(bf16[2,2,2,2,24,1664]{5,4,1,0,3,2:T(8,128)(2,1)S(1)} %pad_maximum_fusion.2), channel_id=1, source_target_pairs={{0,2},{1,3},{2,0},{3,1},{4,6},{5,7},{6,4},{7,5},{8,10},{9,11},{10,... | collective-permute-start | bytes 3833864 | tf_op jit(solution)/shard_map/ppermute | solution.py:365
  132.0 8.0 %collective-permute-start.10 = (bf16[2,2,4,96,768]{4,3,2,1,0:T(8,128)(2,1)}, bf16[2,2,4,96,768]{4,3,2,1,0:T(8,128)(2,1)}, u32[]{:S(2)}, u32[]{:S(2)}) collective-permute-start(bf16[2,2,4,96,768]{4,3,2,1,0:T(8,128)(2,1)} %get-tuple-element.100), channel_id=1, source_target_pairs={{0,2},{1,3},{2,0},{3,1},{4,6},{5,7},{6,4},{7,5},{8,10},{9,11},{10,... | collective-permute-start | bytes 7077896 | tf_op jit(solution)/shard_map/ppermute | solution.py:365
  132.3 8.0 %collective-permute-start.11 = (bf16[2,2,4,96,768]{4,3,2,1,0:T(8,128)(2,1)}, bf16[2,2,4,96,768]{4,3,2,1,0:T(8,128)(2,1)}, u32[]{:S(2)}, u32[]{:S(2)}) collective-permute-start(bf16[2,2,4,96,768]{4,3,2,1,0:T(8,128)(2,1)} %get-tuple-element.101), channel_id=1, source_target_pairs={{0,2},{1,3},{2,0},{3,1},{4,6},{5,7},{6,4},{7,5},{8,10},{9,11},{10,... | collective-permute-start | bytes 7077896 | tf_op jit(solution)/shard_map/ppermute | solution.py:365
  145.8 28.4 %collective-permute-start.14 = (bf16[2,4,96,768]{3,2,1,0:T(8,128)(2,1)}, bf16[2,4,96,768]{3,2,1,0:T(8,128)(2,1)}, u32[]{:S(2)}, u32[]{:S(2)}) collective-permute-start(bf16[2,4,96,768]{3,2,1,0:T(8,128)(2,1)} %fusion.8), channel_id=1, source_target_pairs={{0,4},{1,5},{2,6},{3,7},{4,0},{5,1},{6,2},{7,3},{8,12},{9,13},{10,... | collective-permute-start | bytes 3538952 | tf_op jit(solution)/shard_map/ppermute | solution.py:365
  147.2 28.1 %collective-permute-start.15 = (bf16[2,4,96,768]{3,2,1,0:T(8,128)(2,1)}, bf16[2,4,96,768]{3,2,1,0:T(8,128)(2,1)}, u32[]{:S(2)}, u32[]{:S(2)}) collective-permute-start(bf16[2,4,96,768]{3,2,1,0:T(8,128)(2,1)} %fusion.9), channel_id=1, source_target_pairs={{0,1},{1,0},{2,3},{3,2},{4,5},{5,4},{6,7},{7,6},{8,9},{9,8},{10,11... | collective-permute-start | bytes 3538952 | tf_op jit(solution)/shard_map/ppermute | solution.py:365
  171.7 13.5 %collective-permute-start.12 = (bf16[2,2,4,48,768]{4,3,2,1,0:T(8,128)(2,1)}, bf16[2,2,4,48,768]{4,3,2,1,0:T(8,128)(2,1)}, u32[]{:S(2)}, u32[]{:S(2)}) collective-permute-start(bf16[2,2,4,48,768]{4,3,2,1,0:T(8,128)(2,1)} %get-tuple-element.129), channel_id=1, source_target_pairs={{0,2},{1,3},{2,0},{3,1},{4,6},{5,7},{6,4},{7,5},{8,10},{9,11},{10,... | collective-permute-start | bytes 3538952 | tf_op jit(solution)/shard_map/ppermute | solution.py:365
  171.7 13.5 %collective-permute-start.13 = (bf16[2,2,4,48,768]{4,3,2,1,0:T(8,128)(2,1)}, bf16[2,2,4,48,768]{4,3,2,1,0:T(8,128)(2,1)}, u32[]{:S(2)}, u32[]{:S(2)}) collective-permute-start(bf16[2,2,4,48,768]{4,3,2,1,0:T(8,128)(2,1)} %get-tuple-element.130), channel_id=1, source_target_pairs={{0,2},{1,3},{2,0},{3,1},{4,6},{5,7},{6,4},{7,5},{8,10},{9,11},{10,... | collective-permute-start | bytes 3538952 | tf_op jit(solution)/shard_map/ppermute | solution.py:365
  182.9 2.3 collective-permute-start.16
  183.0 16.4 %collective-permute-start.19 = (bf16[4,96,768]{2,1,0:T(8,128)(2,1)}, bf16[4,96,768]{2,1,0:T(8,128)(2,1)S(1)}, u32[]{:S(2)}, u32[]{:S(2)}) collective-permute-start(bf16[4,96,768]{2,1,0:T(8,128)(2,1)} %fusion.15), channel_id=1, source_target_pairs={{0,1},{1,0},{2,3},{3,2},{4,5},{5,4},{6,7},{7,6},{8,9},{9,8},{10,11... | collective-permute-start | bytes 1769480 | tf_op jit(solution)/shard_map/ppermute | solution.py:365
  183.7 16.4 %collective-permute-start.20 = (bf16[4,96,768]{2,1,0:T(8,128)(2,1)}, bf16[4,96,768]{2,1,0:T(8,128)(2,1)S(1)}, u32[]{:S(2)}, u32[]{:S(2)}) collective-permute-start(bf16[4,96,768]{2,1,0:T(8,128)(2,1)} %fusion.14), channel_id=1, source_target_pairs={{0,4},{1,5},{2,6},{3,7},{4,0},{5,1},{6,2},{7,3},{8,12},{9,13},{10,... | collective-permute-start | bytes 1769480 | tf_op jit(solution)/shard_map/ppermute | solution.py:365
  188.0 23.9 %collective-permute-start.17 = (bf16[2,4,48,768]{3,2,1,0:T(8,128)(2,1)S(1)}, bf16[2,4,48,768]{3,2,1,0:T(8,128)(2,1)S(1)}, u32[]{:S(2)}, u32[]{:S(2)}) collective-permute-start(bf16[2,4,48,768]{3,2,1,0:T(8,128)(2,1)S(1)} %fusion.18), channel_id=1, source_target_pairs={{0,4},{1,5},{2,6},{3,7},{4,0},{5,1},{6,2},{7,3},{8,12},{9,13},{10,... | collective-permute-start | bytes 1769480 | tf_op jit(solution)/shard_map/ppermute | solution.py:365
  188.7 25.0 %collective-permute-start.18 = (bf16[2,4,56,768]{3,2,1,0:T(8,128)(2,1)S(1)}, bf16[2,4,56,768]{3,2,1,0:T(8,128)(2,1)S(1)}, u32[]{:S(2)}, u32[]{:S(2)}) collective-permute-start(bf16[2,4,56,768]{3,2,1,0:T(8,128)(2,1)S(1)} %pad_maximum_fusion.8), channel_id=1, source_target_pairs={{0,1},{1,0},{2,3},{3,2},{4,5},{5,4},{6,7},{7,6},{8,9},{9,8},{10,11... | collective-permute-start | bytes 2064392 | tf_op jit(solution)/shard_map/ppermute | solution.py:365
  199.4 19.5 %copy-start.30 = (bf16[4,96,768]{2,1,0:T(8,128)(2,1)}, bf16[4,96,768]{2,1,0:T(8,128)(2,1)S(1)}, u32[]{:S(2)}) copy-start(bf16[4,96,768]{2,1,0:T(8,128)(2,1)S(1)} %collective-permute-done.19) | copy-start | bytes 1769476
  202.6 16.2 %collective-permute-start.26 = (bf16[2,192,768]{2,1,0:T(8,128)(2,1)S(1)}, bf16[2,192,768]{2,1,0:T(8,128)(2,1)S(1)}, u32[]{:S(2)}, u32[]{:S(2)}) collective-permute-start(bf16[2,192,768]{2,1,0:T(8,128)(2,1)S(1)} %pad_maximum_fusion.11), channel_id=1, source_target_pairs={{0,8},{1,9},{2,10},{3,11},{4,12},{5,13},{6,14},{7,15},{8,0},{9,1},... | collective-permute-start | bytes 1769480 | tf_op jit(solution)/shard_map/ppermute | solution.py:365
  216.0 10.0 %collective-permute-start.22 = (bf16[4,48,768]{2,1,0:T(8,128)(2,1)S(1)}, bf16[4,48,768]{2,1,0:T(8,128)(2,1)S(1)}, u32[]{:S(2)}, u32[]{:S(2)}) collective-permute-start(bf16[4,48,768]{2,1,0:T(8,128)(2,1)S(1)} %fusion.21), channel_id=1, source_target_pairs={{0,1},{1,0},{2,3},{3,2},{4,5},{5,4},{6,7},{7,6},{8,9},{9,8},{10,11... | collective-permute-start | bytes 884744 | tf_op jit(solution)/shard_map/ppermute | solution.py:365
  216.7 9.3 %collective-permute-start.23 = (bf16[4,56,768]{2,1,0:T(8,128)(2,1)S(1)}, bf16[4,56,768]{2,1,0:T(8,128)(2,1)S(1)}, u32[]{:S(2)}, u32[]{:S(2)}) collective-permute-start(bf16[4,56,768]{2,1,0:T(8,128)(2,1)S(1)} %pad_maximum_fusion.12), channel_id=1, source_target_pairs={{0,4},{1,5},{2,6},{3,7},{4,0},{5,1},{6,2},{7,3},{8,12},{9,13},{10,... | collective-permute-start | bytes 1032200 | tf_op jit(solution)/shard_map/ppermute | solution.py:365
  218.2 24.4 %collective-permute-start.21 = (bf16[2,256,768]{2,1,0:T(8,128)(2,1)S(1)}, bf16[2,256,768]{2,1,0:T(8,128)(2,1)S(1)}, u32[]{:S(2)}, u32[]{:S(2)}) collective-permute-start(bf16[2,256,768]{2,1,0:T(8,128)(2,1)S(1)} %pad_maximum_fusion.7), channel_id=1, source_target_pairs={{0,1},{1,0},{2,3},{3,2},{4,5},{5,4},{6,7},{7,6},{8,9},{9,8},{10,11... | collective-permute-start | bytes 2359304 | tf_op jit(solution)/shard_map/ppermute | solution.py:348
  220.3 15.2 %copy-start.29 = (bf16[1,1,96,768]{3,2,1,0:T(8,128)(2,1)S(1)}, bf16[1,1,96,768]{3,2,1,0:T(8,128)(2,1)}, u32[]{:S(2)}) copy-start(bf16[1,1,96,768]{3,2,1,0:T(8,128)(2,1)} %split.272) | copy-start | bytes 442372
  220.3 15.1 %collective-permute-start.27 = (bf16[1,192,768]{2,1,0:T(8,128)(2,1)S(1)}, bf16[1,192,768]{2,1,0:T(8,128)(2,1)S(1)}, u32[]{:S(2)}, u32[]{:S(2)}) collective-permute-start(bf16[1,192,768]{2,1,0:T(8,128)(2,1)S(1)} %pad_maximum_fusion.18), channel_id=1, source_target_pairs={{0,16},{1,17},{2,18},{3,19},{4,20},{5,21},{6,22},{7,23},{8,24},{9,... | collective-permute-start | bytes 884744 | tf_op jit(solution)/shard_map/ppermute | solution.py:365
  228.1 13.4 %collective-permute-start.24 = (bf16[2,104,768]{2,1,0:T(8,128)(2,1)S(1)}, bf16[2,104,768]{2,1,0:T(8,128)(2,1)S(1)}, u32[]{:S(2)}, u32[]{:S(2)}) collective-permute-start(bf16[2,104,768]{2,1,0:T(8,128)(2,1)S(1)} %pad_maximum_fusion.13), channel_id=1, source_target_pairs={{0,8},{1,9},{2,10},{3,11},{4,12},{5,13},{6,14},{7,15},{8,0},{9,1},... | collective-permute-start | bytes 958472 | tf_op jit(solution)/shard_map/ppermute | solution.py:365
  242.6 8.6 %collective-permute-start.25 = (bf16[1,104,768]{2,1,0:T(8,128)(2,1)S(1)}, bf16[1,104,768]{2,1,0:T(8,128)(2,1)S(1)}, u32[]{:S(2)}, u32[]{:S(2)}) collective-permute-start(bf16[1,104,768]{2,1,0:T(8,128)(2,1)S(1)} %pad_maximum_fusion.19), channel_id=1, source_target_pairs={{0,16},{1,17},{2,18},{3,19},{4,20},{5,21},{6,22},{7,23},{8,24},{9,... | collective-permute-start | bytes 479240 | tf_op jit(solution)/shard_map/ppermute | solution.py:365
  (44 other events, 230.3 us)
Sparse Core Ops, SparseCore 0:
  11.6 94.1 all-gather.1

commit v6 on v5

--- a/solution.py
+++ b/solution.py
@@ -121,7 +121,7 @@
     x = x_ref[...]
     top = top_ref[...]
     pre = dot_nn(x, win_ref[...])
-    sig = 1.0 / (1.0 + jnp.exp(-pre))
+    sig = 0.5 * jnp.tanh(0.5 * pre) + 0.5
     hid = (pre * sig).astype(jnp.bfloat16)
     gact = dot_nt(top, wout)
     gpre = (gact * (sig * (1.0 + pre * (1.0 - sig)))).astype(jnp.bfloat16)
@@ -435,6 +435,8 @@
 
 
 def summed(terms, pick):
+    if len(terms) == 2:
+        return pick(terms[0]) + pick(terms[1])
     return sum(pick(term).astype(jnp.float32) for term in terms)
 
 

time: 263 us -> 262 us (level)
    add x0 -> x5, other arithmetic: none -> 7.93 us  [summed(): return pick(terms[0]) + pick(terms[1])]
    convert_element_type x6 -> x3, other arithmetic: 12.7 us -> 5.9 us  [prepare(): self.outgoing.append(total.astype(jnp.bfloat16))]
    add x5 -> x4, other arithmetic: 5.58 us -> 4.21 us  [summed(): return sum((pick(term).astype(jnp.float32) for term in terms))]
    another operation x11 -> x10, other arithmetic: 8.1 us -> 8.08 us
  transfers between devices with their start and end apart: 29 -> 29, of which waited for: 18 -> 17; matrix products, arithmetic and copies ran while one was open for 20% -> 20% of each run, Pallas kernels for 14% -> 14%
where the time goes in v6:
time: 262 us; the launch traced here: 261 us
  waiting for transfers between devices  86.1 us (33%)
  Pallas kernels  62 us (24%)
  other arithmetic  44.9 us (17%)
  starting transfers between devices  30 us (11%)
  between operations  15.1 us (6%)
  local copies, waits for them, and re-layouts  14.2 us (5%)
  matrix products  8.99 us (3%)
    ppermute x26, waiting for transfers between devices, partner_sends(): lax.ppermute(array, ('rows', 'seq'), [(b, b ^ mask) for b in range(device...  74.1 us
    ppermute x26, starting transfers between devices, partner_sends(): lax.ppermute(array, ('rows', 'seq'), [(b, b ^ mask) for b in range(device...  27.8 us
    pallas_call x1, Pallas kernels, ffn(): pl.pallas_call(ffn_kernel, grid_spec=pltpu.PrefetchScalarGridSpec(num_sca...  25.9 us
    pallas_call x2, Pallas kernels, attend_back(): pl.pallas_call(attend_back_kernel, grid=(count,), in_specs=[spec(start),...  18.7 us
    all_gather x1, waiting for transfers between devices, shards(): lax.all_gather(jnp.concatenate([w_in, groups], axis=1), ('rows', 'seq'),...  12 us
    pallas_call x1, Pallas kernels, attend(): pl.pallas_call(attend_kernel, grid=(steps,), in_specs=[spec(0), spec(step...  8.92 us
    pallas_call x1, Pallas kernels, weight_grads(): pl.pallas_call(kernel, grid_spec=pltpu.PrefetchScalarGridSpec(num_scalar_...  8.45 us
    another operation x10, other arithmetic  8.08 us
  transfers between devices with their start and end apart: 29, of which 17 were waited for; matrix products, arithmetic and copies ran while one was open for 20% of the time, Pallas kernels for 14%

profile of v6, /device:TPU:0, one launch (start us, length us, event | category | flops | bytes accessed | tf_op | source)
XLA Modules:
  0.0 261.3 jit_solution(17588401234832375751)
XLA Ops:
  8.4 1.6 pad_maximum_fusion.17
  12.7 4.1 %collective-permute-start.2 = (bf16[24,3200]{1,0:T(8,128)(2,1)S(1)}, bf16[24,3200]{1,0:T(8,128)(2,1)S(1)}, u32[]{:S(2)}, u32[]{:S(2)}) collective-permute-start(bf16[24,3200]{1,0:T(8,128)(2,1)S(1)} %constant_dynamic-update-slice_fusion), channel_id=1, source_target_pairs={{0,16},{1,17},{2,18},{3,19},{4,20},{5,21},{6,22},{7,23},{8,24},{9,... | collective-permute-start | bytes 460808 | tf_op jit(solution)/shard_map/ppermute | solution.py:365
  20.4 11.3 %collective-permute-done.1 = bf16[24,3200]{1,0:T(8,128)(2,1)} collective-permute-done((bf16[24,3200]{1,0:T(8,128)(2,1)S(1)}, bf16[24,3200]{1,0:T(8,128)(2,1)}, u32[]{:S(2)}, u32[]{:S(2)}) %collective-permute-start.1) | collective-permute-done | bytes 153632 | tf_op jit(solution)/shard_map/ppermute | solution.py:365
  33.7 1.8 collective-permute-start.7
  36.1 2.2 collective-permute-start.4
  38.3 2.2 collective-permute-done.7
  40.7 2.4 collective-permute-start.8
  43.1 6.3 %collective-permute-done.4 = bf16[2,2,24,1664]{3,2,1,0:T(8,128)(2,1)S(1)} collective-permute-done((bf16[2,2,24,1664]{3,2,1,0:T(8,128)(2,1)S(1)}, bf16[2,2,24,1664]{3,2,1,0:T(8,128)(2,1)S(1)}, u32[]{:S(2)}, u32[]{:S(2)}) %collective-permute-start.4) | collective-permute-done | bytes 319520 | tf_op jit(solution)/shard_map/ppermute | solution.py:365
  50.9 12.3 %collective-permute-done.8 = bf16[2,2,2,24,1536]{4,3,2,1,0:T(8,128)(2,1)S(1)} collective-permute-done((bf16[2,2,2,24,1536]{4,3,2,1,0:T(8,128)(2,1)S(1)}, bf16[2,2,2,24,1536]{4,3,2,1,0:T(8,128)(2,1)S(1)}, u32[]{:S(2)}, u32[]{:S(2)}) %collective-permute-start.8) | collective-permute-done | bytes 589856 | tf_op jit(solution)/shard_map/ppermute | solution.py:365
  63.4 5.6 %collective-permute-done.5 = bf16[2,2,2,24,1664]{4,3,1,0,2:T(8,128)(2,1)S(1)} collective-permute-done((bf16[2,2,2,24,1664]{4,3,1,0,2:T(8,128)(2,1)S(1)}, bf16[2,2,2,24,1664]{4,3,1,0,2:T(8,128)(2,1)S(1)}, u32[]{:S(2)}, u32[]{:S(2)}) %collective-permute-start.5) | collective-permute-done | bytes 639008 | tf_op jit(solution)/shard_map/ppermute | solution.py:365
  71.4 1.6 pad_maximum_fusion.1
  80.1 8.9 %shard_map.203 = (bf16[512,768]{1,0:T(8,128)(2,1)S(1)}, bf16[768,512]{1,0:T(8,128)(2,1)S(1)}, f32[6,2,512]{2,1,0:T(2,128)S(1)}) custom-call(bf16[512,1536]{1,0:T(8,128)(2,1)S(1)} %convolution_convert_fusion.q_ref.k_ref, bf16[512,1536]{1,0:T(8,128)(2,1)S(1)} %convolution_convert_fusion.q_ref.k_ref, bf16[512,768]{1,0:T(8,128)(2,1)S(1)} %convolution_convert_fusion.1.v_ref, ...), custom_call_target="tpu_custom_call" | custom-call | flops 1048576 | bytes 1024 | tf_op jit(solution)/shard_map/pallas_call | solution.py:61
  89.1 2.4 multiply_reduce_fusion
  93.7 12.0 %all-gather.2.cloned.1.call-done.win_ref.wout_ref = bf16[768,6144]{1,0:T(8,128)(2,1)} async-done(((bf16[24,6144]{1,0:T(8,128)(2,1)}), bf16[768,6144]{1,0:T(8,128)(2,1)}) %all-gather.2.cloned.1.call-update) | async-done | bytes 9437200 | tf_op jit(solution)/shard_map/all_gather | solution.py:535
  105.7 25.9 %shard_map.204 = (bf16[512,768]{1,0:T(8,128)(2,1)}, f32[512,768]{1,0:T(8,128)}, bf16[512,768]{1,0:T(8,128)(2,1)}, bf16[512,768]{1,0:T(8,128)(2,1)}, bf16[2,2,4,9...) custom-call(s32[4]{0:T(128)} %pad_add_fusion.seat_ref, ...), custom_call_target="tpu_custom_call" | custom-call | flops 1048576 | bytes 1024 | tf_op jit(solution)/shard_map/pallas_call | solution.py:252
  133.3 6.2 %shard_map.205 = (bf16[512,256]{1,0:T(8,128)(2,1)S(1)}, bf16[512,256]{1,0:T(8,128)(2,1)S(1)}, bf16[512,256]{1,0:T(8,128)(2,1)S(1)}, f32[2,2,1024]{2,1,0:T(2,128)S(1)}) custom-call(bf16[512,1536]{1,0:T(8,128)(2,1)S(1)} %convolution_convert_fusion.q_ref.k_ref, bf16[512,1536]{1,0:T(8,128)(2,1)S(1)} %convolution_convert_fusion.q_ref.k_ref, ...), custom_call_target="tpu_custom_call" | custom-call | flops 1048576 | bytes 1024 | tf_op jit(solution)/shard_map/pallas_call | solution.py:99
  139.9 2.6 add_bitcast_fusion
  142.5 2.7 %fusion.12 = bf16[2,4,96,768]{3,2,1,0:T(8,128)(2,1)} fusion(bf16[2,2,4,96,768]{4,3,2,1,0:T(8,128)(2,1)S(1)} %copy-done.11, bf16[2,2,4,96,768]{4,3,2,1,0:T(8,128)(2,1)} %collective-permute-done.11), kind=kLoop, calls=%fused_computation.28 | loop fusion | flops 2359296 | bytes 3538944 | tf_op jit(solution)/shard_map/add | solution.py:439
  148.0 12.5 %shard_map.206 = (bf16[512,512]{1,0:T(8,128)(2,1)S(1)}, bf16[512,512]{1,0:T(8,128)(2,1)S(1)}, bf16[512,512]{1,0:T(8,128)(2,1)S(1)}, f32[4,2,1024]{2,1,0:T(2,128)S(1)}) custom-call(bf16[512,1536]{1,0:T(8,128)(2,1)S(1)} %convolution_convert_fusion.q_ref.k_ref, bf16[512,1536]{1,0:T(8,128)(2,1)S(1)} %convolution_convert_fusion.q_ref.k_ref, ...), custom_call_target="tpu_custom_call" | custom-call | flops 1048576 | bytes 1024 | tf_op jit(solution)/shard_map/pallas_call | solution.py:99
  162.0 8.5 %shard_map.207 = (bf16[2,2,4,48,768]{4,3,2,1,0:T(8,128)(2,1)}, bf16[2,2,4,48,768]{4,3,2,1,0:T(8,128)(2,1)}, bf16[2,2,4,48,768]{4,3,2,1,0:T(8,128)(2,1)}, bf16[2,2,4,48,768]{4,3,2,1,0:T(8,128)(2,1)}) custom-call(s32[4]{0:T(128)} %pad_add_fusion.seat_ref, bf16[512,768]{1,0:T(8,128)(2,1)} %copy-done.10, bf16[768,512]{1,0:T(8,128)(2,1)} %copy-done.1, ...), custom_call_target="tpu_custom_call" | custom-call | flops 1048576 | bytes 1024 | tf_op jit(solution)/shard_map/pallas_call | solution.py:302
  176.4 2.5 fusion.14
  178.8 2.3 fusion.13
  191.4 2.4 fusion.7
  194.3 4.6 %collective-permute-done.19 = bf16[4,96,768]{2,1,0:T(8,128)(2,1)S(1)} collective-permute-done((bf16[4,96,768]{2,1,0:T(8,128)(2,1)}, bf16[4,96,768]{2,1,0:T(8,128)(2,1)S(1)}, u32[]{:S(2)}, u32[]{:S(2)}) %collective-permute-start.19) | collective-permute-done | bytes 589856 | tf_op jit(solution)/shard_map/ppermute | solution.py:365
  203.4 7.9 %collective-permute-done.17 = bf16[2,4,48,768]{3,2,1,0:T(8,128)(2,1)S(1)} collective-permute-done((bf16[2,4,48,768]{3,2,1,0:T(8,128)(2,1)S(1)}, bf16[2,4,48,768]{3,2,1,0:T(8,128)(2,1)S(1)}, u32[]{:S(2)}, u32[]{:S(2)}) %collective-permute-start.17) | collective-permute-done | bytes 589856 | tf_op jit(solution)/shard_map/ppermute | solution.py:365
  211.3 1.8 collective-permute-done.18
  219.8 1.9 collective-permute-start.27
  221.7 3.7 %collective-permute-done.22 = bf16[4,48,768]{2,1,0:T(8,128)(2,1)S(1)} collective-permute-done((bf16[4,48,768]{2,1,0:T(8,128)(2,1)S(1)}, bf16[4,48,768]{2,1,0:T(8,128)(2,1)S(1)}, u32[]{:S(2)}, u32[]{:S(2)}) %collective-permute-start.22) | collective-permute-done | bytes 294944 | tf_op jit(solution)/shard_map/ppermute | solution.py:365
  228.8 6.1 %collective-permute-done.27 = bf16[1,192,768]{2,1,0:T(8,128)(2,1)S(1)} collective-permute-done((bf16[1,192,768]{2,1,0:T(8,128)(2,1)S(1)}, bf16[1,192,768]{2,1,0:T(8,128)(2,1)S(1)}, u32[]{:S(2)}, u32[]{:S(2)}) %collective-permute-start.27) | collective-permute-done | bytes 294944 | tf_op jit(solution)/shard_map/ppermute | solution.py:365
  235.1 1.9 convert_add_fusion.7
  237.7 3.2 %collective-permute-done.24 = bf16[2,104,768]{2,1,0:T(8,128)(2,1)S(1)} collective-permute-done((bf16[2,104,768]{2,1,0:T(8,128)(2,1)S(1)}, bf16[2,104,768]{2,1,0:T(8,128)(2,1)S(1)}, u32[]{:S(2)}, u32[]{:S(2)}) %collective-permute-start.24) | collective-permute-done | bytes 319520 | tf_op jit(solution)/shard_map/ppermute | solution.py:365
  244.4 6.3 %collective-permute-done.25 = bf16[1,104,768]{2,1,0:T(8,128)(2,1)S(1)} collective-permute-done((bf16[1,104,768]{2,1,0:T(8,128)(2,1)S(1)}, bf16[1,104,768]{2,1,0:T(8,128)(2,1)S(1)}, u32[]{:S(2)}, u32[]{:S(2)}) %collective-permute-start.25) | collective-permute-done | bytes 159776 | tf_op jit(solution)/shard_map/ppermute | solution.py:365
  (251 shorter events, 68.7 us)
Async XLA Ops:
  7.2 98.5 %all-gather.2.cloned.1.call-start = ((), (), s32[]{:S(2)}) async-start(), calls=%async_computation | async-start | bytes 9732096 | tf_op jit(solution)/shard_map/all_gather | solution.py:535
  12.7 19.9 %collective-permute-start.2 = (bf16[24,3200]{1,0:T(8,128)(2,1)S(1)}, bf16[24,3200]{1,0:T(8,128)(2,1)S(1)}, u32[]{:S(2)}, u32[]{:S(2)}) collective-permute-start(bf16[24,3200]{1,0:T(8,128)(2,1)S(1)} %constant_dynamic-update-slice_fusion), channel_id=1, source_target_pairs={{0,16},{1,17},{2,18},{3,19},{4,20},{5,21},{6,22},{7,23},{8,24},{9,... | collective-permute-start | bytes 460808 | tf_op jit(solution)/shard_map/ppermute | solution.py:365
  16.8 15.8 %collective-permute-start.3 = (bf16[24,3200]{1,0:T(8,128)(2,1)S(1)}, bf16[24,3200]{1,0:T(8,128)(2,1)}, u32[]{:S(2)}, u32[]{:S(2)}) collective-permute-start(bf16[24,3200]{1,0:T(8,128)(2,1)S(1)} %constant_dynamic-update-slice_fusion), channel_id=1, source_target_pairs={{0,24},{1,25},{2,26},{3,27},{4,28},{5,29},{6,30},{7,31},{8,16},{9,... | collective-permute-start | bytes 460808 | tf_op jit(solution)/shard_map/ppermute | solution.py:365
  18.2 13.5 %collective-permute-start.1 = (bf16[24,3200]{1,0:T(8,128)(2,1)S(1)}, bf16[24,3200]{1,0:T(8,128)(2,1)}, u32[]{:S(2)}, u32[]{:S(2)}) collective-permute-start(bf16[24,3200]{1,0:T(8,128)(2,1)S(1)} %constant_dynamic-update-slice_fusion), channel_id=1, source_target_pairs={{0,8},{1,9},{2,10},{3,11},{4,12},{5,13},{6,14},{7,15},{8,0},{9,1},... | collective-permute-start | bytes 460808 | tf_op jit(solution)/shard_map/ppermute | solution.py:365
  18.5 50.8 %collective-permute-start = (bf16[2,256,768]{2,1,0:T(8,128)(2,1)S(1)}, bf16[2,256,768]{2,1,0:T(8,128)(2,1)S(1)}, u32[]{:S(2)}, u32[]{:S(2)}) collective-permute-start(bf16[2,256,768]{2,1,0:T(8,128)(2,1)S(1)} %pad_maximum_fusion.4), channel_id=1, source_target_pairs={{0,1},{1,0},{2,3},{3,2},{4,5},{5,4},{6,7},{7,6},{8,9},{9,8},{10,11... | collective-permute-start | bytes 2359304 | tf_op jit(solution)/shard_map/ppermute | solution.py:337
  20.4 55.8 %copy-start.37 = (s32[1024]{0:T(1024)}, s32[1024]{0:T(1024)S(1)}, u32[]{:S(2)}) copy-start(s32[1024]{0:T(1024)S(1)} %pad.13) | copy-start | bytes 12292
  33.7 6.8 %collective-permute-start.7 = (bf16[2,2,24,1536]{3,2,1,0:T(8,128)(2,1)S(1)}, bf16[2,2,24,1536]{3,2,1,0:T(8,128)(2,1)S(1)}, u32[]{:S(2)}, u32[]{:S(2)}) collective-permute-start(bf16[2,2,24,1536]{3,2,1,0:T(8,128)(2,1)S(1)} %pad_maximum_fusion.16), channel_id=1, source_target_pairs={{0,4},{1,5},{2,6},{3,7},{4,0},{5,1},{6,2},{7,3},{8,12},{9,13},{10,... | collective-permute-start | bytes 884744 | tf_op jit(solution)/shard_map/ppermute | solution.py:365
  36.1 13.2 %collective-permute-start.4 = (bf16[2,2,24,1664]{3,2,1,0:T(8,128)(2,1)S(1)}, bf16[2,2,24,1664]{3,2,1,0:T(8,128)(2,1)S(1)}, u32[]{:S(2)}, u32[]{:S(2)}) collective-permute-start(bf16[2,2,24,1664]{3,2,1,0:T(8,128)(2,1)S(1)} %fusion.24), channel_id=1, source_target_pairs={{0,1},{1,0},{2,3},{3,2},{4,5},{5,4},{6,7},{7,6},{8,9},{9,8},{10,11... | collective-permute-start | bytes 958472 | tf_op jit(solution)/shard_map/ppermute | solution.py:365
  40.7 22.4 %collective-permute-start.8 = (bf16[2,2,2,24,1536]{4,3,2,1,0:T(8,128)(2,1)S(1)}, bf16[2,2,2,24,1536]{4,3,2,1,0:T(8,128)(2,1)S(1)}, u32[]{:S(2)}, u32[]{:S(2)}) collective-permute-start(bf16[2,2,2,24,1536]{4,3,2,1,0:T(8,128)(2,1)S(1)} %pad_maximum_fusion.10), channel_id=1, source_target_pairs={{0,1},{1,0},{2,3},{3,2},{4,5},{5,4},{6,7},{7,6},{8,9},{9,8},{10,11... | collective-permute-start | bytes 1769480 | tf_op jit(solution)/shard_map/ppermute | solution.py:365
  49.5 19.5 %collective-permute-start.5 = (bf16[2,2,2,24,1664]{4,3,1,0,2:T(8,128)(2,1)S(1)}, bf16[2,2,2,24,1664]{4,3,1,0,2:T(8,128)(2,1)S(1)}, u32[]{:S(2)}, u32[]{:S(2)}) collective-permute-start(bf16[2,2,2,24,1664]{4,3,1,0,2:T(8,128)(2,1)S(1)} %pad_maximum_fusion.9), channel_id=1, source_target_pairs={{0,4},{1,5},{2,6},{3,7},{4,0},{5,1},{6,2},{7,3},{8,12},{9,13},{10,... | collective-permute-start | bytes 1916936 | tf_op jit(solution)/shard_map/ppermute | solution.py:365
  63.3 7.9 %collective-permute-start.9 = (bf16[2,2,2,2,24,1536]{5,4,3,2,1,0:T(8,128)(2,1)S(1)}, bf16[2,2,2,2,24,1536]{5,4,3,2,1,0:T(8,128)(2,1)S(1)}, u32[]{:S(2)}, u32[]{:S(2)}) collective-permute-start(bf16[2,2,2,2,24,1536]{5,4,3,2,1,0:T(8,128)(2,1)S(1)} %pad_maximum_fusion.3), channel_id=1, source_target_pairs={{0,2},{1,3},{2,0},{3,1},{4,6},{5,7},{6,4},{7,5},{8,10},{9,11},{10,... | collective-permute-start | bytes 3538952 | tf_op jit(solution)/shard_map/ppermute | solution.py:365
  69.3 3.8 %collective-permute-start.6 = (bf16[2,2,2,2,24,1664]{5,4,1,0,3,2:T(8,128)(2,1)S(1)}, bf16[2,2,2,2,24,1664]{5,4,1,0,3,2:T(8,128)(2,1)S(1)}, u32[]{:S(2)}, u32[]{:S(2)}) collective-permute-start(bf16[2,2,2,2,24,1664]{5,4,1,0,3,2:T(8,128)(2,1)S(1)} %pad_maximum_fusion.2), channel_id=1, source_target_pairs={{0,2},{1,3},{2,0},{3,1},{4,6},{5,7},{6,4},{7,5},{8,10},{9,11},{10,... | collective-permute-start | bytes 3833864 | tf_op jit(solution)/shard_map/ppermute | solution.py:365
  131.6 8.0 %collective-permute-start.10 = (bf16[2,2,4,96,768]{4,3,2,1,0:T(8,128)(2,1)}, bf16[2,2,4,96,768]{4,3,2,1,0:T(8,128)(2,1)}, u32[]{:S(2)}, u32[]{:S(2)}) collective-permute-start(bf16[2,2,4,96,768]{4,3,2,1,0:T(8,128)(2,1)} %get-tuple-element.100), channel_id=1, source_target_pairs={{0,2},{1,3},{2,0},{3,1},{4,6},{5,7},{6,4},{7,5},{8,10},{9,11},{10,... | collective-permute-start | bytes 7077896 | tf_op jit(solution)/shard_map/ppermute | solution.py:365
  131.9 8.0 %collective-permute-start.11 = (bf16[2,2,4,96,768]{4,3,2,1,0:T(8,128)(2,1)}, bf16[2,2,4,96,768]{4,3,2,1,0:T(8,128)(2,1)}, u32[]{:S(2)}, u32[]{:S(2)}) collective-permute-start(bf16[2,2,4,96,768]{4,3,2,1,0:T(8,128)(2,1)} %get-tuple-element.101), channel_id=1, source_target_pairs={{0,2},{1,3},{2,0},{3,1},{4,6},{5,7},{6,4},{7,5},{8,10},{9,11},{10,... | collective-permute-start | bytes 7077896 | tf_op jit(solution)/shard_map/ppermute | solution.py:365
  145.2 28.4 %collective-permute-start.14 = (bf16[2,4,96,768]{3,2,1,0:T(8,128)(2,1)}, bf16[2,4,96,768]{3,2,1,0:T(8,128)(2,1)}, u32[]{:S(2)}, u32[]{:S(2)}) collective-permute-start(bf16[2,4,96,768]{3,2,1,0:T(8,128)(2,1)} %add_bitcast_fusion), channel_id=1, source_target_pairs={{0,4},{1,5},{2,6},{3,7},{4,0},{5,1},{6,2},{7,3},{8,12},{9,13},{10,... | collective-permute-start | bytes 3538952 | tf_op jit(solution)/shard_map/ppermute | solution.py:365
  146.6 28.2 %collective-permute-start.15 = (bf16[2,4,96,768]{3,2,1,0:T(8,128)(2,1)}, bf16[2,4,96,768]{3,2,1,0:T(8,128)(2,1)}, u32[]{:S(2)}, u32[]{:S(2)}) collective-permute-start(bf16[2,4,96,768]{3,2,1,0:T(8,128)(2,1)} %fusion.12), channel_id=1, source_target_pairs={{0,1},{1,0},{2,3},{3,2},{4,5},{5,4},{6,7},{7,6},{8,9},{9,8},{10,11... | collective-permute-start | bytes 3538952 | tf_op jit(solution)/shard_map/ppermute | solution.py:365
  171.1 13.5 %collective-permute-start.12 = (bf16[2,2,4,48,768]{4,3,2,1,0:T(8,128)(2,1)}, bf16[2,2,4,48,768]{4,3,2,1,0:T(8,128)(2,1)}, u32[]{:S(2)}, u32[]{:S(2)}) collective-permute-start(bf16[2,2,4,48,768]{4,3,2,1,0:T(8,128)(2,1)} %get-tuple-element.129), channel_id=1, source_target_pairs={{0,2},{1,3},{2,0},{3,1},{4,6},{5,7},{6,4},{7,5},{8,10},{9,11},{10,... | collective-permute-start | bytes 3538952 | tf_op jit(solution)/shard_map/ppermute | solution.py:365
  171.1 13.5 %collective-permute-start.13 = (bf16[2,2,4,48,768]{4,3,2,1,0:T(8,128)(2,1)}, bf16[2,2,4,48,768]{4,3,2,1,0:T(8,128)(2,1)}, u32[]{:S(2)}, u32[]{:S(2)}) collective-permute-start(bf16[2,2,4,48,768]{4,3,2,1,0:T(8,128)(2,1)} %get-tuple-element.130), channel_id=1, source_target_pairs={{0,2},{1,3},{2,0},{3,1},{4,6},{5,7},{6,4},{7,5},{8,10},{9,11},{10,... | collective-permute-start | bytes 3538952 | tf_op jit(solution)/shard_map/ppermute | solution.py:365
  182.3 2.3 collective-permute-start.16
  182.4 16.4 %collective-permute-start.19 = (bf16[4,96,768]{2,1,0:T(8,128)(2,1)}, bf16[4,96,768]{2,1,0:T(8,128)(2,1)S(1)}, u32[]{:S(2)}, u32[]{:S(2)}) collective-permute-start(bf16[4,96,768]{2,1,0:T(8,128)(2,1)} %fusion.14), channel_id=1, source_target_pairs={{0,1},{1,0},{2,3},{3,2},{4,5},{5,4},{6,7},{7,6},{8,9},{9,8},{10,11... | collective-permute-start | bytes 1769480 | tf_op jit(solution)/shard_map/ppermute | solution.py:365
  183.1 16.4 %collective-permute-start.20 = (bf16[4,96,768]{2,1,0:T(8,128)(2,1)}, bf16[4,96,768]{2,1,0:T(8,128)(2,1)S(1)}, u32[]{:S(2)}, u32[]{:S(2)}) collective-permute-start(bf16[4,96,768]{2,1,0:T(8,128)(2,1)} %fusion.13), channel_id=1, source_target_pairs={{0,4},{1,5},{2,6},{3,7},{4,0},{5,1},{6,2},{7,3},{8,12},{9,13},{10,... | collective-permute-start | bytes 1769480 | tf_op jit(solution)/shard_map/ppermute | solution.py:365
  187.4 24.0 %collective-permute-start.17 = (bf16[2,4,48,768]{3,2,1,0:T(8,128)(2,1)S(1)}, bf16[2,4,48,768]{3,2,1,0:T(8,128)(2,1)S(1)}, u32[]{:S(2)}, u32[]{:S(2)}) collective-permute-start(bf16[2,4,48,768]{3,2,1,0:T(8,128)(2,1)S(1)} %add_bitcast_fusion.1), channel_id=1, source_target_pairs={{0,4},{1,5},{2,6},{3,7},{4,0},{5,1},{6,2},{7,3},{8,12},{9,13},{10,... | collective-permute-start | bytes 1769480 | tf_op jit(solution)/shard_map/ppermute | solution.py:365
  188.0 25.1 %collective-permute-start.18 = (bf16[2,4,56,768]{3,2,1,0:T(8,128)(2,1)S(1)}, bf16[2,4,56,768]{3,2,1,0:T(8,128)(2,1)S(1)}, u32[]{:S(2)}, u32[]{:S(2)}) collective-permute-start(bf16[2,4,56,768]{3,2,1,0:T(8,128)(2,1)S(1)} %pad_maximum_fusion.8), channel_id=1, source_target_pairs={{0,1},{1,0},{2,3},{3,2},{4,5},{5,4},{6,7},{7,6},{8,9},{9,8},{10,11... | collective-permute-start | bytes 2064392 | tf_op jit(solution)/shard_map/ppermute | solution.py:365
  198.8 19.5 %copy-start.30 = (bf16[4,96,768]{2,1,0:T(8,128)(2,1)}, bf16[4,96,768]{2,1,0:T(8,128)(2,1)S(1)}, u32[]{:S(2)}) copy-start(bf16[4,96,768]{2,1,0:T(8,128)(2,1)S(1)} %collective-permute-done.19) | copy-start | bytes 1769476
  202.0 16.2 %collective-permute-start.26 = (bf16[2,192,768]{2,1,0:T(8,128)(2,1)S(1)}, bf16[2,192,768]{2,1,0:T(8,128)(2,1)S(1)}, u32[]{:S(2)}, u32[]{:S(2)}) collective-permute-start(bf16[2,192,768]{2,1,0:T(8,128)(2,1)S(1)} %pad_maximum_fusion.11), channel_id=1, source_target_pairs={{0,8},{1,9},{2,10},{3,11},{4,12},{5,13},{6,14},{7,15},{8,0},{9,1},... | collective-permute-start | bytes 1769480 | tf_op jit(solution)/shard_map/ppermute | solution.py:365
  215.4 10.0 %collective-permute-start.22 = (bf16[4,48,768]{2,1,0:T(8,128)(2,1)S(1)}, bf16[4,48,768]{2,1,0:T(8,128)(2,1)S(1)}, u32[]{:S(2)}, u32[]{:S(2)}) collective-permute-start(bf16[4,48,768]{2,1,0:T(8,128)(2,1)S(1)} %fusion.19), channel_id=1, source_target_pairs={{0,1},{1,0},{2,3},{3,2},{4,5},{5,4},{6,7},{7,6},{8,9},{9,8},{10,11... | collective-permute-start | bytes 884744 | tf_op jit(solution)/shard_map/ppermute | solution.py:365
  216.1 9.3 %collective-permute-start.23 = (bf16[4,56,768]{2,1,0:T(8,128)(2,1)S(1)}, bf16[4,56,768]{2,1,0:T(8,128)(2,1)S(1)}, u32[]{:S(2)}, u32[]{:S(2)}) collective-permute-start(bf16[4,56,768]{2,1,0:T(8,128)(2,1)S(1)} %pad_maximum_fusion.12), channel_id=1, source_target_pairs={{0,4},{1,5},{2,6},{3,7},{4,0},{5,1},{6,2},{7,3},{8,12},{9,13},{10,... | collective-permute-start | bytes 1032200 | tf_op jit(solution)/shard_map/ppermute | solution.py:365
  217.7 24.4 %collective-permute-start.21 = (bf16[2,256,768]{2,1,0:T(8,128)(2,1)S(1)}, bf16[2,256,768]{2,1,0:T(8,128)(2,1)S(1)}, u32[]{:S(2)}, u32[]{:S(2)}) collective-permute-start(bf16[2,256,768]{2,1,0:T(8,128)(2,1)S(1)} %pad_maximum_fusion.7), channel_id=1, source_target_pairs={{0,1},{1,0},{2,3},{3,2},{4,5},{5,4},{6,7},{7,6},{8,9},{9,8},{10,11... | collective-permute-start | bytes 2359304 | tf_op jit(solution)/shard_map/ppermute | solution.py:348
  219.7 15.2 %copy-start.29 = (bf16[1,1,96,768]{3,2,1,0:T(8,128)(2,1)S(1)}, bf16[1,1,96,768]{3,2,1,0:T(8,128)(2,1)}, u32[]{:S(2)}) copy-start(bf16[1,1,96,768]{3,2,1,0:T(8,128)(2,1)} %split.272) | copy-start | bytes 442372
  219.8 15.1 %collective-permute-start.27 = (bf16[1,192,768]{2,1,0:T(8,128)(2,1)S(1)}, bf16[1,192,768]{2,1,0:T(8,128)(2,1)S(1)}, u32[]{:S(2)}, u32[]{:S(2)}) collective-permute-start(bf16[1,192,768]{2,1,0:T(8,128)(2,1)S(1)} %pad_maximum_fusion.18), channel_id=1, source_target_pairs={{0,16},{1,17},{2,18},{3,19},{4,20},{5,21},{6,22},{7,23},{8,24},{9,... | collective-permute-start | bytes 884744 | tf_op jit(solution)/shard_map/ppermute | solution.py:365
  227.5 13.4 %collective-permute-start.24 = (bf16[2,104,768]{2,1,0:T(8,128)(2,1)S(1)}, bf16[2,104,768]{2,1,0:T(8,128)(2,1)S(1)}, u32[]{:S(2)}, u32[]{:S(2)}) collective-permute-start(bf16[2,104,768]{2,1,0:T(8,128)(2,1)S(1)} %pad_maximum_fusion.13), channel_id=1, source_target_pairs={{0,8},{1,9},{2,10},{3,11},{4,12},{5,13},{6,14},{7,15},{8,0},{9,1},... | collective-permute-start | bytes 958472 | tf_op jit(solution)/shard_map/ppermute | solution.py:365
  242.0 8.6 %collective-permute-start.25 = (bf16[1,104,768]{2,1,0:T(8,128)(2,1)S(1)}, bf16[1,104,768]{2,1,0:T(8,128)(2,1)S(1)}, u32[]{:S(2)}, u32[]{:S(2)}) collective-permute-start(bf16[1,104,768]{2,1,0:T(8,128)(2,1)S(1)} %pad_maximum_fusion.19), channel_id=1, source_target_pairs={{0,16},{1,17},{2,18},{3,19},{4,20},{5,21},{6,22},{7,23},{8,24},{9,... | collective-permute-start | bytes 479240 | tf_op jit(solution)/shard_map/ppermute | solution.py:365
  (44 other events, 230.1 us)
Sparse Core Ops, SparseCore 0:
  11.6 94.1 all-gather.1

commit v7 on v6

--- a/solution.py
+++ b/solution.py
@@ -624,9 +624,8 @@
     own_qk, own_vo, rest = small.finish()
     own_w_in = own_w_in.reshape(-1, own, width).transpose(1, 0, 2).reshape(w_in.shape)
     d_w = [own_qk[:own], own_qk[own:], own_vo[:own]]
-    own_gain_attn = sum(
-        jnp.sum(w.astype(f32) * d, axis=1) for w, d in zip((w_query, w_key, w_value), d_w)
-    ) / gain_attn.astype(f32)
+    shares = sum(w.astype(f32) * d for w, d in zip((w_query, w_key, w_value), d_w))
+    own_gain_attn = jnp.sum(shares, axis=1) / gain_attn.astype(f32)
     own_gain_ffn = jnp.sum(w_in.astype(f32) * own_w_in, axis=1) / gain_ffn.astype(f32)
     heads, buckets_count = bias_table.shape
     own_table = rest[:heads, :buckets_count] + rest[:heads, buckets_count : 2 * buckets_count]

time: 262 us -> 261 us (level)
  no operation moved by 1% of the time
where the time goes in v7:
time: 261 us; the launch traced here: 260 us
  waiting for transfers between devices  85.6 us (33%)
  Pallas kernels  61.7 us (24%)
  other arithmetic  44.2 us (17%)
  starting transfers between devices  30.5 us (12%)
  between operations  15.1 us (6%)
  local copies, waits for them, and re-layouts  14.2 us (5%)
  matrix products  8.99 us (3%)
    ppermute x26, waiting for transfers between devices, partner_sends(): lax.ppermute(array, ('rows', 'seq'), [(b, b ^ mask) for b in range(device...  73.5 us
    ppermute x26, starting transfers between devices, partner_sends(): lax.ppermute(array, ('rows', 'seq'), [(b, b ^ mask) for b in range(device...  28.2 us
    pallas_call x1, Pallas kernels, ffn(): pl.pallas_call(ffn_kernel, grid_spec=pltpu.PrefetchScalarGridSpec(num_sca...  25.7 us
    pallas_call x2, Pallas kernels, attend_back(): pl.pallas_call(attend_back_kernel, grid=(count,), in_specs=[spec(start),...  18.7 us
    all_gather x1, waiting for transfers between devices, shards(): lax.all_gather(jnp.concatenate([w_in, groups], axis=1), ('rows', 'seq'),...  12 us
    pallas_call x1, Pallas kernels, attend(): pl.pallas_call(attend_kernel, grid=(steps,), in_specs=[spec(0), spec(step...  8.92 us
    pallas_call x1, Pallas kernels, weight_grads(): pl.pallas_call(kernel, grid_spec=pltpu.PrefetchScalarGridSpec(num_scalar_...  8.44 us
    another operation x10, other arithmetic  8.08 us
  transfers between devices with their start and end apart: 29, of which 17 were waited for; matrix products, arithmetic and copies ran while one was open for 20% of the time, Pallas kernels for 14%

profile of v7, /device:TPU:0, one launch (start us, length us, event | category | flops | bytes accessed | tf_op | source)
XLA Modules:
  0.0 260.3 jit_solution(2799051206742848784)
XLA Ops:
  8.4 1.6 pad_maximum_fusion.17
  12.7 4.1 %collective-permute-start.2 = (bf16[24,3200]{1,0:T(8,128)(2,1)S(1)}, bf16[24,3200]{1,0:T(8,128)(2,1)S(1)}, u32[]{:S(2)}, u32[]{:S(2)}) collective-permute-start(bf16[24,3200]{1,0:T(8,128)(2,1)S(1)} %constant_dynamic-update-slice_fusion), channel_id=1, source_target_pairs={{0,16},{1,17},{2,18},{3,19},{4,20},{5,21},{6,22},{7,23},{8,24},{9,... | collective-permute-start | bytes 460808 | tf_op jit(solution)/shard_map/ppermute | solution.py:365
  20.4 11.3 %collective-permute-done.1 = bf16[24,3200]{1,0:T(8,128)(2,1)} collective-permute-done((bf16[24,3200]{1,0:T(8,128)(2,1)S(1)}, bf16[24,3200]{1,0:T(8,128)(2,1)}, u32[]{:S(2)}, u32[]{:S(2)}) %collective-permute-start.1) | collective-permute-done | bytes 153632 | tf_op jit(solution)/shard_map/ppermute | solution.py:365
  33.7 1.8 collective-permute-start.7
  36.1 2.2 collective-permute-start.4
  38.3 2.2 collective-permute-done.7
  40.7 2.4 collective-permute-start.8
  43.1 6.3 %collective-permute-done.4 = bf16[2,2,24,1664]{3,2,1,0:T(8,128)(2,1)S(1)} collective-permute-done((bf16[2,2,24,1664]{3,2,1,0:T(8,128)(2,1)S(1)}, bf16[2,2,24,1664]{3,2,1,0:T(8,128)(2,1)S(1)}, u32[]{:S(2)}, u32[]{:S(2)}) %collective-permute-start.4) | collective-permute-done | bytes 319520 | tf_op jit(solution)/shard_map/ppermute | solution.py:365
  50.9 12.3 %collective-permute-done.8 = bf16[2,2,2,24,1536]{4,3,2,1,0:T(8,128)(2,1)S(1)} collective-permute-done((bf16[2,2,2,24,1536]{4,3,2,1,0:T(8,128)(2,1)S(1)}, bf16[2,2,2,24,1536]{4,3,2,1,0:T(8,128)(2,1)S(1)}, u32[]{:S(2)}, u32[]{:S(2)}) %collective-permute-start.8) | collective-permute-done | bytes 589856 | tf_op jit(solution)/shard_map/ppermute | solution.py:365
  63.4 5.6 %collective-permute-done.5 = bf16[2,2,2,24,1664]{4,3,1,0,2:T(8,128)(2,1)S(1)} collective-permute-done((bf16[2,2,2,24,1664]{4,3,1,0,2:T(8,128)(2,1)S(1)}, bf16[2,2,2,24,1664]{4,3,1,0,2:T(8,128)(2,1)S(1)}, u32[]{:S(2)}, u32[]{:S(2)}) %collective-permute-start.5) | collective-permute-done | bytes 639008 | tf_op jit(solution)/shard_map/ppermute | solution.py:365
  71.4 1.6 pad_maximum_fusion.1
  80.1 8.9 %shard_map.203 = (bf16[512,768]{1,0:T(8,128)(2,1)S(1)}, bf16[768,512]{1,0:T(8,128)(2,1)S(1)}, f32[6,2,512]{2,1,0:T(2,128)S(1)}) custom-call(bf16[512,1536]{1,0:T(8,128)(2,1)S(1)} %convolution_convert_fusion.q_ref.k_ref, bf16[512,1536]{1,0:T(8,128)(2,1)S(1)} %convolution_convert_fusion.q_ref.k_ref, bf16[512,768]{1,0:T(8,128)(2,1)S(1)} %convolution_convert_fusion.1.v_ref, ...), custom_call_target="tpu_custom_call" | custom-call | flops 1048576 | bytes 1024 | tf_op jit(solution)/shard_map/pallas_call | solution.py:61
  89.1 2.4 multiply_reduce_fusion
  93.8 12.0 %all-gather.2.cloned.1.call-done.win_ref.wout_ref = bf16[768,6144]{1,0:T(8,128)(2,1)} async-done(((bf16[24,6144]{1,0:T(8,128)(2,1)}), bf16[768,6144]{1,0:T(8,128)(2,1)}) %all-gather.2.cloned.1.call-update) | async-done | bytes 9437200 | tf_op jit(solution)/shard_map/all_gather | solution.py:535
  105.7 25.7 %shard_map.204 = (bf16[512,768]{1,0:T(8,128)(2,1)}, f32[512,768]{1,0:T(8,128)}, bf16[512,768]{1,0:T(8,128)(2,1)}, bf16[512,768]{1,0:T(8,128)(2,1)}, bf16[2,2,4,9...) custom-call(s32[4]{0:T(128)} %pad_add_fusion.seat_ref, ...), custom_call_target="tpu_custom_call" | custom-call | flops 1048576 | bytes 1024 | tf_op jit(solution)/shard_map/pallas_call | solution.py:252
  133.1 6.2 %shard_map.205 = (bf16[512,256]{1,0:T(8,128)(2,1)S(1)}, bf16[512,256]{1,0:T(8,128)(2,1)S(1)}, bf16[512,256]{1,0:T(8,128)(2,1)S(1)}, f32[2,2,1024]{2,1,0:T(2,128)S(1)}) custom-call(bf16[512,1536]{1,0:T(8,128)(2,1)S(1)} %convolution_convert_fusion.q_ref.k_ref, bf16[512,1536]{1,0:T(8,128)(2,1)S(1)} %convolution_convert_fusion.q_ref.k_ref, ...), custom_call_target="tpu_custom_call" | custom-call | flops 1048576 | bytes 1024 | tf_op jit(solution)/shard_map/pallas_call | solution.py:99
  139.7 2.6 add_bitcast_fusion
  142.3 2.7 %fusion.12 = bf16[2,4,96,768]{3,2,1,0:T(8,128)(2,1)} fusion(bf16[2,2,4,96,768]{4,3,2,1,0:T(8,128)(2,1)S(1)} %copy-done.11, bf16[2,2,4,96,768]{4,3,2,1,0:T(8,128)(2,1)} %collective-permute-done.11), kind=kLoop, calls=%fused_computation.28 | loop fusion | flops 2359296 | bytes 3538944 | tf_op jit(solution)/shard_map/add | solution.py:439
  147.8 12.5 %shard_map.206 = (bf16[512,512]{1,0:T(8,128)(2,1)S(1)}, bf16[512,512]{1,0:T(8,128)(2,1)S(1)}, bf16[512,512]{1,0:T(8,128)(2,1)S(1)}, f32[4,2,1024]{2,1,0:T(2,128)S(1)}) custom-call(bf16[512,1536]{1,0:T(8,128)(2,1)S(1)} %convolution_convert_fusion.q_ref.k_ref, bf16[512,1536]{1,0:T(8,128)(2,1)S(1)} %convolution_convert_fusion.q_ref.k_ref, ...), custom_call_target="tpu_custom_call" | custom-call | flops 1048576 | bytes 1024 | tf_op jit(solution)/shard_map/pallas_call | solution.py:99
  161.8 8.4 %shard_map.207 = (bf16[2,2,4,48,768]{4,3,2,1,0:T(8,128)(2,1)}, bf16[2,2,4,48,768]{4,3,2,1,0:T(8,128)(2,1)}, bf16[2,2,4,48,768]{4,3,2,1,0:T(8,128)(2,1)}, bf16[2,2,4,48,768]{4,3,2,1,0:T(8,128)(2,1)}) custom-call(s32[4]{0:T(128)} %pad_add_fusion.seat_ref, bf16[512,768]{1,0:T(8,128)(2,1)} %copy-done.10, bf16[768,512]{1,0:T(8,128)(2,1)} %copy-done.1, ...), custom_call_target="tpu_custom_call" | custom-call | flops 1048576 | bytes 1024 | tf_op jit(solution)/shard_map/pallas_call | solution.py:302
  176.2 2.5 fusion.14
  178.6 2.3 fusion.13
  191.2 2.4 fusion.7
  194.1 4.6 %collective-permute-done.19 = bf16[4,96,768]{2,1,0:T(8,128)(2,1)S(1)} collective-permute-done((bf16[4,96,768]{2,1,0:T(8,128)(2,1)}, bf16[4,96,768]{2,1,0:T(8,128)(2,1)S(1)}, u32[]{:S(2)}, u32[]{:S(2)}) %collective-permute-start.19) | collective-permute-done | bytes 589856 | tf_op jit(solution)/shard_map/ppermute | solution.py:365
  203.4 7.7 %collective-permute-done.17 = bf16[2,4,48,768]{3,2,1,0:T(8,128)(2,1)S(1)} collective-permute-done((bf16[2,4,48,768]{3,2,1,0:T(8,128)(2,1)S(1)}, bf16[2,4,48,768]{3,2,1,0:T(8,128)(2,1)S(1)}, u32[]{:S(2)}, u32[]{:S(2)}) %collective-permute-start.17) | collective-permute-done | bytes 589856 | tf_op jit(solution)/shard_map/ppermute | solution.py:365
  211.2 1.8 collective-permute-done.18
  219.6 2.0 collective-permute-start.27
  221.6 3.6 %collective-permute-done.22 = bf16[4,48,768]{2,1,0:T(8,128)(2,1)S(1)} collective-permute-done((bf16[4,48,768]{2,1,0:T(8,128)(2,1)S(1)}, bf16[4,48,768]{2,1,0:T(8,128)(2,1)S(1)}, u32[]{:S(2)}, u32[]{:S(2)}) %collective-permute-start.22) | collective-permute-done | bytes 294944 | tf_op jit(solution)/shard_map/ppermute | solution.py:365
  228.9 5.9 %collective-permute-done.27 = bf16[1,192,768]{2,1,0:T(8,128)(2,1)S(1)} collective-permute-done((bf16[1,192,768]{2,1,0:T(8,128)(2,1)S(1)}, bf16[1,192,768]{2,1,0:T(8,128)(2,1)S(1)}, u32[]{:S(2)}, u32[]{:S(2)}) %collective-permute-start.27) | collective-permute-done | bytes 294944 | tf_op jit(solution)/shard_map/ppermute | solution.py:365
  234.9 1.9 convert_add_fusion.7
  237.6 3.0 %collective-permute-done.24 = bf16[2,104,768]{2,1,0:T(8,128)(2,1)S(1)} collective-permute-done((bf16[2,104,768]{2,1,0:T(8,128)(2,1)S(1)}, bf16[2,104,768]{2,1,0:T(8,128)(2,1)S(1)}, u32[]{:S(2)}, u32[]{:S(2)}) %collective-permute-start.24) | collective-permute-done | bytes 319520 | tf_op jit(solution)/shard_map/ppermute | solution.py:365
  244.0 6.4 %collective-permute-done.25 = bf16[1,104,768]{2,1,0:T(8,128)(2,1)S(1)} collective-permute-done((bf16[1,104,768]{2,1,0:T(8,128)(2,1)S(1)}, bf16[1,104,768]{2,1,0:T(8,128)(2,1)S(1)}, u32[]{:S(2)}, u32[]{:S(2)}) %collective-permute-start.25) | collective-permute-done | bytes 159776 | tf_op jit(solution)/shard_map/ppermute | solution.py:365
  (250 shorter events, 68.4 us)
Async XLA Ops:
  7.2 98.5 %all-gather.2.cloned.1.call-start = ((), (), s32[]{:S(2)}) async-start(), calls=%async_computation | async-start | bytes 9732096 | tf_op jit(solution)/shard_map/all_gather | solution.py:535
  12.7 19.9 %collective-permute-start.2 = (bf16[24,3200]{1,0:T(8,128)(2,1)S(1)}, bf16[24,3200]{1,0:T(8,128)(2,1)S(1)}, u32[]{:S(2)}, u32[]{:S(2)}) collective-permute-start(bf16[24,3200]{1,0:T(8,128)(2,1)S(1)} %constant_dynamic-update-slice_fusion), channel_id=1, source_target_pairs={{0,16},{1,17},{2,18},{3,19},{4,20},{5,21},{6,22},{7,23},{8,24},{9,... | collective-permute-start | bytes 460808 | tf_op jit(solution)/shard_map/ppermute | solution.py:365
  16.8 15.8 %collective-permute-start.3 = (bf16[24,3200]{1,0:T(8,128)(2,1)S(1)}, bf16[24,3200]{1,0:T(8,128)(2,1)}, u32[]{:S(2)}, u32[]{:S(2)}) collective-permute-start(bf16[24,3200]{1,0:T(8,128)(2,1)S(1)} %constant_dynamic-update-slice_fusion), channel_id=1, source_target_pairs={{0,24},{1,25},{2,26},{3,27},{4,28},{5,29},{6,30},{7,31},{8,16},{9,... | collective-permute-start | bytes 460808 | tf_op jit(solution)/shard_map/ppermute | solution.py:365
  18.2 13.5 %collective-permute-start.1 = (bf16[24,3200]{1,0:T(8,128)(2,1)S(1)}, bf16[24,3200]{1,0:T(8,128)(2,1)}, u32[]{:S(2)}, u32[]{:S(2)}) collective-permute-start(bf16[24,3200]{1,0:T(8,128)(2,1)S(1)} %constant_dynamic-update-slice_fusion), channel_id=1, source_target_pairs={{0,8},{1,9},{2,10},{3,11},{4,12},{5,13},{6,14},{7,15},{8,0},{9,1},... | collective-permute-start | bytes 460808 | tf_op jit(solution)/shard_map/ppermute | solution.py:365
  18.5 50.8 %collective-permute-start = (bf16[2,256,768]{2,1,0:T(8,128)(2,1)S(1)}, bf16[2,256,768]{2,1,0:T(8,128)(2,1)S(1)}, u32[]{:S(2)}, u32[]{:S(2)}) collective-permute-start(bf16[2,256,768]{2,1,0:T(8,128)(2,1)S(1)} %pad_maximum_fusion.4), channel_id=1, source_target_pairs={{0,1},{1,0},{2,3},{3,2},{4,5},{5,4},{6,7},{7,6},{8,9},{9,8},{10,11... | collective-permute-start | bytes 2359304 | tf_op jit(solution)/shard_map/ppermute | solution.py:337
  20.4 55.9 %copy-start.37 = (s32[1024]{0:T(1024)}, s32[1024]{0:T(1024)S(1)}, u32[]{:S(2)}) copy-start(s32[1024]{0:T(1024)S(1)} %pad.13) | copy-start | bytes 12292
  33.7 6.8 %collective-permute-start.7 = (bf16[2,2,24,1536]{3,2,1,0:T(8,128)(2,1)S(1)}, bf16[2,2,24,1536]{3,2,1,0:T(8,128)(2,1)S(1)}, u32[]{:S(2)}, u32[]{:S(2)}) collective-permute-start(bf16[2,2,24,1536]{3,2,1,0:T(8,128)(2,1)S(1)} %pad_maximum_fusion.16), channel_id=1, source_target_pairs={{0,4},{1,5},{2,6},{3,7},{4,0},{5,1},{6,2},{7,3},{8,12},{9,13},{10,... | collective-permute-start | bytes 884744 | tf_op jit(solution)/shard_map/ppermute | solution.py:365
  36.1 13.2 %collective-permute-start.4 = (bf16[2,2,24,1664]{3,2,1,0:T(8,128)(2,1)S(1)}, bf16[2,2,24,1664]{3,2,1,0:T(8,128)(2,1)S(1)}, u32[]{:S(2)}, u32[]{:S(2)}) collective-permute-start(bf16[2,2,24,1664]{3,2,1,0:T(8,128)(2,1)S(1)} %fusion.24), channel_id=1, source_target_pairs={{0,1},{1,0},{2,3},{3,2},{4,5},{5,4},{6,7},{7,6},{8,9},{9,8},{10,11... | collective-permute-start | bytes 958472 | tf_op jit(solution)/shard_map/ppermute | solution.py:365
  40.7 22.4 %collective-permute-start.8 = (bf16[2,2,2,24,1536]{4,3,2,1,0:T(8,128)(2,1)S(1)}, bf16[2,2,2,24,1536]{4,3,2,1,0:T(8,128)(2,1)S(1)}, u32[]{:S(2)}, u32[]{:S(2)}) collective-permute-start(bf16[2,2,2,24,1536]{4,3,2,1,0:T(8,128)(2,1)S(1)} %pad_maximum_fusion.10), channel_id=1, source_target_pairs={{0,1},{1,0},{2,3},{3,2},{4,5},{5,4},{6,7},{7,6},{8,9},{9,8},{10,11... | collective-permute-start | bytes 1769480 | tf_op jit(solution)/shard_map/ppermute | solution.py:365
  49.5 19.5 %collective-permute-start.5 = (bf16[2,2,2,24,1664]{4,3,1,0,2:T(8,128)(2,1)S(1)}, bf16[2,2,2,24,1664]{4,3,1,0,2:T(8,128)(2,1)S(1)}, u32[]{:S(2)}, u32[]{:S(2)}) collective-permute-start(bf16[2,2,2,24,1664]{4,3,1,0,2:T(8,128)(2,1)S(1)} %pad_maximum_fusion.9), channel_id=1, source_target_pairs={{0,4},{1,5},{2,6},{3,7},{4,0},{5,1},{6,2},{7,3},{8,12},{9,13},{10,... | collective-permute-start | bytes 1916936 | tf_op jit(solution)/shard_map/ppermute | solution.py:365
  63.3 7.9 %collective-permute-start.9 = (bf16[2,2,2,2,24,1536]{5,4,3,2,1,0:T(8,128)(2,1)S(1)}, bf16[2,2,2,2,24,1536]{5,4,3,2,1,0:T(8,128)(2,1)S(1)}, u32[]{:S(2)}, u32[]{:S(2)}) collective-permute-start(bf16[2,2,2,2,24,1536]{5,4,3,2,1,0:T(8,128)(2,1)S(1)} %pad_maximum_fusion.3), channel_id=1, source_target_pairs={{0,2},{1,3},{2,0},{3,1},{4,6},{5,7},{6,4},{7,5},{8,10},{9,11},{10,... | collective-permute-start | bytes 3538952 | tf_op jit(solution)/shard_map/ppermute | solution.py:365
  69.3 3.7 %collective-permute-start.6 = (bf16[2,2,2,2,24,1664]{5,4,1,0,3,2:T(8,128)(2,1)S(1)}, bf16[2,2,2,2,24,1664]{5,4,1,0,3,2:T(8,128)(2,1)S(1)}, u32[]{:S(2)}, u32[]{:S(2)}) collective-permute-start(bf16[2,2,2,2,24,1664]{5,4,1,0,3,2:T(8,128)(2,1)S(1)} %pad_maximum_fusion.2), channel_id=1, source_target_pairs={{0,2},{1,3},{2,0},{3,1},{4,6},{5,7},{6,4},{7,5},{8,10},{9,11},{10,... | collective-permute-start | bytes 3833864 | tf_op jit(solution)/shard_map/ppermute | solution.py:365
  131.4 8.0 %collective-permute-start.10 = (bf16[2,2,4,96,768]{4,3,2,1,0:T(8,128)(2,1)}, bf16[2,2,4,96,768]{4,3,2,1,0:T(8,128)(2,1)}, u32[]{:S(2)}, u32[]{:S(2)}) collective-permute-start(bf16[2,2,4,96,768]{4,3,2,1,0:T(8,128)(2,1)} %get-tuple-element.100), channel_id=1, source_target_pairs={{0,2},{1,3},{2,0},{3,1},{4,6},{5,7},{6,4},{7,5},{8,10},{9,11},{10,... | collective-permute-start | bytes 7077896 | tf_op jit(solution)/shard_map/ppermute | solution.py:365
  131.7 8.0 %collective-permute-start.11 = (bf16[2,2,4,96,768]{4,3,2,1,0:T(8,128)(2,1)}, bf16[2,2,4,96,768]{4,3,2,1,0:T(8,128)(2,1)}, u32[]{:S(2)}, u32[]{:S(2)}) collective-permute-start(bf16[2,2,4,96,768]{4,3,2,1,0:T(8,128)(2,1)} %get-tuple-element.101), channel_id=1, source_target_pairs={{0,2},{1,3},{2,0},{3,1},{4,6},{5,7},{6,4},{7,5},{8,10},{9,11},{10,... | collective-permute-start | bytes 7077896 | tf_op jit(solution)/shard_map/ppermute | solution.py:365
  145.0 28.4 %collective-permute-start.14 = (bf16[2,4,96,768]{3,2,1,0:T(8,128)(2,1)}, bf16[2,4,96,768]{3,2,1,0:T(8,128)(2,1)}, u32[]{:S(2)}, u32[]{:S(2)}) collective-permute-start(bf16[2,4,96,768]{3,2,1,0:T(8,128)(2,1)} %add_bitcast_fusion), channel_id=1, source_target_pairs={{0,4},{1,5},{2,6},{3,7},{4,0},{5,1},{6,2},{7,3},{8,12},{9,13},{10,... | collective-permute-start | bytes 3538952 | tf_op jit(solution)/shard_map/ppermute | solution.py:365
  146.4 28.2 %collective-permute-start.15 = (bf16[2,4,96,768]{3,2,1,0:T(8,128)(2,1)}, bf16[2,4,96,768]{3,2,1,0:T(8,128)(2,1)}, u32[]{:S(2)}, u32[]{:S(2)}) collective-permute-start(bf16[2,4,96,768]{3,2,1,0:T(8,128)(2,1)} %fusion.12), channel_id=1, source_target_pairs={{0,1},{1,0},{2,3},{3,2},{4,5},{5,4},{6,7},{7,6},{8,9},{9,8},{10,11... | collective-permute-start | bytes 3538952 | tf_op jit(solution)/shard_map/ppermute | solution.py:365
  170.9 13.5 %collective-permute-start.12 = (bf16[2,2,4,48,768]{4,3,2,1,0:T(8,128)(2,1)}, bf16[2,2,4,48,768]{4,3,2,1,0:T(8,128)(2,1)}, u32[]{:S(2)}, u32[]{:S(2)}) collective-permute-start(bf16[2,2,4,48,768]{4,3,2,1,0:T(8,128)(2,1)} %get-tuple-element.129), channel_id=1, source_target_pairs={{0,2},{1,3},{2,0},{3,1},{4,6},{5,7},{6,4},{7,5},{8,10},{9,11},{10,... | collective-permute-start | bytes 3538952 | tf_op jit(solution)/shard_map/ppermute | solution.py:365
  170.9 13.5 %collective-permute-start.13 = (bf16[2,2,4,48,768]{4,3,2,1,0:T(8,128)(2,1)}, bf16[2,2,4,48,768]{4,3,2,1,0:T(8,128)(2,1)}, u32[]{:S(2)}, u32[]{:S(2)}) collective-permute-start(bf16[2,2,4,48,768]{4,3,2,1,0:T(8,128)(2,1)} %get-tuple-element.130), channel_id=1, source_target_pairs={{0,2},{1,3},{2,0},{3,1},{4,6},{5,7},{6,4},{7,5},{8,10},{9,11},{10,... | collective-permute-start | bytes 3538952 | tf_op jit(solution)/shard_map/ppermute | solution.py:365
  182.2 2.3 collective-permute-start.16
  182.2 16.4 %collective-permute-start.19 = (bf16[4,96,768]{2,1,0:T(8,128)(2,1)}, bf16[4,96,768]{2,1,0:T(8,128)(2,1)S(1)}, u32[]{:S(2)}, u32[]{:S(2)}) collective-permute-start(bf16[4,96,768]{2,1,0:T(8,128)(2,1)} %fusion.14), channel_id=1, source_target_pairs={{0,1},{1,0},{2,3},{3,2},{4,5},{5,4},{6,7},{7,6},{8,9},{9,8},{10,11... | collective-permute-start | bytes 1769480 | tf_op jit(solution)/shard_map/ppermute | solution.py:365
  182.9 16.4 %collective-permute-start.20 = (bf16[4,96,768]{2,1,0:T(8,128)(2,1)}, bf16[4,96,768]{2,1,0:T(8,128)(2,1)S(1)}, u32[]{:S(2)}, u32[]{:S(2)}) collective-permute-start(bf16[4,96,768]{2,1,0:T(8,128)(2,1)} %fusion.13), channel_id=1, source_target_pairs={{0,4},{1,5},{2,6},{3,7},{4,0},{5,1},{6,2},{7,3},{8,12},{9,13},{10,... | collective-permute-start | bytes 1769480 | tf_op jit(solution)/shard_map/ppermute | solution.py:365
  187.2 24.0 %collective-permute-start.17 = (bf16[2,4,48,768]{3,2,1,0:T(8,128)(2,1)S(1)}, bf16[2,4,48,768]{3,2,1,0:T(8,128)(2,1)S(1)}, u32[]{:S(2)}, u32[]{:S(2)}) collective-permute-start(bf16[2,4,48,768]{3,2,1,0:T(8,128)(2,1)S(1)} %add_bitcast_fusion.1), channel_id=1, source_target_pairs={{0,4},{1,5},{2,6},{3,7},{4,0},{5,1},{6,2},{7,3},{8,12},{9,13},{10,... | collective-permute-start | bytes 1769480 | tf_op jit(solution)/shard_map/ppermute | solution.py:365
  187.8 25.1 %collective-permute-start.18 = (bf16[2,4,56,768]{3,2,1,0:T(8,128)(2,1)S(1)}, bf16[2,4,56,768]{3,2,1,0:T(8,128)(2,1)S(1)}, u32[]{:S(2)}, u32[]{:S(2)}) collective-permute-start(bf16[2,4,56,768]{3,2,1,0:T(8,128)(2,1)S(1)} %pad_maximum_fusion.8), channel_id=1, source_target_pairs={{0,1},{1,0},{2,3},{3,2},{4,5},{5,4},{6,7},{7,6},{8,9},{9,8},{10,11... | collective-permute-start | bytes 2064392 | tf_op jit(solution)/shard_map/ppermute | solution.py:365
  198.6 19.5 %copy-start.30 = (bf16[4,96,768]{2,1,0:T(8,128)(2,1)}, bf16[4,96,768]{2,1,0:T(8,128)(2,1)S(1)}, u32[]{:S(2)}) copy-start(bf16[4,96,768]{2,1,0:T(8,128)(2,1)S(1)} %collective-permute-done.19) | copy-start | bytes 1769476
  201.9 16.3 %collective-permute-start.26 = (bf16[2,192,768]{2,1,0:T(8,128)(2,1)S(1)}, bf16[2,192,768]{2,1,0:T(8,128)(2,1)S(1)}, u32[]{:S(2)}, u32[]{:S(2)}) collective-permute-start(bf16[2,192,768]{2,1,0:T(8,128)(2,1)S(1)} %pad_maximum_fusion.11), channel_id=1, source_target_pairs={{0,8},{1,9},{2,10},{3,11},{4,12},{5,13},{6,14},{7,15},{8,0},{9,1},... | collective-permute-start | bytes 1769480 | tf_op jit(solution)/shard_map/ppermute | solution.py:365
  215.2 10.0 %collective-permute-start.22 = (bf16[4,48,768]{2,1,0:T(8,128)(2,1)S(1)}, bf16[4,48,768]{2,1,0:T(8,128)(2,1)S(1)}, u32[]{:S(2)}, u32[]{:S(2)}) collective-permute-start(bf16[4,48,768]{2,1,0:T(8,128)(2,1)S(1)} %fusion.19), channel_id=1, source_target_pairs={{0,1},{1,0},{2,3},{3,2},{4,5},{5,4},{6,7},{7,6},{8,9},{9,8},{10,11... | collective-permute-start | bytes 884744 | tf_op jit(solution)/shard_map/ppermute | solution.py:365
  215.9 9.3 %collective-permute-start.23 = (bf16[4,56,768]{2,1,0:T(8,128)(2,1)S(1)}, bf16[4,56,768]{2,1,0:T(8,128)(2,1)S(1)}, u32[]{:S(2)}, u32[]{:S(2)}) collective-permute-start(bf16[4,56,768]{2,1,0:T(8,128)(2,1)S(1)} %pad_maximum_fusion.12), channel_id=1, source_target_pairs={{0,4},{1,5},{2,6},{3,7},{4,0},{5,1},{6,2},{7,3},{8,12},{9,13},{10,... | collective-permute-start | bytes 1032200 | tf_op jit(solution)/shard_map/ppermute | solution.py:365
  217.5 24.2 %collective-permute-start.21 = (bf16[2,256,768]{2,1,0:T(8,128)(2,1)S(1)}, bf16[2,256,768]{2,1,0:T(8,128)(2,1)S(1)}, u32[]{:S(2)}, u32[]{:S(2)}) collective-permute-start(bf16[2,256,768]{2,1,0:T(8,128)(2,1)S(1)} %pad_maximum_fusion.7), channel_id=1, source_target_pairs={{0,1},{1,0},{2,3},{3,2},{4,5},{5,4},{6,7},{7,6},{8,9},{9,8},{10,11... | collective-permute-start | bytes 2359304 | tf_op jit(solution)/shard_map/ppermute | solution.py:348
  219.6 15.2 %copy-start.29 = (bf16[1,1,96,768]{3,2,1,0:T(8,128)(2,1)S(1)}, bf16[1,1,96,768]{3,2,1,0:T(8,128)(2,1)}, u32[]{:S(2)}) copy-start(bf16[1,1,96,768]{3,2,1,0:T(8,128)(2,1)} %split.272) | copy-start | bytes 442372
  219.6 15.1 %collective-permute-start.27 = (bf16[1,192,768]{2,1,0:T(8,128)(2,1)S(1)}, bf16[1,192,768]{2,1,0:T(8,128)(2,1)S(1)}, u32[]{:S(2)}, u32[]{:S(2)}) collective-permute-start(bf16[1,192,768]{2,1,0:T(8,128)(2,1)S(1)} %pad_maximum_fusion.18), channel_id=1, source_target_pairs={{0,16},{1,17},{2,18},{3,19},{4,20},{5,21},{6,22},{7,23},{8,24},{9,... | collective-permute-start | bytes 884744 | tf_op jit(solution)/shard_map/ppermute | solution.py:365
  227.3 13.2 %collective-permute-start.24 = (bf16[2,104,768]{2,1,0:T(8,128)(2,1)S(1)}, bf16[2,104,768]{2,1,0:T(8,128)(2,1)S(1)}, u32[]{:S(2)}, u32[]{:S(2)}) collective-permute-start(bf16[2,104,768]{2,1,0:T(8,128)(2,1)S(1)} %pad_maximum_fusion.13), channel_id=1, source_target_pairs={{0,8},{1,9},{2,10},{3,11},{4,12},{5,13},{6,14},{7,15},{8,0},{9,1},... | collective-permute-start | bytes 958472 | tf_op jit(solution)/shard_map/ppermute | solution.py:365
  241.6 8.7 %collective-permute-start.25 = (bf16[1,104,768]{2,1,0:T(8,128)(2,1)S(1)}, bf16[1,104,768]{2,1,0:T(8,128)(2,1)S(1)}, u32[]{:S(2)}, u32[]{:S(2)}) collective-permute-start(bf16[1,104,768]{2,1,0:T(8,128)(2,1)S(1)} %pad_maximum_fusion.19), channel_id=1, source_target_pairs={{0,16},{1,17},{2,18},{3,19},{4,20},{5,21},{6,22},{7,23},{8,24},{9,... | collective-permute-start | bytes 479240 | tf_op jit(solution)/shard_map/ppermute | solution.py:365
  (44 other events, 228.6 us)
Sparse Core Ops, SparseCore 0:
  11.6 94.1 all-gather.1
